TPU v7x, 128 devices: a whole 4x4x4 slice. The times are simulated.
128 devices in a mesh: rows: 16 (over y, x), cols: 8 (over z, core).
Axes of the slice: x: 4, y: 4, z: 4, core: 2. Of those that a mesh axis runs over, the one named last changes fastest.
Arguments:
- affiliations: float32 [131072, 512], P(('rows', 'cols')), as said below
- tile_block: int32 [128, 240], P(('rows', 'cols')), may hold values from 0 to 1023, as said below
- tile_target: int32 [128, 240], P(('rows', 'cols')), may hold values from 0 to 7
- tile_pattern: int32 [128, 240], P(('rows', 'cols')), may hold values from 0 to 191
- tile_count: int32 [128], P(('rows', 'cols')), may hold values from 15 to 240, as said below
- block_home: int32 [1024], replicated, may hold values from 0 to 1023, as said below
- patterns: int32 [192, 5, 128], replicated, may hold values from 0 to 1073741823, as said below
Outputs:
- updated_affiliations: float32 [131072, 512], P(('rows', 'cols'))
Inputs may be any that keep to these rules, and one draw needn't show every extreme that they name: Live tiles of a device are the first tile_count of its slots, in order of their neighbour's owner row (storage block // 64); some device has exactly 240. `tile_block`: A live tile's neighbour is stored on a device of the same cols index and another rows index; a device's live tiles name at most 4 distinct blocks of one owner row, and in every draw some device names exactly 4 of every other owner row; a (target, neighbour) pair is live at most once on a device; slots past the count hold valid block numbers. `block_home`: A permutation of the node blocks. `patterns`: bits at rows 128 and beyond are zero. `affiliations`: Positive.
All inputs are finite; a program needn't handle non-finite values.
Results may differ from a plain program's by a relative error of at most 0.0003.
Values may be sent and summed in bfloat16 or wider, within the bound.
No kernel may reach another device: no remote copies, remote signals or barrier semaphores. Data moves between devices by JAX's collectives and lax.ppermute only.
A program may use at most 192 MiB of HBM per device.

v0:
```python
import functools

import jax
import jax.numpy as jnp
from jax import lax
from jax.experimental import pallas as pl
from jax.experimental.pallas import tpu as pltpu
from jax.sharding import Mesh
from jax.sharding import PartitionSpec as P

C = 512
BLOCK = 128
STEPS = 2
BPD = 8
SIDE = 4
CAP = 4
N_COLS = 8
NODES = 131072
UNIT = 1572864
PATTERNS = 192
TILES = 240
PARTS = 3
GROUP = (4, 4, 2)
KEYS = PARTS * BPD
SLOTS = TILES + sum(BPD * (g - 1) + 2 * g for g in GROUP) // 8 * 8 + 8
STARTS = SLOTS + SLOTS // 2
LIST = STARTS + 8
EMPTY = PATTERNS * 64
FLOOR = 0.001
STEP_SIZE = 0.3 / NODES
OWN_ROWS = BPD * BLOCK
SENT_ROWS = OWN_ROWS + 16
PICKED = SIDE * CAP
HALF_ROWS = OWN_ROWS // 2

ALL = ("rows_0", "rows_1", "cols_0", "cols_1")
VMEM = pl.BlockSpec(memory_space=pltpu.VMEM)
SMEM = pl.BlockSpec(memory_space=pltpu.SMEM)
HBM = pl.BlockSpec(memory_space=pltpu.HBM)


def pairs(first, second):
    out = []
    for y in range(SIDE):
        for x in range(SIDE):
            for z in range(4):
                for core in range(2):
                    dx, dy = (first, second) if core == 0 else (second, first)
                    sy, sx = (y + dy) % SIDE, (x + dx) % SIDE
                    out.append((((sy * 4 + sx) * 4 + z) * 2 + core, ((y * 4 + x) * 4 + z) * 2 + core))
    return out


def fetch(value, first, second):
    return lax.ppermute(value, ALL, pairs(first, second))


def sum_over_cols(part):
    for axis, size in (("cols_1", 2), ("cols_0", 4)):
        step = 1
        while step < size:
            part = part + lax.ppermute(part, axis, [(i, i ^ step) for i in range(size)])
            step *= 2
    return part


OWNERS = (
    ((1, 0), (1, 1), (1, 3), (3, 0), (3, 1), (3, 3), (0, 1), (0, 2), (0, 3)),
    ((2, 0), (2, 1), (2, 3), (2, 2)),
    ((1, 2), (3, 2)),
)


def clear(ref, start, size, value):
    def body(i, _):
        for j in range(8):
            ref[start + 8 * i + j] = value
        return 0

    lax.fori_loop(0, size // 8, body, 0)


def ask_kernel(place, blocks, targets, count, home, requests, codes, rank, fill, base):
    first, second, core = place[0], place[1], place[2]
    clear(rank, 0, 128, -1)
    clear(fill, 0, 16, 0)
    clear(requests, 0, 64, 0)
    base[0] = 0
    for part, owners in enumerate(OWNERS):
        for i, (m, k) in enumerate(owners):
            base[m * SIDE + k] = part * 512 + i * CAP

    def note(t, _):
        slot = home[blocks[t]]
        row = slot >> 6
        local = slot & (BPD - 1)
        y, x = row >> 2, row & (SIDE - 1)
        owner_first = jnp.where(core == 0, x, y)
        owner_second = jnp.where(core == 0, y, x)
        k = (owner_first - first) & (SIDE - 1)
        m = (owner_second - second) & (SIDE - 1)
        pair = m * SIDE + k
        seen = rank[pair * BPD + local]
        held = fill[pair]
        mine = jnp.minimum(jnp.where(seen < 0, held, seen), CAP - 1)
        rank[pair * BPD + local] = mine
        fill[pair] = jnp.where(seen < 0, held + 1, held)
        requests[pair * CAP + mine] = local
        codes[t] = base[pair] + mine + targets[t] * 64
        return 0

    lax.fori_loop(0, count[0], note, 0)


def ask(place, blocks, targets, count, home):
    i32 = jnp.int32
    return pl.pallas_call(
        ask_kernel,
        out_shape=(jax.ShapeDtypeStruct((64,), i32), jax.ShapeDtypeStruct((TILES,), i32)),
        in_specs=[SMEM] * 5,
        out_specs=(SMEM,) * 2,
        scratch_shapes=[pltpu.SMEM((128,), i32), pltpu.SMEM((16,), i32), pltpu.SMEM((16,), i32)],
        compiler_params=pltpu.CompilerParams(vmem_limit_bytes=2 << 20),
        name="ask",
    )(place, blocks, targets, count, home)


def sort_kernel(codes, pattern_ids, count, lists, per_key):
    clear(per_key, 0, KEYS, 0)
    clear(lists, 0, SLOTS, EMPTY)
    clear(lists, SLOTS, SLOTS // 2, 0)

    def tally(t, _):
        key = codes[t] >> 6
        per_key[key] = per_key[key] + 1
        return 0

    lax.fori_loop(0, count[0], tally, 0)
    slot = jnp.int32(0)
    for part, size in enumerate(GROUP):
        lists[STARTS + part] = slot
        start = slot
        for target in range(BPD):
            key = part * BPD + target
            tiles = per_key[key]
            per_key[key] = slot
            slot = slot + ((tiles + size - 1) & -size)
        slot = start + jnp.maximum(2 * size, (slot - start + 2 * size - 1) & -(2 * size))
    lists[STARTS + PARTS] = slot

    def put(t, _):
        code = codes[t]
        key = code >> 6
        at = per_key[key]
        per_key[key] = at + 1
        lists[at] = pattern_ids[t] * 64 + (code & 63)
        lists[SLOTS + (at >> 1)] = key & (BPD - 1)
        return 0

    lax.fori_loop(0, count[0], put, 0)


def sort_tiles(codes, pattern_ids, count):
    i32 = jnp.int32
    return pl.pallas_call(
        sort_kernel,
        out_shape=jax.ShapeDtypeStruct((LIST,), i32),
        in_specs=[SMEM] * 3,
        out_specs=SMEM,
        scratch_shapes=[pltpu.SMEM((KEYS,), i32)],
        compiler_params=pltpu.CompilerParams(vmem_limit_bytes=2 << 20),
        name="sort_tiles",
    )(codes, pattern_ids, count)


def sum_rows(total):
    high = total.astype(jnp.bfloat16).astype(jnp.float32)
    rest = total - high
    middle = rest.astype(jnp.bfloat16).astype(jnp.float32)
    low = rest - middle
    row = lax.broadcasted_iota(jnp.int32, (16, C), 0)
    out = jnp.where(row == 0, high, jnp.where(row == 1, middle, jnp.where(row == 2, low, 0.0)))
    return out.astype(jnp.bfloat16)


def first_kernel(current, sent):
    total = jnp.zeros((8, C), jnp.float32)
    for j in range(BPD):
        rows = current[pl.ds(j * BLOCK, BLOCK), :]
        sent[pl.ds(j * BLOCK, BLOCK), :] = rows.astype(jnp.bfloat16)
        total = total + jnp.sum(rows.reshape(BLOCK // 8, 8, C), axis=0)
    sent[pl.ds(OWN_ROWS, 16), :] = sum_rows(jnp.sum(total, axis=0, keepdims=True))


def first(current):
    return pl.pallas_call(
        first_kernel,
        out_shape=jax.ShapeDtypeStruct((SENT_ROWS, C), jnp.bfloat16),
        in_specs=[VMEM],
        out_specs=VMEM,
        compiler_params=pltpu.CompilerParams(vmem_limit_bytes=20 << 20),
        name="first",
    )(current)


def move(table, local, out, at):
    rows = pl.ds(pl.multiple_of(local * BLOCK, BLOCK), BLOCK)
    out[pl.ds(at * BLOCK, BLOCK), :] = table[rows, :]


def pick_early_kernel(asked, own, far1, far3, pass1, pass3, out1, out3):
    pass1[...] = far1[pl.ds(0, HALF_ROWS), :]
    pass3[...] = far3[pl.ds(HALF_ROWS, HALF_ROWS + 16), :]
    for m, out in ((1, out1), (3, out3)):
        for i, (k, table) in enumerate(((0, own), (1, far1), (3, far3))):
            for r in range(CAP):
                move(table, asked[m - 1, k * CAP + r], out, i * CAP + r)


def pick_early(asked, own, far1, far3):
    b16 = jnp.bfloat16
    out = jax.ShapeDtypeStruct((3 * CAP * BLOCK, C), b16)
    return pl.pallas_call(
        pick_early_kernel,
        out_shape=(
            jax.ShapeDtypeStruct((HALF_ROWS, C), b16),
            jax.ShapeDtypeStruct((HALF_ROWS + 16, C), b16),
            out,
            out,
        ),
        in_specs=[SMEM] + [VMEM] * 3,
        out_specs=(VMEM,) * 4,
        compiler_params=pltpu.CompilerParams(vmem_limit_bytes=20 << 20),
        name="pick_early",
    )(asked, own, far1, far3)


def pick_late_kernel(asked, wanted, own, far1, far3, low2, high2, near, out1, out3, out2, line, far2):
    far2[pl.ds(0, HALF_ROWS), :] = low2[...]
    far2[pl.ds(HALF_ROWS, HALF_ROWS + 16), :] = high2[...]
    tables = ((0, own), (1, far1), (3, far3), (2, far2))
    for r in range(CAP):
        move(far2, asked[0, 2 * CAP + r], out1, r)
        move(far2, asked[2, 2 * CAP + r], out3, r)
    for i, (k, table) in enumerate(tables):
        for r in range(CAP):
            move(table, asked[1, k * CAP + r], out2, i * CAP + r)
            if k > 0:
                move(table, wanted[k * CAP + r], near, (k - 1) * CAP + r)
    rows = sum(t[pl.ds(OWN_ROWS, 16), :].astype(jnp.float32) for _, t in tables)
    sums = jnp.sum(rows, axis=0, keepdims=True)
    line[...] = jnp.broadcast_to(sums, (8, C))


def pick_late(asked, wanted, own, far1, far3, low2, high2):
    b16 = jnp.bfloat16
    piece = jax.ShapeDtypeStruct((CAP * BLOCK, C), b16)
    return pl.pallas_call(
        pick_late_kernel,
        out_shape=(
            jax.ShapeDtypeStruct((3 * CAP * BLOCK, C), b16),
            piece,
            piece,
            jax.ShapeDtypeStruct((PICKED * BLOCK, C), b16),
            jax.ShapeDtypeStruct((8, C), jnp.float32),
        ),
        in_specs=[SMEM] * 2 + [VMEM] * 5,
        out_specs=(VMEM,) * 5,
        scratch_shapes=[pltpu.VMEM((SENT_ROWS, C), b16)],
        compiler_params=pltpu.CompilerParams(vmem_limit_bytes=20 << 20),
        name="pick_late",
    )(asked, wanted, own, far1, far3, low2, high2)


def tile_kernel(part, table_count, resume, finish, *refs):
    refs = list(refs)
    lists, words, own = refs[:3]
    tables = refs[3 : 3 + table_count]
    refs = refs[3 + table_count :]
    if resume:
        earlier = refs.pop(0)
    if finish:
        current, all_sums, fresh = refs[:3]
        refs = refs[3:]
        if finish == "more":
            sent = refs.pop(0)
    if finish == "end":
        ready, sems = refs[:2]
        refs = refs[2:]
    total, score_a, score_b, bits = refs[:4]

    row = lax.broadcasted_iota(jnp.int32, (BLOCK, BLOCK), 0)
    bits[...] = lax.shift_left(jnp.ones_like(row), lax.rem(row, 30))
    total[...] = earlier[...] if resume else jnp.zeros_like(total)
    sub = lax.broadcasted_iota(jnp.int32, (8, BLOCK), 0)
    if table_count == 1:
        held = tables[0]
    else:
        held = refs[4]
        at = 0
        for table in tables:
            held[pl.ds(at, table.shape[0]), :] = table[...]
            at += table.shape[0]

    def rows_of(index):
        return pl.ds(pl.multiple_of(index * BLOCK, BLOCK), BLOCK)

    def word_rows(pattern):
        rows = []
        for v in range(BLOCK // 8):
            low, high = 8 * v // 30, (8 * v + 7) // 30
            chunk = jnp.broadcast_to(words[pattern, low : low + 1, :], (8, BLOCK))
            if high != low:
                other = jnp.broadcast_to(words[pattern, high : high + 1, :], (8, BLOCK))
                chunk = jnp.where(sub + 8 * v < 30 * high, chunk, other)
            rows.append(chunk)
        return jnp.concatenate(rows, axis=0)

    size = GROUP[part]

    def target(slot):
        return rows_of(lists[SLOTS + (slot >> 1)])

    def remote(slot, i):
        return held[rows_of(lists[slot + i] & 63), :]

    def score(slot, out):
        mine = own[target(slot), :]
        for i in range(size):
            out[:, i * BLOCK : (i + 1) * BLOCK] = lax.dot_general(
                mine,
                remote(slot, i),
                (((1,), (1,)), ((), ())),
                preferred_element_type=jnp.float32,
            )

    def add(slot, scores):
        weights = []
        for i in range(size):
            packed = word_rows(lists[slot + i] >> 6)
            negative = jnp.minimum(scores[:, i * BLOCK : (i + 1) * BLOCK] * (-1.0 / UNIT), -FLOOR)
            weight = 1.0 / (1.0 - jnp.exp(negative))
            linked = (packed & bits[...]) != 0
            weights.append(jnp.where(linked, weight, 0.0).astype(jnp.bfloat16))
        total[target(slot), :] += jnp.dot(
            jnp.concatenate(weights, axis=1),
            jnp.concatenate([remote(slot, i) for i in range(size)], axis=0),
            preferred_element_type=jnp.float32,
        )

    start, stop = lists[STARTS + part], lists[STARTS + part + 1]
    score(start, score_a)

    def two(i, _):
        slot = pl.multiple_of(start + 2 * size * i, size)
        score(slot + size, score_b)
        add(slot, score_a)
        score(jnp.minimum(slot + 2 * size, stop - size), score_a)
        add(slot + size, score_b)
        return 0

    lax.fori_loop(0, lax.shift_right_logical(stop - start, size.bit_length()), two, 0)

    if not finish:
        return
    col_sums = all_sums[0:1, :]
    moved_sums = jnp.zeros((8, C), jnp.float32)
    copies = []
    for j in range(BPD):
        at = pl.ds(j * BLOCK, BLOCK)
        moved = jnp.maximum(current[at, :] + STEP_SIZE * (total[at, :] - col_sums), 0.0)
        if finish == "more":
            fresh[at, :] = moved
            sent[at, :] = moved.astype(jnp.bfloat16)
            moved_sums = moved_sums + jnp.sum(moved.reshape(BLOCK // 8, 8, C), axis=0)
        else:
            ready[at, :] = moved
            copies.append(pltpu.make_async_copy(ready.at[at, :], fresh.at[at, :], sems.at[j]))
            copies[j].start()
    if finish == "more":
        sent[pl.ds(OWN_ROWS, 16), :] = sum_rows(jnp.sum(moved_sums, axis=0, keepdims=True))
    for copy in copies:
        copy.wait()


def run_tiles(name, part, lists, words, own, tables, earlier=None, current=None, sums=None, finish=""):
    f32 = jnp.float32
    blocks = jax.ShapeDtypeStruct((OWN_ROWS, C), f32)
    args = [lists, words, own, *tables]
    specs = [SMEM] + [VMEM] * (2 + len(tables))
    scratch = []
    out = [blocks]
    if earlier is not None:
        args.append(earlier)
        specs.append(VMEM)
    if finish:
        args += [current, sums]
        specs += [VMEM] * 2
        if finish == "end":
            scratch += [pltpu.VMEM((OWN_ROWS, C), f32), pltpu.SemaphoreType.DMA((BPD,))]
        scratch.append(pltpu.VMEM((OWN_ROWS, C), f32))
        if finish == "more":
            out.append(jax.ShapeDtypeStruct((SENT_ROWS, C), jnp.bfloat16))
    scratch += [
        pltpu.VMEM((BLOCK, GROUP[part] * BLOCK), f32),
        pltpu.VMEM((BLOCK, GROUP[part] * BLOCK), f32),
        pltpu.VMEM((BLOCK, BLOCK), jnp.int32),
    ]
    if len(tables) > 1:
        scratch.append(pltpu.VMEM((sum(t.shape[0] for t in tables), C), jnp.bfloat16))
    return pl.pallas_call(
        functools.partial(tile_kernel, part, len(tables), earlier is not None, finish),
        out_shape=tuple(out),
        in_specs=specs,
        out_specs=(HBM,) if finish == "end" else (VMEM,) * len(out),
        scratch_shapes=scratch,
        compiler_params=pltpu.CompilerParams(vmem_limit_bytes=24 << 20),
        name=name,
    )(*args)


def per_device(affiliations, tile_block, tile_target, tile_pattern, tile_count, block_home, patterns):
    y, x = lax.axis_index("rows_0"), lax.axis_index("rows_1")
    core = lax.axis_index("cols_1")
    place = jnp.stack([jnp.where(core == 0, x, y), jnp.where(core == 0, y, x), core])
    current = affiliations
    own = first(current)
    requests, codes = ask(
        place.astype(jnp.int32), tile_block[0], tile_target[0], tile_count, block_home
    )
    requests = requests.reshape(SIDE, PICKED)
    asked = jnp.stack([fetch(requests[m], 0, SIDE - m) for m in (1, 2, 3)])
    words = jnp.concatenate([patterns, jnp.zeros((1, *patterns.shape[1:]), jnp.int32)], axis=0)

    lists = sort_tiles(codes, tile_pattern[0], tile_count)
    for step in range(STEPS):
        far1, far3 = fetch(own, 1, 0), fetch(own, 3, 0)
        pass1, pass3, out1, out3 = pick_early(asked, own, far1, far3)
        low2, high2 = fetch(pass1, 1, 0), fetch(pass3, 3, 0)
        side1, side3 = fetch(out1, 0, 1), fetch(out3, 0, 3)
        lists, low2, high2 = lax.optimization_barrier((lists, low2, high2))
        near, out1, out3, out2, line = pick_late(asked, requests[0], own, far1, far3, low2, high2)
        lines = tuple(fetch(line, 0, m) for m in (1, 3, 2))
        lines, out2, side1, side3 = lax.optimization_barrier((lines, out2, side1, side3))
        side2 = fetch(out2, 0, 2)
        late1, late3 = fetch(out1, 0, 1), fetch(out3, 0, 3)
        col_sums = sum_over_cols(line + lines[0] + lines[1] + lines[2])
        tables = (side1, side3, near)
        (total,) = run_tiles("sides", 0, lists, words, own, tables)
        (total,) = run_tiles("across", 1, lists, words, own, (side2,), total)
        total, late1, late3 = lax.optimization_barrier((total, late1, late3))
        finish = "more" if step < STEPS - 1 else "end"
        current, *own_next = run_tiles(
            "late", 2, lists, words, own, (late1, late3), total, current, col_sums, finish
        )
        if own_next:
            (own,) = own_next
    return current


def solution(mesh):
    torus = Mesh(mesh.devices.reshape(4, 4, 4, 2), ALL)
    return jax.shard_map(
        per_device,
        mesh=torus,
        in_specs=(P(ALL, None), P(ALL, None), P(ALL, None), P(ALL, None), P(ALL), P(), P()),
        out_specs=P(ALL, None),
        check_vma=False,
    )
```

profile of v0, /device:TPU:32, one launch (start us, length us, event | category | flops | bytes accessed | tf_op | source)
XLA Modules:
  0.0 167.4 jit_solution(15988540292488301632)
XLA Ops:
  0.0 1.6 copy-done
  1.6 0.1 first.1.own.refs_2_
  1.7 1.6 collective-permute-start.4
  3.3 1.7 %collective-permute-start.3 = (bf16[1040,512]{1,0:T(8,128)(2,1)S(1)}, bf16[1040,512]{1,0:T(8,128)(2,1)S(1)}, u32[]{:S(2)}, u32[]{:S(2)}) collective-permute-start(bf16[1040,512]{1,0:T(8,128)(2,1)S(1)} %first.1.own.refs_2_), channel_id=1, source_target_pairs={{8,0},{33,1},{10,2},{35,3},{12,4},{37,5},{14,6},{39,7},{16,8},{41,... | collective-permute-start | bytes 3194888 | tf_op jit(solution)/shard_map/ppermute | solution.py:55
  5.7 0.1 pad_add_fusion.1.place
  5.8 3.9 %ask.1 = (s32[64]{0:T(128)S(1)}, s32[240]{0:T(256)S(1)}) custom-call(s32[3]{0:T(128)S(1)} %pad_add_fusion.1.place, s32[240]{0:T(256)S(1)} %bitcast.9, s32[240]{0:T(256)S(1)} %bitcast.10, s32[1]{0:T(128)S(6)} %copy.9.count, s32[1024]{0:T(1024)S(1)} %copy-done.2), custom_call_target="tpu_custom_call" | custom-call | tf_op jit(solution)/shard_map/ask/pallas_call | solution.py:117
  9.7 0.1 fusion
  9.7 2.8 %collective-permute-start.2 = (s32[16]{0:T(128)S(1)}, s32[16]{0:T(128)S(1)}, u32[]{:S(2)}, u32[]{:S(2)}) collective-permute-start(s32[16]{0:T(128)S(1)} %get-tuple-element.98), channel_id=1, source_target_pairs={{32,0},{9,1},{34,2},{11,3},{36,4},{13,5},{38,6},{15,7},{40,8},{17,... | collective-permute-start | bytes 200 | tf_op jit(solution)/shard_map/ppermute | solution.py:55
  12.5 0.7 collective-permute-start.1
  13.2 1.0 collective-permute-start
  14.2 3.4 %collective-permute-done.1 = s32[16]{0:T(128)S(1)} collective-permute-done((s32[16]{0:T(128)S(1)}, s32[16]{0:T(128)S(1)}, u32[]{:S(2)}, u32[]{:S(2)}) %collective-permute-start.1) | collective-permute-done | bytes 96 | tf_op jit(solution)/shard_map/ppermute | solution.py:55
  17.6 0.3 collective-permute-done
  18.0 0.3 collective-permute-done.3.far1
  18.3 0.8 pick_early.2
  19.1 3.1 %collective-permute-start.10 = (bf16[1536,512]{1,0:T(8,128)(2,1)S(1)}, bf16[1536,512]{1,0:T(8,128)(2,1)S(1)}, u32[]{:S(2)}, u32[]{:S(2)}) collective-permute-start(bf16[1536,512]{1,0:T(8,128)(2,1)S(1)} %get-tuple-element.60), channel_id=1, source_target_pairs={{32,0},{9,1},{34,2},{11,3},{36,4},{13,5},{38,6},{15,7},{40,8},{17,... | collective-permute-start | bytes 4718600 | tf_op jit(solution)/shard_map/ppermute | solution.py:55
  22.2 1.5 collective-permute-start.6
  23.7 1.7 %collective-permute-start.5 = (bf16[512,512]{1,0:T(8,128)(2,1)S(1)}, bf16[512,512]{1,0:T(8,128)(2,1)S(1)}, u32[]{:S(2)}, u32[]{:S(2)}) collective-permute-start(bf16[512,512]{1,0:T(8,128)(2,1)S(1)} %get-tuple-element.53), channel_id=1, source_target_pairs={{8,0},{33,1},{10,2},{35,3},{12,4},{37,5},{14,6},{39,7},{16,8},{41,... | collective-permute-start | bytes 1572872 | tf_op jit(solution)/shard_map/ppermute | solution.py:55
  25.4 3.8 %sort_tiles.1.refs_0_ = s32[488]{0:T(512)S(1)} custom-call(s32[240]{0:T(256)S(1)} %get-tuple-element.51.codes, s32[240]{0:T(256)S(1)} %bitcast.11, s32[1]{0:T(128)S(6)} %copy.9.count), custom_call_target="tpu_custom_call" | custom-call | tf_op jit(solution)/shard_map/sort_tiles/pallas_call | solution.py:165
  29.2 9.3 %collective-permute-done.5.low2 = bf16[512,512]{1,0:T(8,128)(2,1)S(1)} collective-permute-done((bf16[512,512]{1,0:T(8,128)(2,1)S(1)}, bf16[512,512]{1,0:T(8,128)(2,1)S(1)}, u32[]{:S(2)}, u32[]{:S(2)}) %collective-permute-start.5) | collective-permute-done | bytes 524320 | tf_op jit(solution)/shard_map/ppermute | solution.py:55
  38.6 0.1 collective-permute-done.6.high2
  38.6 1.0 pick_late.2
  39.6 2.3 %collective-permute-start.9 = (f32[8,512]{1,0:T(8,128)S(1)}, f32[8,512]{1,0:T(8,128)S(1)}, u32[]{:S(2)}, u32[]{:S(2)}) collective-permute-start(f32[8,512]{1,0:T(8,128)S(1)} %get-tuple-element.58), channel_id=1, source_target_pairs={{64,0},{17,1},{66,2},{19,3},{68,4},{21,5},{70,6},{23,7},{72,8},{25... | collective-permute-start | bytes 49160 | tf_op jit(solution)/shard_map/ppermute | solution.py:55
  41.9 1.9 %collective-permute-start.8 = (f32[8,512]{1,0:T(8,128)S(1)}, f32[8,512]{1,0:T(8,128)S(1)}, u32[]{:S(2)}, u32[]{:S(2)}) collective-permute-start(f32[8,512]{1,0:T(8,128)S(1)} %get-tuple-element.58), channel_id=1, source_target_pairs={{96,0},{25,1},{98,2},{27,3},{100,4},{29,5},{102,6},{31,7},{104,8},... | collective-permute-start | bytes 49160 | tf_op jit(solution)/shard_map/ppermute | solution.py:55
  43.8 1.3 collective-permute-start.7
  45.1 3.2 %collective-permute-done.9 = f32[8,512]{1,0:T(8,128)S(1)} collective-permute-done((f32[8,512]{1,0:T(8,128)S(1)}, f32[8,512]{1,0:T(8,128)S(1)}, u32[]{:S(2)}, u32[]{:S(2)}) %collective-permute-start.9) | collective-permute-done | bytes 16416 | tf_op jit(solution)/shard_map/ppermute | solution.py:55
  48.3 0.7 collective-permute-start.12
  49.1 1.7 %collective-permute-start.13 = (bf16[512,512]{1,0:T(8,128)(2,1)S(1)}, bf16[512,512]{1,0:T(8,128)(2,1)S(1)}, u32[]{:S(2)}, u32[]{:S(2)}) collective-permute-start(bf16[512,512]{1,0:T(8,128)(2,1)S(1)} %get-tuple-element.66), channel_id=1, source_target_pairs={{32,0},{9,1},{34,2},{11,3},{36,4},{13,5},{38,6},{15,7},{40,8},{17,... | collective-permute-start | bytes 1572872 | tf_op jit(solution)/shard_map/ppermute | solution.py:55
  50.8 0.3 collective-permute-start.14
  51.1 1.2 collective-permute-done.15
  52.3 0.1 collective-permute-start.16
  52.4 3.6 %collective-permute-done.16 = f32[8,512]{1,0:T(8,128)S(1)} collective-permute-done((f32[8,512]{1,0:T(8,128)S(1)}, f32[8,512]{1,0:T(8,128)S(1)}, u32[]{:S(2)}, u32[]{:S(2)}) %collective-permute-start.16) | collective-permute-done | bytes 16416 | tf_op jit(solution)/shard_map/ppermute | solution.py:62
  56.0 3.0 %collective-permute-start.17 = (f32[8,512]{1,0:T(8,128)S(1)}, f32[8,512]{1,0:T(8,128)S(1)}, u32[]{:S(2)}, u32[]{:S(2)}) collective-permute-start(f32[8,512]{1,0:T(8,128)S(1)} %add.42), channel_id=1, source_target_pairs={{0,4},{2,6},{4,0},{6,2},{1,5},{3,7},{5,1},{7,3},{8,12},{10,14},{12... | collective-permute-start | bytes 49160 | tf_op jit(solution)/shard_map/ppermute | solution.py:62
  59.0 0.3 copy.8
  59.4 7.2 %sides.2.refs_4_ = f32[1024,512]{1,0:T(8,128)S(1)} custom-call(s32[488]{0:T(512)S(1)} %sort_tiles.1.refs_0_, s32[193,5,128]{2,1,0:T(8,128)S(1)} %concatenate.3.refs_1_, bf16[1040,512]{1,0:T(8,128)(2,1)S(1)} %first.1.own.refs_2_, bf16[1536,512]{1,0:T(8,128)(2,1)S(1)} %collective-permute-done.10.refs_3_, ...), custom_call_target="tpu_custom_call" | custom-call | tf_op jit(solution)/shard_map/sides/pallas_call | solution.py:411
  66.6 9.4 %collective-permute-done.12.refs_3_ = bf16[2048,512]{1,0:T(8,128)(2,1)S(1)} collective-permute-done((bf16[2048,512]{1,0:T(8,128)(2,1)S(1)}, bf16[2048,512]{1,0:T(8,128)(2,1)S(1)}, u32[]{:S(2)}, u32[]{:S(2)}) %collective-permute-start.12) | collective-permute-done | bytes 2097184 | tf_op jit(solution)/shard_map/ppermute | solution.py:55
  76.1 4.8 %across.2.refs_5_ = f32[1024,512]{1,0:T(8,128)S(1)} custom-call(s32[488]{0:T(512)S(1)} %sort_tiles.1.refs_0_, s32[193,5,128]{2,1,0:T(8,128)S(1)} %concatenate.3.refs_1_, bf16[1040,512]{1,0:T(8,128)(2,1)S(1)} %first.1.own.refs_2_, bf16[2048,512]{1,0:T(8,128)(2,1)S(1)} %collective-permute-done.12.refs_3_, f32[1024,512]{1,0:T(8,128)S(1)} %sides.2.refs_4_), custom_call_target="tpu_custom_call" | custom-call | tf_op jit(solution)/shard_map/across/pallas_call | solution.py:411
  80.9 0.7 collective-permute-done.14.refs_4_
  81.6 2.6 %late.2 = (f32[1024,512]{1,0:T(8,128)S(1)}, bf16[1040,512]{1,0:T(8,128)(2,1)S(1)}) custom-call(s32[488]{0:T(512)S(1)} %sort_tiles.1.refs_0_, s32[193,5,128]{2,1,0:T(8,128)S(1)} %concatenate.3.refs_1_, bf16[1040,512]{1,0:T(8,128)(2,1)S(1)} %first.1.own.refs_2_, bf16[512,512]{1,0:T(8,128)(2,1)S(1)} %collective-permute-done.13.refs_3_, ...), custom_call_target="tpu_custom_call" | custom-call | tf_op jit(solution)/shard_map/late/pallas_call | solution.py:411
  84.2 0.7 collective-permute-start.19
  84.9 3.2 %collective-permute-start.18 = (bf16[1040,512]{1,0:T(8,128)(2,1)S(1)}, bf16[1040,512]{1,0:T(8,128)(2,1)S(1)}, u32[]{:S(2)}, u32[]{:S(2)}) collective-permute-start(bf16[1040,512]{1,0:T(8,128)(2,1)S(1)} %get-tuple-element.74.own.refs_2_), channel_id=1, source_target_pairs={{8,0},{33,1},{10,2},{35,3},{12,4},{37,5},{14,6},{39,7},{16,8},{41,... | collective-permute-start | bytes 3194888 | tf_op jit(solution)/shard_map/ppermute | solution.py:55
  88.1 12.9 %collective-permute-done.19.far3 = bf16[1040,512]{1,0:T(8,128)(2,1)S(1)} collective-permute-done((bf16[1040,512]{1,0:T(8,128)(2,1)S(1)}, bf16[1040,512]{1,0:T(8,128)(2,1)S(1)}, u32[]{:S(2)}, u32[]{:S(2)}) %collective-permute-start.19) | collective-permute-done | bytes 1064992 | tf_op jit(solution)/shard_map/ppermute | solution.py:55
  101.0 0.8 pick_early.3
  101.8 2.6 %collective-permute-start.25 = (bf16[1536,512]{1,0:T(8,128)(2,1)S(1)}, bf16[1536,512]{1,0:T(8,128)(2,1)S(1)}, u32[]{:S(2)}, u32[]{:S(2)}) collective-permute-start(bf16[1536,512]{1,0:T(8,128)(2,1)S(1)} %get-tuple-element.82), channel_id=1, source_target_pairs={{32,0},{9,1},{34,2},{11,3},{36,4},{13,5},{38,6},{15,7},{40,8},{17,... | collective-permute-start | bytes 4718600 | tf_op jit(solution)/shard_map/ppermute | solution.py:55
  104.4 2.4 %collective-permute-start.21 = (bf16[528,512]{1,0:T(8,128)(2,1)S(1)}, bf16[528,512]{1,0:T(8,128)(2,1)S(1)}, u32[]{:S(2)}, u32[]{:S(2)}) collective-permute-start(bf16[528,512]{1,0:T(8,128)(2,1)S(1)} %get-tuple-element.76), channel_id=1, source_target_pairs={{24,0},{97,1},{26,2},{99,3},{28,4},{101,5},{30,6},{103,7},{0,8},{1... | collective-permute-start | bytes 1622024 | tf_op jit(solution)/shard_map/ppermute | solution.py:55
  106.8 0.8 collective-permute-start.20
  107.6 14.3 %collective-permute-done.20.low2 = bf16[512,512]{1,0:T(8,128)(2,1)S(1)} collective-permute-done((bf16[512,512]{1,0:T(8,128)(2,1)S(1)}, bf16[512,512]{1,0:T(8,128)(2,1)S(1)}, u32[]{:S(2)}, u32[]{:S(2)}) %collective-permute-start.20) | collective-permute-done | bytes 524320 | tf_op jit(solution)/shard_map/ppermute | solution.py:55
  121.9 1.0 pick_late.3
  122.9 1.4 collective-permute-start.24
  124.2 2.6 %collective-permute-start.23 = (f32[8,512]{1,0:T(8,128)S(1)}, f32[8,512]{1,0:T(8,128)S(1)}, u32[]{:S(2)}, u32[]{:S(2)}) collective-permute-start(f32[8,512]{1,0:T(8,128)S(1)} %get-tuple-element.80), channel_id=1, source_target_pairs={{96,0},{25,1},{98,2},{27,3},{100,4},{29,5},{102,6},{31,7},{104,8},... | collective-permute-start | bytes 49160 | tf_op jit(solution)/shard_map/ppermute | solution.py:55
  126.8 0.7 collective-permute-start.22
  127.5 1.8 %collective-permute-done.24 = f32[8,512]{1,0:T(8,128)S(1)} collective-permute-done((f32[8,512]{1,0:T(8,128)S(1)}, f32[8,512]{1,0:T(8,128)S(1)}, u32[]{:S(2)}, u32[]{:S(2)}) %collective-permute-start.24) | collective-permute-done | bytes 16416 | tf_op jit(solution)/shard_map/ppermute | solution.py:55
  129.4 1.2 collective-permute-done.22
  130.5 0.7 collective-permute-start.27
  131.2 2.1 %collective-permute-start.28 = (bf16[512,512]{1,0:T(8,128)(2,1)S(1)}, bf16[512,512]{1,0:T(8,128)(2,1)S(1)}, u32[]{:S(2)}, u32[]{:S(2)}) collective-permute-start(bf16[512,512]{1,0:T(8,128)(2,1)S(1)} %get-tuple-element.88), channel_id=1, source_target_pairs={{32,0},{9,1},{34,2},{11,3},{36,4},{13,5},{38,6},{15,7},{40,8},{17,... | collective-permute-start | bytes 1572872 | tf_op jit(solution)/shard_map/ppermute | solution.py:55
  133.3 0.1 collective-permute-start.30
  133.4 1.2 collective-permute-done.30
  134.6 1.2 collective-permute-start.31
  135.8 2.6 %collective-permute-done.31 = f32[8,512]{1,0:T(8,128)S(1)} collective-permute-done((f32[8,512]{1,0:T(8,128)S(1)}, f32[8,512]{1,0:T(8,128)S(1)}, u32[]{:S(2)}, u32[]{:S(2)}) %collective-permute-start.31) | collective-permute-done | bytes 16416 | tf_op jit(solution)/shard_map/ppermute | solution.py:62
  138.3 2.1 %collective-permute-start.32 = (f32[8,512]{1,0:T(8,128)S(1)}, f32[8,512]{1,0:T(8,128)S(1)}, u32[]{:S(2)}, u32[]{:S(2)}) collective-permute-start(f32[8,512]{1,0:T(8,128)S(1)} %add.48), channel_id=1, source_target_pairs={{0,4},{2,6},{4,0},{6,2},{1,5},{3,7},{5,1},{7,3},{8,12},{10,14},{12... | collective-permute-start | bytes 49160 | tf_op jit(solution)/shard_map/ppermute | solution.py:62
  140.5 7.3 %sides.3.refs_4_ = f32[1024,512]{1,0:T(8,128)S(1)} custom-call(s32[488]{0:T(512)S(1)} %sort_tiles.1.refs_0_, s32[193,5,128]{2,1,0:T(8,128)S(1)} %concatenate.3.refs_1_, bf16[1040,512]{1,0:T(8,128)(2,1)S(1)} %get-tuple-element.74.own.refs_2_, bf16[1536,512]{1,0:T(8,128)(2,1)S(1)} %collective-permute-done.25.refs_3_, ...), custom_call_target="tpu_custom_call" | custom-call | tf_op jit(solution)/shard_map/sides/pallas_call | solution.py:411
  147.8 10.4 %collective-permute-done.27.refs_3_ = bf16[2048,512]{1,0:T(8,128)(2,1)S(1)} collective-permute-done((bf16[2048,512]{1,0:T(8,128)(2,1)S(1)}, bf16[2048,512]{1,0:T(8,128)(2,1)S(1)}, u32[]{:S(2)}, u32[]{:S(2)}) %collective-permute-start.27) | collective-permute-done | bytes 2097184 | tf_op jit(solution)/shard_map/ppermute | solution.py:55
  158.2 4.8 %across.3.refs_5_ = f32[1024,512]{1,0:T(8,128)S(1)} custom-call(s32[488]{0:T(512)S(1)} %sort_tiles.1.refs_0_, s32[193,5,128]{2,1,0:T(8,128)S(1)} %concatenate.3.refs_1_, bf16[1040,512]{1,0:T(8,128)(2,1)S(1)} %get-tuple-element.74.own.refs_2_, bf16[2048,512]{1,0:T(8,128)(2,1)S(1)} %collective-permute-done.27.refs_3_, f32[1024,512]{1,0:T(8,128)S(1)} %sides.3.refs_4_), custom_call_target="tpu_custom_call" | custom-call | tf_op jit(solution)/shard_map/across/pallas_call | solution.py:411
  163.0 0.7 collective-permute-done.29.refs_4_
  163.7 3.6 %late.3 = f32[1024,512]{1,0:T(8,128)} custom-call(s32[488]{0:T(512)S(1)} %sort_tiles.1.refs_0_, s32[193,5,128]{2,1,0:T(8,128)S(1)} %concatenate.3.refs_1_, bf16[1040,512]{1,0:T(8,128)(2,1)S(1)} %get-tuple-element.74.own.refs_2_, bf16[512,512]{1,0:T(8,128)(2,1)S(1)} %collective-permute-done.28.refs_3_, bf16[512,512]{1,0:T(8,128)(2,1)S(1)} %collective-permute-done.29.refs_4_, ...), custom_call_target="tpu_custom_call" | custom-call | tf_op jit(solution)/shard_map/late/pallas_call | solution.py:411
  (42 shorter events, 0.3 us)
Async XLA Ops:
  0.0 1.6 copy-start
  1.6 4.2 %copy-start.2 = (s32[1024]{0:T(1024)S(1)}, s32[1024]{0:T(1024)}, u32[]{:S(2)}) copy-start(s32[1024]{0:T(1024)} %home.1) | copy-start | bytes 12292
  1.6 4.2 %copy-start.3 = (s32[1,240]{1,0:T(1,128)S(1)}, s32[1,240]{1,0:T(1,128)}, u32[]{:S(2)}) copy-start(s32[1,240]{1,0:T(1,128)} %param.8) | copy-start | bytes 2884
  1.6 4.2 %copy-start.4 = (s32[1,240]{1,0:T(1,128)S(1)}, s32[1,240]{1,0:T(1,128)}, u32[]{:S(2)}) copy-start(s32[1,240]{1,0:T(1,128)} %param.9) | copy-start | bytes 2884
  1.7 16.3 %collective-permute-start.4 = (bf16[1040,512]{1,0:T(8,128)(2,1)S(1)}, bf16[1040,512]{1,0:T(8,128)(2,1)S(1)}, u32[]{:S(2)}, u32[]{:S(2)}) collective-permute-start(bf16[1040,512]{1,0:T(8,128)(2,1)S(1)} %first.1.own.refs_2_), channel_id=1, source_target_pairs={{24,0},{97,1},{26,2},{99,3},{28,4},{101,5},{30,6},{103,7},{0,8},{1... | collective-permute-start | bytes 3194888 | tf_op jit(solution)/shard_map/ppermute | solution.py:55
  3.3 15.0 %collective-permute-start.3 = (bf16[1040,512]{1,0:T(8,128)(2,1)S(1)}, bf16[1040,512]{1,0:T(8,128)(2,1)S(1)}, u32[]{:S(2)}, u32[]{:S(2)}) collective-permute-start(bf16[1040,512]{1,0:T(8,128)(2,1)S(1)} %first.1.own.refs_2_), channel_id=1, source_target_pairs={{8,0},{33,1},{10,2},{35,3},{12,4},{37,5},{14,6},{39,7},{16,8},{41,... | collective-permute-start | bytes 3194888 | tf_op jit(solution)/shard_map/ppermute | solution.py:55
  9.7 4.4 %collective-permute-start.2 = (s32[16]{0:T(128)S(1)}, s32[16]{0:T(128)S(1)}, u32[]{:S(2)}, u32[]{:S(2)}) collective-permute-start(s32[16]{0:T(128)S(1)} %get-tuple-element.98), channel_id=1, source_target_pairs={{32,0},{9,1},{34,2},{11,3},{36,4},{13,5},{38,6},{15,7},{40,8},{17,... | collective-permute-start | bytes 200 | tf_op jit(solution)/shard_map/ppermute | solution.py:55
  12.5 5.1 %collective-permute-start.1 = (s32[16]{0:T(128)S(1)}, s32[16]{0:T(128)S(1)}, u32[]{:S(2)}, u32[]{:S(2)}) collective-permute-start(s32[16]{0:T(128)S(1)} %get-tuple-element.99), channel_id=1, source_target_pairs={{64,0},{17,1},{66,2},{19,3},{68,4},{21,5},{70,6},{23,7},{72,8},{25... | collective-permute-start | bytes 200 | tf_op jit(solution)/shard_map/ppermute | solution.py:55
  13.2 4.8 %collective-permute-start = (s32[16]{0:T(128)S(1)}, s32[16]{0:T(128)S(1)}, u32[]{:S(2)}, u32[]{:S(2)}) collective-permute-start(s32[16]{0:T(128)S(1)} %get-tuple-element.100), channel_id=1, source_target_pairs={{96,0},{25,1},{98,2},{27,3},{100,4},{29,5},{102,6},{31,7},{104,8},... | collective-permute-start | bytes 200 | tf_op jit(solution)/shard_map/ppermute | solution.py:55
  18.0 7.5 %copy-start.5 = (s32[1,240]{1,0:T(1,128)S(1)}, s32[1,240]{1,0:T(1,128)}, u32[]{:S(2)}) copy-start(s32[1,240]{1,0:T(1,128)} %param.10) | copy-start | bytes 2884
  19.1 29.2 %collective-permute-start.10 = (bf16[1536,512]{1,0:T(8,128)(2,1)S(1)}, bf16[1536,512]{1,0:T(8,128)(2,1)S(1)}, u32[]{:S(2)}, u32[]{:S(2)}) collective-permute-start(bf16[1536,512]{1,0:T(8,128)(2,1)S(1)} %get-tuple-element.60), channel_id=1, source_target_pairs={{32,0},{9,1},{34,2},{11,3},{36,4},{13,5},{38,6},{15,7},{40,8},{17,... | collective-permute-start | bytes 4718600 | tf_op jit(solution)/shard_map/ppermute | solution.py:55
  22.2 26.1 %collective-permute-start.11 = (bf16[1536,512]{1,0:T(8,128)(2,1)S(1)}, bf16[1536,512]{1,0:T(8,128)(2,1)S(1)}, u32[]{:S(2)}, u32[]{:S(2)}) collective-permute-start(bf16[1536,512]{1,0:T(8,128)(2,1)S(1)} %get-tuple-element.61), channel_id=1, source_target_pairs={{96,0},{25,1},{98,2},{27,3},{100,4},{29,5},{102,6},{31,7},{104,8},... | collective-permute-start | bytes 4718600 | tf_op jit(solution)/shard_map/ppermute | solution.py:55
  22.2 16.4 %collective-permute-start.6 = (bf16[528,512]{1,0:T(8,128)(2,1)S(1)}, bf16[528,512]{1,0:T(8,128)(2,1)S(1)}, u32[]{:S(2)}, u32[]{:S(2)}) collective-permute-start(bf16[528,512]{1,0:T(8,128)(2,1)S(1)} %get-tuple-element.54), channel_id=1, source_target_pairs={{24,0},{97,1},{26,2},{99,3},{28,4},{101,5},{30,6},{103,7},{0,8},{1... | collective-permute-start | bytes 1622024 | tf_op jit(solution)/shard_map/ppermute | solution.py:55
  23.7 14.9 %collective-permute-start.5 = (bf16[512,512]{1,0:T(8,128)(2,1)S(1)}, bf16[512,512]{1,0:T(8,128)(2,1)S(1)}, u32[]{:S(2)}, u32[]{:S(2)}) collective-permute-start(bf16[512,512]{1,0:T(8,128)(2,1)S(1)} %get-tuple-element.53), channel_id=1, source_target_pairs={{8,0},{33,1},{10,2},{35,3},{12,4},{37,5},{14,6},{39,7},{16,8},{41,... | collective-permute-start | bytes 1572872 | tf_op jit(solution)/shard_map/ppermute | solution.py:55
  38.6 20.4 %copy-start.6 = (s32[192,5,128]{2,0,1:T(8,128)S(1)}, s32[192,5,128]{2,0,1:T(8,128)}, u32[]{:S(2)}) copy-start(s32[192,5,128]{2,0,1:T(8,128)} %param.13) | copy-start | bytes 1474564
  39.6 8.7 %collective-permute-start.9 = (f32[8,512]{1,0:T(8,128)S(1)}, f32[8,512]{1,0:T(8,128)S(1)}, u32[]{:S(2)}, u32[]{:S(2)}) collective-permute-start(f32[8,512]{1,0:T(8,128)S(1)} %get-tuple-element.58), channel_id=1, source_target_pairs={{64,0},{17,1},{66,2},{19,3},{68,4},{21,5},{70,6},{23,7},{72,8},{25... | collective-permute-start | bytes 49160 | tf_op jit(solution)/shard_map/ppermute | solution.py:55
  41.9 6.4 %collective-permute-start.8 = (f32[8,512]{1,0:T(8,128)S(1)}, f32[8,512]{1,0:T(8,128)S(1)}, u32[]{:S(2)}, u32[]{:S(2)}) collective-permute-start(f32[8,512]{1,0:T(8,128)S(1)} %get-tuple-element.58), channel_id=1, source_target_pairs={{96,0},{25,1},{98,2},{27,3},{100,4},{29,5},{102,6},{31,7},{104,8},... | collective-permute-start | bytes 49160 | tf_op jit(solution)/shard_map/ppermute | solution.py:55
  43.8 4.6 %collective-permute-start.7 = (f32[8,512]{1,0:T(8,128)S(1)}, f32[8,512]{1,0:T(8,128)S(1)}, u32[]{:S(2)}, u32[]{:S(2)}) collective-permute-start(f32[8,512]{1,0:T(8,128)S(1)} %get-tuple-element.58), channel_id=1, source_target_pairs={{32,0},{9,1},{34,2},{11,3},{36,4},{13,5},{38,6},{15,7},{40,8},{17,... | collective-permute-start | bytes 49160 | tf_op jit(solution)/shard_map/ppermute | solution.py:55
  48.3 27.7 %collective-permute-start.12 = (bf16[2048,512]{1,0:T(8,128)(2,1)S(1)}, bf16[2048,512]{1,0:T(8,128)(2,1)S(1)}, u32[]{:S(2)}, u32[]{:S(2)}) collective-permute-start(bf16[2048,512]{1,0:T(8,128)(2,1)S(1)} %get-tuple-element.62), channel_id=1, source_target_pairs={{64,0},{17,1},{66,2},{19,3},{68,4},{21,5},{70,6},{23,7},{72,8},{25... | collective-permute-start | bytes 6291464 | tf_op jit(solution)/shard_map/ppermute | solution.py:55
  49.1 31.8 %collective-permute-start.13 = (bf16[512,512]{1,0:T(8,128)(2,1)S(1)}, bf16[512,512]{1,0:T(8,128)(2,1)S(1)}, u32[]{:S(2)}, u32[]{:S(2)}) collective-permute-start(bf16[512,512]{1,0:T(8,128)(2,1)S(1)} %get-tuple-element.66), channel_id=1, source_target_pairs={{32,0},{9,1},{34,2},{11,3},{36,4},{13,5},{38,6},{15,7},{40,8},{17,... | collective-permute-start | bytes 1572872 | tf_op jit(solution)/shard_map/ppermute | solution.py:55
  50.8 30.8 %collective-permute-start.14 = (bf16[512,512]{1,0:T(8,128)(2,1)S(1)}, bf16[512,512]{1,0:T(8,128)(2,1)S(1)}, u32[]{:S(2)}, u32[]{:S(2)}) collective-permute-start(bf16[512,512]{1,0:T(8,128)(2,1)S(1)} %get-tuple-element.67), channel_id=1, source_target_pairs={{96,0},{25,1},{98,2},{27,3},{100,4},{29,5},{102,6},{31,7},{104,8},... | collective-permute-start | bytes 1572872 | tf_op jit(solution)/shard_map/ppermute | solution.py:55
  51.1 1.2 collective-permute-start.15
  52.3 3.7 %collective-permute-start.16 = (f32[8,512]{1,0:T(8,128)S(1)}, f32[8,512]{1,0:T(8,128)S(1)}, u32[]{:S(2)}, u32[]{:S(2)}) collective-permute-start(f32[8,512]{1,0:T(8,128)S(1)} %add.41), channel_id=1, source_target_pairs={{0,2},{2,0},{4,6},{6,4},{1,3},{3,1},{5,7},{7,5},{8,10},{10,8},{12,... | collective-permute-start | bytes 49160 | tf_op jit(solution)/shard_map/ppermute | solution.py:62
  56.0 10.6 %collective-permute-start.17 = (f32[8,512]{1,0:T(8,128)S(1)}, f32[8,512]{1,0:T(8,128)S(1)}, u32[]{:S(2)}, u32[]{:S(2)}) collective-permute-start(f32[8,512]{1,0:T(8,128)S(1)} %add.42), channel_id=1, source_target_pairs={{0,4},{2,6},{4,0},{6,2},{1,5},{3,7},{5,1},{7,3},{8,12},{10,14},{12... | collective-permute-start | bytes 49160 | tf_op jit(solution)/shard_map/ppermute | solution.py:62
  66.6 15.0 %copy-start.1 = (f32[1024,512]{1,0:T(8,128)S(1)}, f32[1024,512]{1,0:T(8,128)}, u32[]{:S(2)}) copy-start(f32[1024,512]{1,0:T(8,128)} %refs_6_.1) | copy-start | bytes 6291460
  84.2 16.7 %collective-permute-start.19 = (bf16[1040,512]{1,0:T(8,128)(2,1)S(1)}, bf16[1040,512]{1,0:T(8,128)(2,1)S(1)}, u32[]{:S(2)}, u32[]{:S(2)}) collective-permute-start(bf16[1040,512]{1,0:T(8,128)(2,1)S(1)} %get-tuple-element.74.own.refs_2_), channel_id=1, source_target_pairs={{24,0},{97,1},{26,2},{99,3},{28,4},{101,5},{30,6},{103,7},{0,8},{1... | collective-permute-start | bytes 3194888 | tf_op jit(solution)/shard_map/ppermute | solution.py:55
  84.9 16.1 %collective-permute-start.18 = (bf16[1040,512]{1,0:T(8,128)(2,1)S(1)}, bf16[1040,512]{1,0:T(8,128)(2,1)S(1)}, u32[]{:S(2)}, u32[]{:S(2)}) collective-permute-start(bf16[1040,512]{1,0:T(8,128)(2,1)S(1)} %get-tuple-element.74.own.refs_2_), channel_id=1, source_target_pairs={{8,0},{33,1},{10,2},{35,3},{12,4},{37,5},{14,6},{39,7},{16,8},{41,... | collective-permute-start | bytes 3194888 | tf_op jit(solution)/shard_map/ppermute | solution.py:55
  101.8 28.7 %collective-permute-start.25 = (bf16[1536,512]{1,0:T(8,128)(2,1)S(1)}, bf16[1536,512]{1,0:T(8,128)(2,1)S(1)}, u32[]{:S(2)}, u32[]{:S(2)}) collective-permute-start(bf16[1536,512]{1,0:T(8,128)(2,1)S(1)} %get-tuple-element.82), channel_id=1, source_target_pairs={{32,0},{9,1},{34,2},{11,3},{36,4},{13,5},{38,6},{15,7},{40,8},{17,... | collective-permute-start | bytes 4718600 | tf_op jit(solution)/shard_map/ppermute | solution.py:55
  104.4 26.2 %collective-permute-start.26 = (bf16[1536,512]{1,0:T(8,128)(2,1)S(1)}, bf16[1536,512]{1,0:T(8,128)(2,1)S(1)}, u32[]{:S(2)}, u32[]{:S(2)}) collective-permute-start(bf16[1536,512]{1,0:T(8,128)(2,1)S(1)} %get-tuple-element.83), channel_id=1, source_target_pairs={{96,0},{25,1},{98,2},{27,3},{100,4},{29,5},{102,6},{31,7},{104,8},... | collective-permute-start | bytes 4718600 | tf_op jit(solution)/shard_map/ppermute | solution.py:55
  104.4 17.5 %collective-permute-start.21 = (bf16[528,512]{1,0:T(8,128)(2,1)S(1)}, bf16[528,512]{1,0:T(8,128)(2,1)S(1)}, u32[]{:S(2)}, u32[]{:S(2)}) collective-permute-start(bf16[528,512]{1,0:T(8,128)(2,1)S(1)} %get-tuple-element.76), channel_id=1, source_target_pairs={{24,0},{97,1},{26,2},{99,3},{28,4},{101,5},{30,6},{103,7},{0,8},{1... | collective-permute-start | bytes 1622024 | tf_op jit(solution)/shard_map/ppermute | solution.py:55
  106.8 15.1 %collective-permute-start.20 = (bf16[512,512]{1,0:T(8,128)(2,1)S(1)}, bf16[512,512]{1,0:T(8,128)(2,1)S(1)}, u32[]{:S(2)}, u32[]{:S(2)}) collective-permute-start(bf16[512,512]{1,0:T(8,128)(2,1)S(1)} %get-tuple-element.75), channel_id=1, source_target_pairs={{8,0},{33,1},{10,2},{35,3},{12,4},{37,5},{14,6},{39,7},{16,8},{41,... | collective-permute-start | bytes 1572872 | tf_op jit(solution)/shard_map/ppermute | solution.py:55
  122.9 6.5 %collective-permute-start.24 = (f32[8,512]{1,0:T(8,128)S(1)}, f32[8,512]{1,0:T(8,128)S(1)}, u32[]{:S(2)}, u32[]{:S(2)}) collective-permute-start(f32[8,512]{1,0:T(8,128)S(1)} %get-tuple-element.80), channel_id=1, source_target_pairs={{64,0},{17,1},{66,2},{19,3},{68,4},{21,5},{70,6},{23,7},{72,8},{25... | collective-permute-start | bytes 49160 | tf_op jit(solution)/shard_map/ppermute | solution.py:55
  124.2 5.1 %collective-permute-start.23 = (f32[8,512]{1,0:T(8,128)S(1)}, f32[8,512]{1,0:T(8,128)S(1)}, u32[]{:S(2)}, u32[]{:S(2)}) collective-permute-start(f32[8,512]{1,0:T(8,128)S(1)} %get-tuple-element.80), channel_id=1, source_target_pairs={{96,0},{25,1},{98,2},{27,3},{100,4},{29,5},{102,6},{31,7},{104,8},... | collective-permute-start | bytes 49160 | tf_op jit(solution)/shard_map/ppermute | solution.py:55
  126.8 3.7 %collective-permute-start.22 = (f32[8,512]{1,0:T(8,128)S(1)}, f32[8,512]{1,0:T(8,128)S(1)}, u32[]{:S(2)}, u32[]{:S(2)}) collective-permute-start(f32[8,512]{1,0:T(8,128)S(1)} %get-tuple-element.80), channel_id=1, source_target_pairs={{32,0},{9,1},{34,2},{11,3},{36,4},{13,5},{38,6},{15,7},{40,8},{17,... | collective-permute-start | bytes 49160 | tf_op jit(solution)/shard_map/ppermute | solution.py:55
  130.5 27.6 %collective-permute-start.27 = (bf16[2048,512]{1,0:T(8,128)(2,1)S(1)}, bf16[2048,512]{1,0:T(8,128)(2,1)S(1)}, u32[]{:S(2)}, u32[]{:S(2)}) collective-permute-start(bf16[2048,512]{1,0:T(8,128)(2,1)S(1)} %get-tuple-element.84), channel_id=1, source_target_pairs={{64,0},{17,1},{66,2},{19,3},{68,4},{21,5},{70,6},{23,7},{72,8},{25... | collective-permute-start | bytes 6291464 | tf_op jit(solution)/shard_map/ppermute | solution.py:55
  131.2 31.8 %collective-permute-start.28 = (bf16[512,512]{1,0:T(8,128)(2,1)S(1)}, bf16[512,512]{1,0:T(8,128)(2,1)S(1)}, u32[]{:S(2)}, u32[]{:S(2)}) collective-permute-start(bf16[512,512]{1,0:T(8,128)(2,1)S(1)} %get-tuple-element.88), channel_id=1, source_target_pairs={{32,0},{9,1},{34,2},{11,3},{36,4},{13,5},{38,6},{15,7},{40,8},{17,... | collective-permute-start | bytes 1572872 | tf_op jit(solution)/shard_map/ppermute | solution.py:55
  133.3 30.4 %collective-permute-start.29 = (bf16[512,512]{1,0:T(8,128)(2,1)S(1)}, bf16[512,512]{1,0:T(8,128)(2,1)S(1)}, u32[]{:S(2)}, u32[]{:S(2)}) collective-permute-start(bf16[512,512]{1,0:T(8,128)(2,1)S(1)} %get-tuple-element.89), channel_id=1, source_target_pairs={{96,0},{25,1},{98,2},{27,3},{100,4},{29,5},{102,6},{31,7},{104,8},... | collective-permute-start | bytes 1572872 | tf_op jit(solution)/shard_map/ppermute | solution.py:55
  133.3 1.3 collective-permute-start.30
  134.6 3.7 %collective-permute-start.31 = (f32[8,512]{1,0:T(8,128)S(1)}, f32[8,512]{1,0:T(8,128)S(1)}, u32[]{:S(2)}, u32[]{:S(2)}) collective-permute-start(f32[8,512]{1,0:T(8,128)S(1)} %add.47), channel_id=1, source_target_pairs={{0,2},{2,0},{4,6},{6,4},{1,3},{3,1},{5,7},{7,5},{8,10},{10,8},{12,... | collective-permute-start | bytes 49160 | tf_op jit(solution)/shard_map/ppermute | solution.py:62
  138.3 9.4 %collective-permute-start.32 = (f32[8,512]{1,0:T(8,128)S(1)}, f32[8,512]{1,0:T(8,128)S(1)}, u32[]{:S(2)}, u32[]{:S(2)}) collective-permute-start(f32[8,512]{1,0:T(8,128)S(1)} %add.48), channel_id=1, source_target_pairs={{0,4},{2,6},{4,0},{6,2},{1,5},{3,7},{5,1},{7,3},{8,12},{10,14},{12... | collective-permute-start | bytes 49160 | tf_op jit(solution)/shard_map/ppermute | solution.py:62
where the time goes:
time: 170 us; the launch traced here: 167 us
  waiting for transfers between devices  76.7 us (45%)
  starting transfers between devices  45.9 us (27%)
  Pallas kernels  41.7 us (25%)
  local copies, waits for them, and re-layouts  2.05 us (1%)
    ppermute x27, waiting for transfers between devices, fetch(): return lax.ppermute(value, ALL, pairs(first, second))  68.1 us
    ppermute x27, starting transfers between devices, fetch(): return lax.ppermute(value, ALL, pairs(first, second))  39.4 us
    pallas_call x6, Pallas kernels, run_tiles(): pl.pallas_call(functools.partial(tile_kernel, part, len(tables), earlier...  30.3 us
    ppermute x6, waiting for transfers between devices, sum_over_cols(): part = part + lax.ppermute(part, axis, [(i, i ^ step) for i in range(size)])  8.55 us
    ppermute x6, starting transfers between devices, sum_over_cols(): part = part + lax.ppermute(part, axis, [(i, i ^ step) for i in range(size)])  6.48 us
    pallas_call x1, Pallas kernels, ask(): pl.pallas_call(ask_kernel, out_shape=(jax.ShapeDtypeStruct((64,), i32), j...  3.87 us
    pallas_call x1, Pallas kernels, sort_tiles(): pl.pallas_call(sort_kernel, out_shape=jax.ShapeDtypeStruct((LIST,), i32),...  3.78 us
  transfers between devices with their start and end apart: 33, of which 19 were waited for; matrix products, arithmetic and copies ran while one was open for 0% of the time, Pallas kernels for 20%

commit v1 on v0

--- a/solution.py
+++ b/solution.py
@@ -19,10 +19,10 @@
 UNIT = 1572864
 PATTERNS = 192
 TILES = 240
-PARTS = 3
-GROUP = (4, 4, 2)
+PARTS = 4
+GROUP = (4, 4, 4, 4)
 KEYS = PARTS * BPD
-SLOTS = TILES + sum(BPD * (g - 1) + 2 * g for g in GROUP) // 8 * 8 + 8
+SLOTS = TILES + sum(BPD * (g - 1) + 2 * g for g in GROUP) // 16 * 16 + 16
 STARTS = SLOTS + SLOTS // 2
 LIST = STARTS + 8
 EMPTY = PATTERNS * 64
@@ -66,7 +66,8 @@
 
 OWNERS = (
     ((1, 0), (1, 1), (1, 3), (3, 0), (3, 1), (3, 3), (0, 1), (0, 2), (0, 3)),
-    ((2, 0), (2, 1), (2, 3), (2, 2)),
+    ((2, 0), (2, 1)),
+    ((2, 3), (2, 2)),
     ((1, 2), (3, 2)),
 )
 
@@ -235,7 +236,7 @@
     )(asked, own, far1, far3)
 
 
-def pick_late_kernel(asked, wanted, own, far1, far3, low2, high2, near, out1, out3, out2, line, far2):
+def pick_late_kernel(asked, wanted, own, far1, far3, low2, high2, near, out1, out3, out2a, out2b, line, far2):
     far2[pl.ds(0, HALF_ROWS), :] = low2[...]
     far2[pl.ds(HALF_ROWS, HALF_ROWS + 16), :] = high2[...]
     tables = ((0, own), (1, far1), (3, far3), (2, far2))
@@ -244,7 +245,8 @@
         move(far2, asked[2, 2 * CAP + r], out3, r)
     for i, (k, table) in enumerate(tables):
         for r in range(CAP):
-            move(table, asked[1, k * CAP + r], out2, i * CAP + r)
+            out, at = (out2a, i) if i < 2 else (out2b, i - 2)
+            move(table, asked[1, k * CAP + r], out, at * CAP + r)
             if k > 0:
                 move(table, wanted[k * CAP + r], near, (k - 1) * CAP + r)
     rows = sum(t[pl.ds(OWN_ROWS, 16), :].astype(jnp.float32) for _, t in tables)
@@ -261,11 +263,12 @@
             jax.ShapeDtypeStruct((3 * CAP * BLOCK, C), b16),
             piece,
             piece,
-            jax.ShapeDtypeStruct((PICKED * BLOCK, C), b16),
+            jax.ShapeDtypeStruct((2 * CAP * BLOCK, C), b16),
+            jax.ShapeDtypeStruct((2 * CAP * BLOCK, C), b16),
             jax.ShapeDtypeStruct((8, C), jnp.float32),
         ),
         in_specs=[SMEM] * 2 + [VMEM] * 5,
-        out_specs=(VMEM,) * 5,
+        out_specs=(VMEM,) * 6,
         scratch_shapes=[pltpu.VMEM((SENT_ROWS, C), b16)],
         compiler_params=pltpu.CompilerParams(vmem_limit_bytes=20 << 20),
         name="pick_late",
@@ -439,19 +442,23 @@
         low2, high2 = fetch(pass1, 1, 0), fetch(pass3, 3, 0)
         side1, side3 = fetch(out1, 0, 1), fetch(out3, 0, 3)
         lists, low2, high2 = lax.optimization_barrier((lists, low2, high2))
-        near, out1, out3, out2, line = pick_late(asked, requests[0], own, far1, far3, low2, high2)
+        near, out1, out3, out2a, out2b, line = pick_late(asked, requests[0], own, far1, far3, low2, high2)
         lines = tuple(fetch(line, 0, m) for m in (1, 3, 2))
-        lines, out2, side1, side3 = lax.optimization_barrier((lines, out2, side1, side3))
-        side2 = fetch(out2, 0, 2)
+        lines, out2a, out2b, side1, side3 = lax.optimization_barrier(
+            (lines, out2a, out2b, side1, side3)
+        )
+        side2a, side2b = fetch(out2a, 0, 2), fetch(out2b, 0, 2)
         late1, late3 = fetch(out1, 0, 1), fetch(out3, 0, 3)
         col_sums = sum_over_cols(line + lines[0] + lines[1] + lines[2])
         tables = (side1, side3, near)
         (total,) = run_tiles("sides", 0, lists, words, own, tables)
-        (total,) = run_tiles("across", 1, lists, words, own, (side2,), total)
+        (total,) = run_tiles("across", 1, lists, words, own, (side2a,), total)
+        total, side2b = lax.optimization_barrier((total, side2b))
+        (total,) = run_tiles("across_more", 2, lists, words, own, (side2b,), total)
         total, late1, late3 = lax.optimization_barrier((total, late1, late3))
         finish = "more" if step < STEPS - 1 else "end"
         current, *own_next = run_tiles(
-            "late", 2, lists, words, own, (late1, late3), total, current, col_sums, finish
+            "late", 3, lists, words, own, (late1, late3), total, current, col_sums, finish
         )
         if own_next:
             (own,) = own_next

time: 170 us -> 174 us (1.024); the launches traced: 167 us -> 173 us
  starting transfers between devices: 45.9 us -> 54.2 us
  waiting for transfers between devices: 76.7 us -> 71.6 us
  Pallas kernels: 41.7 us -> 44.3 us
    ppermute x27 -> x29, starting transfers between devices: 39.4 us -> 51 us  [fetch(): return lax.ppermute(value, ALL, pairs(first, second))]
    ppermute x27 -> x29, waiting for transfers between devices: 68.1 us -> 61.9 us  [fetch(): return lax.ppermute(value, ALL, pairs(first, second))]
    ppermute x6, starting transfers between devices: 6.48 us -> 3.18 us  [sum_over_cols(): part = part + lax.ppermute(part, axis, [(i, i ^ step) for i in range(size)])]
    pallas_call x6 -> x8, Pallas kernels: 30.3 us -> 33.4 us  [run_tiles(): pl.pallas_call(functools.partial(tile_kernel, part, len(tables), earlier...]
  transfers between devices with their start and end apart: 33 -> 35, of which waited for: 19 -> 19; matrix products, arithmetic and copies ran while one was open for 0% -> 0% of each run, Pallas kernels for 20% -> 20%
where the time goes in v1:
time: 174 us; the launch traced here: 173 us
  waiting for transfers between devices  71.6 us (41%)
  starting transfers between devices  54.2 us (31%)
  Pallas kernels  44.3 us (25%)
  local copies, waits for them, and re-layouts  2.05 us (1%)
    ppermute x29, waiting for transfers between devices, fetch(): return lax.ppermute(value, ALL, pairs(first, second))  61.9 us
    ppermute x29, starting transfers between devices, fetch(): return lax.ppermute(value, ALL, pairs(first, second))  51 us
    pallas_call x8, Pallas kernels, run_tiles(): pl.pallas_call(functools.partial(tile_kernel, part, len(tables), earlier...  33.4 us
    ppermute x6, waiting for transfers between devices, sum_over_cols(): part = part + lax.ppermute(part, axis, [(i, i ^ step) for i in range(size)])  9.71 us
    pallas_call x1, Pallas kernels, sort_tiles(): pl.pallas_call(sort_kernel, out_shape=jax.ShapeDtypeStruct((LIST,), i32),...  3.63 us
    pallas_call x1, Pallas kernels, ask(): pl.pallas_call(ask_kernel, out_shape=(jax.ShapeDtypeStruct((64,), i32), j...  3.52 us
  transfers between devices with their start and end apart: 35, of which 19 were waited for; matrix products, arithmetic and copies ran while one was open for 0% of the time, Pallas kernels for 20%

profile of v1, /device:TPU:32, one launch (start us, length us, event | category | flops | bytes accessed | tf_op | source)
XLA Modules:
  0.0 173.3 jit_solution(6739653323156153724)
XLA Ops:
  0.0 1.6 copy-done
  1.6 0.1 first.1.own.refs_2_
  1.7 1.6 collective-permute-start.4
  3.3 1.7 %collective-permute-start.3 = (bf16[1040,512]{1,0:T(8,128)(2,1)S(1)}, bf16[1040,512]{1,0:T(8,128)(2,1)S(1)}, u32[]{:S(2)}, u32[]{:S(2)}) collective-permute-start(bf16[1040,512]{1,0:T(8,128)(2,1)S(1)} %first.1.own.refs_2_), channel_id=1, source_target_pairs={{8,0},{33,1},{10,2},{35,3},{12,4},{37,5},{14,6},{39,7},{16,8},{41,... | collective-permute-start | bytes 3194888 | tf_op jit(solution)/shard_map/ppermute | solution.py:55
  5.8 3.5 %ask.1 = (s32[64]{0:T(128)S(1)}, s32[240]{0:T(256)S(1)}) custom-call(s32[3]{0:T(128)S(1)} %pad_add_fusion.1.place, s32[240]{0:T(256)S(1)} %bitcast.9, s32[240]{0:T(256)S(1)} %bitcast.10, s32[1]{0:T(128)S(6)} %copy.9.count, s32[1024]{0:T(1024)S(1)} %copy-done.2), custom_call_target="tpu_custom_call" | custom-call | tf_op jit(solution)/shard_map/ask/pallas_call | solution.py:118
  9.4 2.9 %collective-permute-start.2 = (s32[16]{0:T(128)S(1)}, s32[16]{0:T(128)S(1)}, u32[]{:S(2)}, u32[]{:S(2)}) collective-permute-start(s32[16]{0:T(128)S(1)} %get-tuple-element.114), channel_id=1, source_target_pairs={{32,0},{9,1},{34,2},{11,3},{36,4},{13,5},{38,6},{15,7},{40,8},{17,... | collective-permute-start | bytes 200 | tf_op jit(solution)/shard_map/ppermute | solution.py:55
  12.3 1.1 collective-permute-start.1
  13.3 0.6 collective-permute-start
  13.9 3.4 %collective-permute-done.1 = s32[16]{0:T(128)S(1)} collective-permute-done((s32[16]{0:T(128)S(1)}, s32[16]{0:T(128)S(1)}, u32[]{:S(2)}, u32[]{:S(2)}) %collective-permute-start.1) | collective-permute-done | bytes 96 | tf_op jit(solution)/shard_map/ppermute | solution.py:55
  17.4 0.7 collective-permute-done
  18.1 0.2 collective-permute-done.3.far1
  18.3 0.8 pick_early.2
  19.1 3.1 %collective-permute-start.10 = (bf16[1536,512]{1,0:T(8,128)(2,1)S(1)}, bf16[1536,512]{1,0:T(8,128)(2,1)S(1)}, u32[]{:S(2)}, u32[]{:S(2)}) collective-permute-start(bf16[1536,512]{1,0:T(8,128)(2,1)S(1)} %get-tuple-element.69), channel_id=1, source_target_pairs={{32,0},{9,1},{34,2},{11,3},{36,4},{13,5},{38,6},{15,7},{40,8},{17,... | collective-permute-start | bytes 4718600 | tf_op jit(solution)/shard_map/ppermute | solution.py:55
  22.2 1.5 collective-permute-start.6
  23.7 1.7 %collective-permute-start.5 = (bf16[512,512]{1,0:T(8,128)(2,1)S(1)}, bf16[512,512]{1,0:T(8,128)(2,1)S(1)}, u32[]{:S(2)}, u32[]{:S(2)}) collective-permute-start(bf16[512,512]{1,0:T(8,128)(2,1)S(1)} %get-tuple-element.61), channel_id=1, source_target_pairs={{8,0},{33,1},{10,2},{35,3},{12,4},{37,5},{14,6},{39,7},{16,8},{41,... | collective-permute-start | bytes 1572872 | tf_op jit(solution)/shard_map/ppermute | solution.py:55
  25.4 3.6 %sort_tiles.1.refs_0_ = s32[584]{0:T(1024)S(1)} custom-call(s32[240]{0:T(256)S(1)} %get-tuple-element.59.codes, s32[240]{0:T(256)S(1)} %bitcast.11, s32[1]{0:T(128)S(6)} %copy.9.count), custom_call_target="tpu_custom_call" | custom-call | tf_op jit(solution)/shard_map/sort_tiles/pallas_call | solution.py:166
  29.1 9.5 %collective-permute-done.5.low2 = bf16[512,512]{1,0:T(8,128)(2,1)S(1)} collective-permute-done((bf16[512,512]{1,0:T(8,128)(2,1)S(1)}, bf16[512,512]{1,0:T(8,128)(2,1)S(1)}, u32[]{:S(2)}, u32[]{:S(2)}) %collective-permute-start.5) | collective-permute-done | bytes 524320 | tf_op jit(solution)/shard_map/ppermute | solution.py:55
  38.6 1.0 pick_late.2
  39.6 2.3 %collective-permute-start.9 = (f32[8,512]{1,0:T(8,128)S(1)}, f32[8,512]{1,0:T(8,128)S(1)}, u32[]{:S(2)}, u32[]{:S(2)}) collective-permute-start(f32[8,512]{1,0:T(8,128)S(1)} %get-tuple-element.66), channel_id=1, source_target_pairs={{64,0},{17,1},{66,2},{19,3},{68,4},{21,5},{70,6},{23,7},{72,8},{25... | collective-permute-start | bytes 49160 | tf_op jit(solution)/shard_map/ppermute | solution.py:55
  41.9 1.9 %collective-permute-start.8 = (f32[8,512]{1,0:T(8,128)S(1)}, f32[8,512]{1,0:T(8,128)S(1)}, u32[]{:S(2)}, u32[]{:S(2)}) collective-permute-start(f32[8,512]{1,0:T(8,128)S(1)} %get-tuple-element.66), channel_id=1, source_target_pairs={{96,0},{25,1},{98,2},{27,3},{100,4},{29,5},{102,6},{31,7},{104,8},... | collective-permute-start | bytes 49160 | tf_op jit(solution)/shard_map/ppermute | solution.py:55
  43.8 1.3 collective-permute-start.7
  45.1 3.2 %collective-permute-done.9 = f32[8,512]{1,0:T(8,128)S(1)} collective-permute-done((f32[8,512]{1,0:T(8,128)S(1)}, f32[8,512]{1,0:T(8,128)S(1)}, u32[]{:S(2)}, u32[]{:S(2)}) %collective-permute-start.9) | collective-permute-done | bytes 16416 | tf_op jit(solution)/shard_map/ppermute | solution.py:55
  48.3 0.7 collective-permute-start.12
  49.1 2.9 %collective-permute-start.13 = (bf16[1024,512]{1,0:T(8,128)(2,1)S(1)}, bf16[1024,512]{1,0:T(8,128)(2,1)S(1)}, u32[]{:S(2)}, u32[]{:S(2)}) collective-permute-start(bf16[1024,512]{1,0:T(8,128)(2,1)S(1)} %get-tuple-element.75), channel_id=1, source_target_pairs={{64,0},{17,1},{66,2},{19,3},{68,4},{21,5},{70,6},{23,7},{72,8},{25... | collective-permute-start | bytes 3145736 | tf_op jit(solution)/shard_map/ppermute | solution.py:55
  52.0 1.6 collective-permute-start.14
  53.6 0.4 collective-permute-start.15
  54.0 1.2 collective-permute-done.16
  55.2 0.1 collective-permute-start.17
  55.3 3.6 %collective-permute-done.17 = f32[8,512]{1,0:T(8,128)S(1)} collective-permute-done((f32[8,512]{1,0:T(8,128)S(1)}, f32[8,512]{1,0:T(8,128)S(1)}, u32[]{:S(2)}, u32[]{:S(2)}) %collective-permute-start.17) | collective-permute-done | bytes 16416 | tf_op jit(solution)/shard_map/ppermute | solution.py:62
  58.9 3.0 %collective-permute-start.18 = (f32[8,512]{1,0:T(8,128)S(1)}, f32[8,512]{1,0:T(8,128)S(1)}, u32[]{:S(2)}, u32[]{:S(2)}) collective-permute-start(f32[8,512]{1,0:T(8,128)S(1)} %add.42), channel_id=1, source_target_pairs={{0,4},{2,6},{4,0},{6,2},{1,5},{3,7},{5,1},{7,3},{8,12},{10,14},{12... | collective-permute-start | bytes 49160 | tf_op jit(solution)/shard_map/ppermute | solution.py:62
  61.9 0.3 copy.8
  62.3 7.8 %sides.2.refs_4_ = f32[1024,512]{1,0:T(8,128)S(1)} custom-call(s32[584]{0:T(1024)S(1)} %sort_tiles.1.refs_0_, s32[193,5,128]{2,1,0:T(8,128)S(1)} %concatenate.3.refs_1_, bf16[1040,512]{1,0:T(8,128)(2,1)S(1)} %first.1.own.refs_2_, bf16[1536,512]{1,0:T(8,128)(2,1)S(1)} %collective-permute-done.10.refs_3_, ...), custom_call_target="tpu_custom_call" | custom-call | tf_op jit(solution)/shard_map/sides/pallas_call | solution.py:414
  70.1 2.8 %across.2.refs_4_ = f32[1024,512]{1,0:T(8,128)S(1)} custom-call(s32[584]{0:T(1024)S(1)} %sort_tiles.1.refs_0_, s32[193,5,128]{2,1,0:T(8,128)S(1)} %concatenate.3.refs_1_, bf16[1040,512]{1,0:T(8,128)(2,1)S(1)} %first.1.own.refs_2_, bf16[1024,512]{1,0:T(8,128)(2,1)S(1)} %collective-permute-done.12.refs_3_, f32[1024,512]{1,0:T(8,128)S(1)} %sides.2.refs_4_), custom_call_target="tpu_custom_call" | custom-call | tf_op jit(solution)/shard_map/across/pallas_call | solution.py:414
  72.9 3.1 %collective-permute-done.13.refs_3_ = bf16[1024,512]{1,0:T(8,128)(2,1)S(1)} collective-permute-done((bf16[1024,512]{1,0:T(8,128)(2,1)S(1)}, bf16[1024,512]{1,0:T(8,128)(2,1)S(1)}, u32[]{:S(2)}, u32[]{:S(2)}) %collective-permute-start.13) | collective-permute-done | bytes 1048608 | tf_op jit(solution)/shard_map/ppermute | solution.py:55
  76.1 2.2 %across_more.2.refs_5_ = f32[1024,512]{1,0:T(8,128)S(1)} custom-call(s32[584]{0:T(1024)S(1)} %sort_tiles.1.refs_0_, s32[193,5,128]{2,1,0:T(8,128)S(1)} %concatenate.3.refs_1_, bf16[1040,512]{1,0:T(8,128)(2,1)S(1)} %first.1.own.refs_2_, bf16[1024,512]{1,0:T(8,128)(2,1)S(1)} %collective-permute-done.13.refs_3_, f32[1024,512]{1,0:T(8,128)S(1)} %across.2.refs_4_), custom_call_target="tpu_custom_call" | custom-call | tf_op jit(solution)/shard_map/across_more/pallas_call | solution.py:414
  78.3 2.3 %collective-permute-done.14.refs_3_ = bf16[512,512]{1,0:T(8,128)(2,1)S(1)} collective-permute-done((bf16[512,512]{1,0:T(8,128)(2,1)S(1)}, bf16[512,512]{1,0:T(8,128)(2,1)S(1)}, u32[]{:S(2)}, u32[]{:S(2)}) %collective-permute-start.14) | collective-permute-done | bytes 524320 | tf_op jit(solution)/shard_map/ppermute | solution.py:55
  80.6 1.0 collective-permute-done.15.refs_4_
  81.6 3.5 %late.2 = (f32[1024,512]{1,0:T(8,128)S(1)}, bf16[1040,512]{1,0:T(8,128)(2,1)S(1)}) custom-call(s32[584]{0:T(1024)S(1)} %sort_tiles.1.refs_0_, s32[193,5,128]{2,1,0:T(8,128)S(1)} %concatenate.3.refs_1_, bf16[1040,512]{1,0:T(8,128)(2,1)S(1)} %first.1.own.refs_2_, bf16[512,512]{1,0:T(8,128)(2,1)S(1)} %collective-permute-done.14.refs_3_, ...), custom_call_target="tpu_custom_call" | custom-call | tf_op jit(solution)/shard_map/late/pallas_call | solution.py:414
  85.1 1.0 collective-permute-start.20
  86.1 2.7 %collective-permute-start.19 = (bf16[1040,512]{1,0:T(8,128)(2,1)S(1)}, bf16[1040,512]{1,0:T(8,128)(2,1)S(1)}, u32[]{:S(2)}, u32[]{:S(2)}) collective-permute-start(bf16[1040,512]{1,0:T(8,128)(2,1)S(1)} %get-tuple-element.86.own.refs_2_), channel_id=1, source_target_pairs={{8,0},{33,1},{10,2},{35,3},{12,4},{37,5},{14,6},{39,7},{16,8},{41,... | collective-permute-start | bytes 3194888 | tf_op jit(solution)/shard_map/ppermute | solution.py:55
  88.8 12.9 %collective-permute-done.20.far3 = bf16[1040,512]{1,0:T(8,128)(2,1)S(1)} collective-permute-done((bf16[1040,512]{1,0:T(8,128)(2,1)S(1)}, bf16[1040,512]{1,0:T(8,128)(2,1)S(1)}, u32[]{:S(2)}, u32[]{:S(2)}) %collective-permute-start.20) | collective-permute-done | bytes 1064992 | tf_op jit(solution)/shard_map/ppermute | solution.py:55
  101.7 0.8 pick_early.3
  102.6 1.8 %collective-permute-start.26 = (bf16[1536,512]{1,0:T(8,128)(2,1)S(1)}, bf16[1536,512]{1,0:T(8,128)(2,1)S(1)}, u32[]{:S(2)}, u32[]{:S(2)}) collective-permute-start(bf16[1536,512]{1,0:T(8,128)(2,1)S(1)} %get-tuple-element.95), channel_id=1, source_target_pairs={{32,0},{9,1},{34,2},{11,3},{36,4},{13,5},{38,6},{15,7},{40,8},{17,... | collective-permute-start | bytes 4718600 | tf_op jit(solution)/shard_map/ppermute | solution.py:55
  104.4 0.2 collective-permute-start.27
  104.7 2.1 %collective-permute-start.22 = (bf16[528,512]{1,0:T(8,128)(2,1)S(1)}, bf16[528,512]{1,0:T(8,128)(2,1)S(1)}, u32[]{:S(2)}, u32[]{:S(2)}) collective-permute-start(bf16[528,512]{1,0:T(8,128)(2,1)S(1)} %get-tuple-element.88), channel_id=1, source_target_pairs={{24,0},{97,1},{26,2},{99,3},{28,4},{101,5},{30,6},{103,7},{0,8},{1... | collective-permute-start | bytes 1622024 | tf_op jit(solution)/shard_map/ppermute | solution.py:55
  106.7 1.6 collective-permute-start.21
  108.4 14.6 %collective-permute-done.21.low2 = bf16[512,512]{1,0:T(8,128)(2,1)S(1)} collective-permute-done((bf16[512,512]{1,0:T(8,128)(2,1)S(1)}, bf16[512,512]{1,0:T(8,128)(2,1)S(1)}, u32[]{:S(2)}, u32[]{:S(2)}) %collective-permute-start.21) | collective-permute-done | bytes 524320 | tf_op jit(solution)/shard_map/ppermute | solution.py:55
  123.0 1.0 pick_late.3
  124.0 6.2 %collective-permute-start.25 = (f32[8,512]{1,0:T(8,128)S(1)}, f32[8,512]{1,0:T(8,128)S(1)}, u32[]{:S(2)}, u32[]{:S(2)}) collective-permute-start(f32[8,512]{1,0:T(8,128)S(1)} %get-tuple-element.92), channel_id=1, source_target_pairs={{64,0},{17,1},{66,2},{19,3},{68,4},{21,5},{70,6},{23,7},{72,8},{25... | collective-permute-start | bytes 49160 | tf_op jit(solution)/shard_map/ppermute | solution.py:55
  130.2 0.2 collective-permute-start.24
  130.4 3.0 %collective-permute-start.23 = (f32[8,512]{1,0:T(8,128)S(1)}, f32[8,512]{1,0:T(8,128)S(1)}, u32[]{:S(2)}, u32[]{:S(2)}) collective-permute-start(f32[8,512]{1,0:T(8,128)S(1)} %get-tuple-element.92), channel_id=1, source_target_pairs={{32,0},{9,1},{34,2},{11,3},{36,4},{13,5},{38,6},{15,7},{40,8},{17,... | collective-permute-start | bytes 49160 | tf_op jit(solution)/shard_map/ppermute | solution.py:55
  133.4 1.7 collective-permute-done.24
  135.1 1.5 collective-permute-start.28
  136.6 2.1 %collective-permute-start.29 = (bf16[1024,512]{1,0:T(8,128)(2,1)S(1)}, bf16[1024,512]{1,0:T(8,128)(2,1)S(1)}, u32[]{:S(2)}, u32[]{:S(2)}) collective-permute-start(bf16[1024,512]{1,0:T(8,128)(2,1)S(1)} %get-tuple-element.101), channel_id=1, source_target_pairs={{64,0},{17,1},{66,2},{19,3},{68,4},{21,5},{70,6},{23,7},{72,8},{25... | collective-permute-start | bytes 3145736 | tf_op jit(solution)/shard_map/ppermute | solution.py:55
  138.7 3.2 %collective-permute-start.30 = (bf16[512,512]{1,0:T(8,128)(2,1)S(1)}, bf16[512,512]{1,0:T(8,128)(2,1)S(1)}, u32[]{:S(2)}, u32[]{:S(2)}) collective-permute-start(bf16[512,512]{1,0:T(8,128)(2,1)S(1)} %get-tuple-element.104), channel_id=1, source_target_pairs={{32,0},{9,1},{34,2},{11,3},{36,4},{13,5},{38,6},{15,7},{40,8},{17,... | collective-permute-start | bytes 1572872 | tf_op jit(solution)/shard_map/ppermute | solution.py:55
  141.9 0.1 collective-permute-start.32
  142.0 1.2 collective-permute-done.32
  143.2 3.7 %collective-permute-done.33 = f32[8,512]{1,0:T(8,128)S(1)} collective-permute-done((f32[8,512]{1,0:T(8,128)S(1)}, f32[8,512]{1,0:T(8,128)S(1)}, u32[]{:S(2)}, u32[]{:S(2)}) %collective-permute-start.33) | collective-permute-done | bytes 16416 | tf_op jit(solution)/shard_map/ppermute | solution.py:62
  146.9 7.8 %sides.3.refs_4_ = f32[1024,512]{1,0:T(8,128)S(1)} custom-call(s32[584]{0:T(1024)S(1)} %sort_tiles.1.refs_0_, s32[193,5,128]{2,1,0:T(8,128)S(1)} %concatenate.3.refs_1_, bf16[1040,512]{1,0:T(8,128)(2,1)S(1)} %get-tuple-element.86.own.refs_2_, bf16[1536,512]{1,0:T(8,128)(2,1)S(1)} %collective-permute-done.26.refs_3_, ...), custom_call_target="tpu_custom_call" | custom-call | tf_op jit(solution)/shard_map/sides/pallas_call | solution.py:414
  154.8 2.8 %across.3.refs_4_ = f32[1024,512]{1,0:T(8,128)S(1)} custom-call(s32[584]{0:T(1024)S(1)} %sort_tiles.1.refs_0_, s32[193,5,128]{2,1,0:T(8,128)S(1)} %concatenate.3.refs_1_, bf16[1040,512]{1,0:T(8,128)(2,1)S(1)} %get-tuple-element.86.own.refs_2_, bf16[1024,512]{1,0:T(8,128)(2,1)S(1)} %collective-permute-done.28.refs_3_, f32[1024,512]{1,0:T(8,128)S(1)} %sides.3.refs_4_), custom_call_target="tpu_custom_call" | custom-call | tf_op jit(solution)/shard_map/across/pallas_call | solution.py:414
  157.6 5.3 %collective-permute-done.29.refs_3_ = bf16[1024,512]{1,0:T(8,128)(2,1)S(1)} collective-permute-done((bf16[1024,512]{1,0:T(8,128)(2,1)S(1)}, bf16[1024,512]{1,0:T(8,128)(2,1)S(1)}, u32[]{:S(2)}, u32[]{:S(2)}) %collective-permute-start.29) | collective-permute-done | bytes 1048608 | tf_op jit(solution)/shard_map/ppermute | solution.py:55
  162.8 2.3 %across_more.3.refs_5_ = f32[1024,512]{1,0:T(8,128)S(1)} custom-call(s32[584]{0:T(1024)S(1)} %sort_tiles.1.refs_0_, s32[193,5,128]{2,1,0:T(8,128)S(1)} %concatenate.3.refs_1_, bf16[1040,512]{1,0:T(8,128)(2,1)S(1)} %get-tuple-element.86.own.refs_2_, bf16[1024,512]{1,0:T(8,128)(2,1)S(1)} %collective-permute-done.29.refs_3_, f32[1024,512]{1,0:T(8,128)S(1)} %across.3.refs_4_), custom_call_target="tpu_custom_call" | custom-call | tf_op jit(solution)/shard_map/across_more/pallas_call | solution.py:414
  165.1 3.8 %collective-permute-done.30.refs_3_ = bf16[512,512]{1,0:T(8,128)(2,1)S(1)} collective-permute-done((bf16[512,512]{1,0:T(8,128)(2,1)S(1)}, bf16[512,512]{1,0:T(8,128)(2,1)S(1)}, u32[]{:S(2)}, u32[]{:S(2)}) %collective-permute-start.30) | collective-permute-done | bytes 524320 | tf_op jit(solution)/shard_map/ppermute | solution.py:55
  168.9 4.3 %late.3 = f32[1024,512]{1,0:T(8,128)} custom-call(s32[584]{0:T(1024)S(1)} %sort_tiles.1.refs_0_, s32[193,5,128]{2,1,0:T(8,128)S(1)} %concatenate.3.refs_1_, bf16[1040,512]{1,0:T(8,128)(2,1)S(1)} %get-tuple-element.86.own.refs_2_, bf16[512,512]{1,0:T(8,128)(2,1)S(1)} %collective-permute-done.30.refs_3_, bf16[512,512]{1,0:T(8,128)(2,1)S(1)} %collective-permute-done.31.refs_4_, ...), custom_call_target="tpu_custom_call" | custom-call | tf_op jit(solution)/shard_map/late/pallas_call | solution.py:414
  (48 shorter events, 0.5 us)
Async XLA Ops:
  0.0 1.6 copy-start
  1.6 4.2 %copy-start.2 = (s32[1024]{0:T(1024)S(1)}, s32[1024]{0:T(1024)}, u32[]{:S(2)}) copy-start(s32[1024]{0:T(1024)} %home.1) | copy-start | bytes 12292
  1.6 4.2 %copy-start.3 = (s32[1,240]{1,0:T(1,128)S(1)}, s32[1,240]{1,0:T(1,128)}, u32[]{:S(2)}) copy-start(s32[1,240]{1,0:T(1,128)} %param.8) | copy-start | bytes 2884
  1.6 4.2 %copy-start.4 = (s32[1,240]{1,0:T(1,128)S(1)}, s32[1,240]{1,0:T(1,128)}, u32[]{:S(2)}) copy-start(s32[1,240]{1,0:T(1,128)} %param.9) | copy-start | bytes 2884
  1.7 16.4 %collective-permute-start.4 = (bf16[1040,512]{1,0:T(8,128)(2,1)S(1)}, bf16[1040,512]{1,0:T(8,128)(2,1)S(1)}, u32[]{:S(2)}, u32[]{:S(2)}) collective-permute-start(bf16[1040,512]{1,0:T(8,128)(2,1)S(1)} %first.1.own.refs_2_), channel_id=1, source_target_pairs={{24,0},{97,1},{26,2},{99,3},{28,4},{101,5},{30,6},{103,7},{0,8},{1... | collective-permute-start | bytes 3194888 | tf_op jit(solution)/shard_map/ppermute | solution.py:55
  3.3 15.0 %collective-permute-start.3 = (bf16[1040,512]{1,0:T(8,128)(2,1)S(1)}, bf16[1040,512]{1,0:T(8,128)(2,1)S(1)}, u32[]{:S(2)}, u32[]{:S(2)}) collective-permute-start(bf16[1040,512]{1,0:T(8,128)(2,1)S(1)} %first.1.own.refs_2_), channel_id=1, source_target_pairs={{8,0},{33,1},{10,2},{35,3},{12,4},{37,5},{14,6},{39,7},{16,8},{41,... | collective-permute-start | bytes 3194888 | tf_op jit(solution)/shard_map/ppermute | solution.py:55
  9.4 4.6 %collective-permute-start.2 = (s32[16]{0:T(128)S(1)}, s32[16]{0:T(128)S(1)}, u32[]{:S(2)}, u32[]{:S(2)}) collective-permute-start(s32[16]{0:T(128)S(1)} %get-tuple-element.114), channel_id=1, source_target_pairs={{32,0},{9,1},{34,2},{11,3},{36,4},{13,5},{38,6},{15,7},{40,8},{17,... | collective-permute-start | bytes 200 | tf_op jit(solution)/shard_map/ppermute | solution.py:55
  12.3 5.1 %collective-permute-start.1 = (s32[16]{0:T(128)S(1)}, s32[16]{0:T(128)S(1)}, u32[]{:S(2)}, u32[]{:S(2)}) collective-permute-start(s32[16]{0:T(128)S(1)} %get-tuple-element.115), channel_id=1, source_target_pairs={{64,0},{17,1},{66,2},{19,3},{68,4},{21,5},{70,6},{23,7},{72,8},{25... | collective-permute-start | bytes 200 | tf_op jit(solution)/shard_map/ppermute | solution.py:55
  13.3 4.8 %collective-permute-start = (s32[16]{0:T(128)S(1)}, s32[16]{0:T(128)S(1)}, u32[]{:S(2)}, u32[]{:S(2)}) collective-permute-start(s32[16]{0:T(128)S(1)} %get-tuple-element.116), channel_id=1, source_target_pairs={{96,0},{25,1},{98,2},{27,3},{100,4},{29,5},{102,6},{31,7},{104,8},... | collective-permute-start | bytes 200 | tf_op jit(solution)/shard_map/ppermute | solution.py:55
  18.1 7.4 %copy-start.5 = (s32[1,240]{1,0:T(1,128)S(1)}, s32[1,240]{1,0:T(1,128)}, u32[]{:S(2)}) copy-start(s32[1,240]{1,0:T(1,128)} %param.10) | copy-start | bytes 2884
  19.1 29.2 %collective-permute-start.10 = (bf16[1536,512]{1,0:T(8,128)(2,1)S(1)}, bf16[1536,512]{1,0:T(8,128)(2,1)S(1)}, u32[]{:S(2)}, u32[]{:S(2)}) collective-permute-start(bf16[1536,512]{1,0:T(8,128)(2,1)S(1)} %get-tuple-element.69), channel_id=1, source_target_pairs={{32,0},{9,1},{34,2},{11,3},{36,4},{13,5},{38,6},{15,7},{40,8},{17,... | collective-permute-start | bytes 4718600 | tf_op jit(solution)/shard_map/ppermute | solution.py:55
  22.2 26.1 %collective-permute-start.11 = (bf16[1536,512]{1,0:T(8,128)(2,1)S(1)}, bf16[1536,512]{1,0:T(8,128)(2,1)S(1)}, u32[]{:S(2)}, u32[]{:S(2)}) collective-permute-start(bf16[1536,512]{1,0:T(8,128)(2,1)S(1)} %get-tuple-element.70), channel_id=1, source_target_pairs={{96,0},{25,1},{98,2},{27,3},{100,4},{29,5},{102,6},{31,7},{104,8},... | collective-permute-start | bytes 4718600 | tf_op jit(solution)/shard_map/ppermute | solution.py:55
  22.2 16.4 %collective-permute-start.6 = (bf16[528,512]{1,0:T(8,128)(2,1)S(1)}, bf16[528,512]{1,0:T(8,128)(2,1)S(1)}, u32[]{:S(2)}, u32[]{:S(2)}) collective-permute-start(bf16[528,512]{1,0:T(8,128)(2,1)S(1)} %get-tuple-element.62), channel_id=1, source_target_pairs={{24,0},{97,1},{26,2},{99,3},{28,4},{101,5},{30,6},{103,7},{0,8},{1... | collective-permute-start | bytes 1622024 | tf_op jit(solution)/shard_map/ppermute | solution.py:55
  23.7 14.9 %collective-permute-start.5 = (bf16[512,512]{1,0:T(8,128)(2,1)S(1)}, bf16[512,512]{1,0:T(8,128)(2,1)S(1)}, u32[]{:S(2)}, u32[]{:S(2)}) collective-permute-start(bf16[512,512]{1,0:T(8,128)(2,1)S(1)} %get-tuple-element.61), channel_id=1, source_target_pairs={{8,0},{33,1},{10,2},{35,3},{12,4},{37,5},{14,6},{39,7},{16,8},{41,... | collective-permute-start | bytes 1572872 | tf_op jit(solution)/shard_map/ppermute | solution.py:55
  38.6 23.3 %copy-start.6 = (s32[192,5,128]{2,0,1:T(8,128)S(1)}, s32[192,5,128]{2,0,1:T(8,128)}, u32[]{:S(2)}) copy-start(s32[192,5,128]{2,0,1:T(8,128)} %param.13) | copy-start | bytes 1474564
  39.6 8.7 %collective-permute-start.9 = (f32[8,512]{1,0:T(8,128)S(1)}, f32[8,512]{1,0:T(8,128)S(1)}, u32[]{:S(2)}, u32[]{:S(2)}) collective-permute-start(f32[8,512]{1,0:T(8,128)S(1)} %get-tuple-element.66), channel_id=1, source_target_pairs={{64,0},{17,1},{66,2},{19,3},{68,4},{21,5},{70,6},{23,7},{72,8},{25... | collective-permute-start | bytes 49160 | tf_op jit(solution)/shard_map/ppermute | solution.py:55
  41.9 6.4 %collective-permute-start.8 = (f32[8,512]{1,0:T(8,128)S(1)}, f32[8,512]{1,0:T(8,128)S(1)}, u32[]{:S(2)}, u32[]{:S(2)}) collective-permute-start(f32[8,512]{1,0:T(8,128)S(1)} %get-tuple-element.66), channel_id=1, source_target_pairs={{96,0},{25,1},{98,2},{27,3},{100,4},{29,5},{102,6},{31,7},{104,8},... | collective-permute-start | bytes 49160 | tf_op jit(solution)/shard_map/ppermute | solution.py:55
  43.8 4.6 %collective-permute-start.7 = (f32[8,512]{1,0:T(8,128)S(1)}, f32[8,512]{1,0:T(8,128)S(1)}, u32[]{:S(2)}, u32[]{:S(2)}) collective-permute-start(f32[8,512]{1,0:T(8,128)S(1)} %get-tuple-element.66), channel_id=1, source_target_pairs={{32,0},{9,1},{34,2},{11,3},{36,4},{13,5},{38,6},{15,7},{40,8},{17,... | collective-permute-start | bytes 49160 | tf_op jit(solution)/shard_map/ppermute | solution.py:55
  48.3 21.8 %collective-permute-start.12 = (bf16[1024,512]{1,0:T(8,128)(2,1)S(1)}, bf16[1024,512]{1,0:T(8,128)(2,1)S(1)}, u32[]{:S(2)}, u32[]{:S(2)}) collective-permute-start(bf16[1024,512]{1,0:T(8,128)(2,1)S(1)} %get-tuple-element.71), channel_id=1, source_target_pairs={{64,0},{17,1},{66,2},{19,3},{68,4},{21,5},{70,6},{23,7},{72,8},{25... | collective-permute-start | bytes 3145736 | tf_op jit(solution)/shard_map/ppermute | solution.py:55
  49.1 27.0 %collective-permute-start.13 = (bf16[1024,512]{1,0:T(8,128)(2,1)S(1)}, bf16[1024,512]{1,0:T(8,128)(2,1)S(1)}, u32[]{:S(2)}, u32[]{:S(2)}) collective-permute-start(bf16[1024,512]{1,0:T(8,128)(2,1)S(1)} %get-tuple-element.75), channel_id=1, source_target_pairs={{64,0},{17,1},{66,2},{19,3},{68,4},{21,5},{70,6},{23,7},{72,8},{25... | collective-permute-start | bytes 3145736 | tf_op jit(solution)/shard_map/ppermute | solution.py:55
  52.0 28.6 %collective-permute-start.14 = (bf16[512,512]{1,0:T(8,128)(2,1)S(1)}, bf16[512,512]{1,0:T(8,128)(2,1)S(1)}, u32[]{:S(2)}, u32[]{:S(2)}) collective-permute-start(bf16[512,512]{1,0:T(8,128)(2,1)S(1)} %get-tuple-element.78), channel_id=1, source_target_pairs={{32,0},{9,1},{34,2},{11,3},{36,4},{13,5},{38,6},{15,7},{40,8},{17,... | collective-permute-start | bytes 1572872 | tf_op jit(solution)/shard_map/ppermute | solution.py:55
  53.6 28.0 %collective-permute-start.15 = (bf16[512,512]{1,0:T(8,128)(2,1)S(1)}, bf16[512,512]{1,0:T(8,128)(2,1)S(1)}, u32[]{:S(2)}, u32[]{:S(2)}) collective-permute-start(bf16[512,512]{1,0:T(8,128)(2,1)S(1)} %get-tuple-element.79), channel_id=1, source_target_pairs={{96,0},{25,1},{98,2},{27,3},{100,4},{29,5},{102,6},{31,7},{104,8},... | collective-permute-start | bytes 1572872 | tf_op jit(solution)/shard_map/ppermute | solution.py:55
  54.0 1.2 collective-permute-start.16
  55.2 3.7 %collective-permute-start.17 = (f32[8,512]{1,0:T(8,128)S(1)}, f32[8,512]{1,0:T(8,128)S(1)}, u32[]{:S(2)}, u32[]{:S(2)}) collective-permute-start(f32[8,512]{1,0:T(8,128)S(1)} %add.41), channel_id=1, source_target_pairs={{0,2},{2,0},{4,6},{6,4},{1,3},{3,1},{5,7},{7,5},{8,10},{10,8},{12,... | collective-permute-start | bytes 49160 | tf_op jit(solution)/shard_map/ppermute | solution.py:62
  58.9 11.2 %collective-permute-start.18 = (f32[8,512]{1,0:T(8,128)S(1)}, f32[8,512]{1,0:T(8,128)S(1)}, u32[]{:S(2)}, u32[]{:S(2)}) collective-permute-start(f32[8,512]{1,0:T(8,128)S(1)} %add.42), channel_id=1, source_target_pairs={{0,4},{2,6},{4,0},{6,2},{1,5},{3,7},{5,1},{7,3},{8,12},{10,14},{12... | collective-permute-start | bytes 49160 | tf_op jit(solution)/shard_map/ppermute | solution.py:62
  72.9 8.7 %copy-start.1 = (f32[1024,512]{1,0:T(8,128)S(1)}, f32[1024,512]{1,0:T(8,128)}, u32[]{:S(2)}) copy-start(f32[1024,512]{1,0:T(8,128)} %refs_6_.1) | copy-start | bytes 6291460
  85.1 16.6 %collective-permute-start.20 = (bf16[1040,512]{1,0:T(8,128)(2,1)S(1)}, bf16[1040,512]{1,0:T(8,128)(2,1)S(1)}, u32[]{:S(2)}, u32[]{:S(2)}) collective-permute-start(bf16[1040,512]{1,0:T(8,128)(2,1)S(1)} %get-tuple-element.86.own.refs_2_), channel_id=1, source_target_pairs={{24,0},{97,1},{26,2},{99,3},{28,4},{101,5},{30,6},{103,7},{0,8},{1... | collective-permute-start | bytes 3194888 | tf_op jit(solution)/shard_map/ppermute | solution.py:55
  86.1 15.7 %collective-permute-start.19 = (bf16[1040,512]{1,0:T(8,128)(2,1)S(1)}, bf16[1040,512]{1,0:T(8,128)(2,1)S(1)}, u32[]{:S(2)}, u32[]{:S(2)}) collective-permute-start(bf16[1040,512]{1,0:T(8,128)(2,1)S(1)} %get-tuple-element.86.own.refs_2_), channel_id=1, source_target_pairs={{8,0},{33,1},{10,2},{35,3},{12,4},{37,5},{14,6},{39,7},{16,8},{41,... | collective-permute-start | bytes 3194888 | tf_op jit(solution)/shard_map/ppermute | solution.py:55
  102.6 32.5 %collective-permute-start.26 = (bf16[1536,512]{1,0:T(8,128)(2,1)S(1)}, bf16[1536,512]{1,0:T(8,128)(2,1)S(1)}, u32[]{:S(2)}, u32[]{:S(2)}) collective-permute-start(bf16[1536,512]{1,0:T(8,128)(2,1)S(1)} %get-tuple-element.95), channel_id=1, source_target_pairs={{32,0},{9,1},{34,2},{11,3},{36,4},{13,5},{38,6},{15,7},{40,8},{17,... | collective-permute-start | bytes 4718600 | tf_op jit(solution)/shard_map/ppermute | solution.py:55
  104.4 30.7 %collective-permute-start.27 = (bf16[1536,512]{1,0:T(8,128)(2,1)S(1)}, bf16[1536,512]{1,0:T(8,128)(2,1)S(1)}, u32[]{:S(2)}, u32[]{:S(2)}) collective-permute-start(bf16[1536,512]{1,0:T(8,128)(2,1)S(1)} %get-tuple-element.96), channel_id=1, source_target_pairs={{96,0},{25,1},{98,2},{27,3},{100,4},{29,5},{102,6},{31,7},{104,8},... | collective-permute-start | bytes 4718600 | tf_op jit(solution)/shard_map/ppermute | solution.py:55
  104.7 18.3 %collective-permute-start.22 = (bf16[528,512]{1,0:T(8,128)(2,1)S(1)}, bf16[528,512]{1,0:T(8,128)(2,1)S(1)}, u32[]{:S(2)}, u32[]{:S(2)}) collective-permute-start(bf16[528,512]{1,0:T(8,128)(2,1)S(1)} %get-tuple-element.88), channel_id=1, source_target_pairs={{24,0},{97,1},{26,2},{99,3},{28,4},{101,5},{30,6},{103,7},{0,8},{1... | collective-permute-start | bytes 1622024 | tf_op jit(solution)/shard_map/ppermute | solution.py:55
  106.7 16.3 %collective-permute-start.21 = (bf16[512,512]{1,0:T(8,128)(2,1)S(1)}, bf16[512,512]{1,0:T(8,128)(2,1)S(1)}, u32[]{:S(2)}, u32[]{:S(2)}) collective-permute-start(bf16[512,512]{1,0:T(8,128)(2,1)S(1)} %get-tuple-element.87), channel_id=1, source_target_pairs={{8,0},{33,1},{10,2},{35,3},{12,4},{37,5},{14,6},{39,7},{16,8},{41,... | collective-permute-start | bytes 1572872 | tf_op jit(solution)/shard_map/ppermute | solution.py:55
  124.0 9.4 %collective-permute-start.25 = (f32[8,512]{1,0:T(8,128)S(1)}, f32[8,512]{1,0:T(8,128)S(1)}, u32[]{:S(2)}, u32[]{:S(2)}) collective-permute-start(f32[8,512]{1,0:T(8,128)S(1)} %get-tuple-element.92), channel_id=1, source_target_pairs={{64,0},{17,1},{66,2},{19,3},{68,4},{21,5},{70,6},{23,7},{72,8},{25... | collective-permute-start | bytes 49160 | tf_op jit(solution)/shard_map/ppermute | solution.py:55
  130.2 4.9 %collective-permute-start.24 = (f32[8,512]{1,0:T(8,128)S(1)}, f32[8,512]{1,0:T(8,128)S(1)}, u32[]{:S(2)}, u32[]{:S(2)}) collective-permute-start(f32[8,512]{1,0:T(8,128)S(1)} %get-tuple-element.92), channel_id=1, source_target_pairs={{96,0},{25,1},{98,2},{27,3},{100,4},{29,5},{102,6},{31,7},{104,8},... | collective-permute-start | bytes 49160 | tf_op jit(solution)/shard_map/ppermute | solution.py:55
  130.4 4.8 %collective-permute-start.23 = (f32[8,512]{1,0:T(8,128)S(1)}, f32[8,512]{1,0:T(8,128)S(1)}, u32[]{:S(2)}, u32[]{:S(2)}) collective-permute-start(f32[8,512]{1,0:T(8,128)S(1)} %get-tuple-element.92), channel_id=1, source_target_pairs={{32,0},{9,1},{34,2},{11,3},{36,4},{13,5},{38,6},{15,7},{40,8},{17,... | collective-permute-start | bytes 49160 | tf_op jit(solution)/shard_map/ppermute | solution.py:55
  135.1 19.6 %collective-permute-start.28 = (bf16[1024,512]{1,0:T(8,128)(2,1)S(1)}, bf16[1024,512]{1,0:T(8,128)(2,1)S(1)}, u32[]{:S(2)}, u32[]{:S(2)}) collective-permute-start(bf16[1024,512]{1,0:T(8,128)(2,1)S(1)} %get-tuple-element.97), channel_id=1, source_target_pairs={{64,0},{17,1},{66,2},{19,3},{68,4},{21,5},{70,6},{23,7},{72,8},{25... | collective-permute-start | bytes 3145736 | tf_op jit(solution)/shard_map/ppermute | solution.py:55
  136.6 26.3 %collective-permute-start.29 = (bf16[1024,512]{1,0:T(8,128)(2,1)S(1)}, bf16[1024,512]{1,0:T(8,128)(2,1)S(1)}, u32[]{:S(2)}, u32[]{:S(2)}) collective-permute-start(bf16[1024,512]{1,0:T(8,128)(2,1)S(1)} %get-tuple-element.101), channel_id=1, source_target_pairs={{64,0},{17,1},{66,2},{19,3},{68,4},{21,5},{70,6},{23,7},{72,8},{25... | collective-permute-start | bytes 3145736 | tf_op jit(solution)/shard_map/ppermute | solution.py:55
  138.7 30.1 %collective-permute-start.30 = (bf16[512,512]{1,0:T(8,128)(2,1)S(1)}, bf16[512,512]{1,0:T(8,128)(2,1)S(1)}, u32[]{:S(2)}, u32[]{:S(2)}) collective-permute-start(bf16[512,512]{1,0:T(8,128)(2,1)S(1)} %get-tuple-element.104), channel_id=1, source_target_pairs={{32,0},{9,1},{34,2},{11,3},{36,4},{13,5},{38,6},{15,7},{40,8},{17,... | collective-permute-start | bytes 1572872 | tf_op jit(solution)/shard_map/ppermute | solution.py:55
  141.9 27.0 %collective-permute-start.31 = (bf16[512,512]{1,0:T(8,128)(2,1)S(1)}, bf16[512,512]{1,0:T(8,128)(2,1)S(1)}, u32[]{:S(2)}, u32[]{:S(2)}) collective-permute-start(bf16[512,512]{1,0:T(8,128)(2,1)S(1)} %get-tuple-element.105), channel_id=1, source_target_pairs={{96,0},{25,1},{98,2},{27,3},{100,4},{29,5},{102,6},{31,7},{104,8},... | collective-permute-start | bytes 1572872 | tf_op jit(solution)/shard_map/ppermute | solution.py:55
  141.9 1.3 collective-permute-start.32
  143.2 3.7 %collective-permute-start.33 = (f32[8,512]{1,0:T(8,128)S(1)}, f32[8,512]{1,0:T(8,128)S(1)}, u32[]{:S(2)}, u32[]{:S(2)}) collective-permute-start(f32[8,512]{1,0:T(8,128)S(1)} %add.47), channel_id=1, source_target_pairs={{0,2},{2,0},{4,6},{6,4},{1,3},{3,1},{5,7},{7,5},{8,10},{10,8},{12,... | collective-permute-start | bytes 49160 | tf_op jit(solution)/shard_map/ppermute | solution.py:62
  146.9 7.8 %collective-permute-start.34 = (f32[8,512]{1,0:T(8,128)S(1)}, f32[8,512]{1,0:T(8,128)S(1)}, u32[]{:S(2)}, u32[]{:S(2)}) collective-permute-start(f32[8,512]{1,0:T(8,128)S(1)} %add.48), channel_id=1, source_target_pairs={{0,4},{2,6},{4,0},{6,2},{1,5},{3,7},{5,1},{7,3},{8,12},{10,14},{12... | collective-permute-start | bytes 49160 | tf_op jit(solution)/shard_map/ppermute | solution.py:62

commit v2 on v1

--- a/solution.py
+++ b/solution.py
@@ -19,8 +19,8 @@
 UNIT = 1572864
 PATTERNS = 192
 TILES = 240
-PARTS = 4
-GROUP = (4, 4, 4, 4)
+PARTS = 6
+GROUP = (4, 4, 4, 4, 4, 4)
 KEYS = PARTS * BPD
 SLOTS = TILES + sum(BPD * (g - 1) + 2 * g for g in GROUP) // 16 * 16 + 16
 STARTS = SLOTS + SLOTS // 2
@@ -55,17 +55,14 @@
     return lax.ppermute(value, ALL, pairs(first, second))
 
 
-def sum_over_cols(part):
-    for axis, size in (("cols_1", 2), ("cols_0", 4)):
-        step = 1
-        while step < size:
-            part = part + lax.ppermute(part, axis, [(i, i ^ step) for i in range(size)])
-            step *= 2
-    return part
+def swap(value, axis, step):
+    return lax.ppermute(value, axis, [(i, i ^ step) for i in range(lax.axis_size(axis))])
 
 
 OWNERS = (
-    ((1, 0), (1, 1), (1, 3), (3, 0), (3, 1), (3, 3), (0, 1), (0, 2), (0, 3)),
+    ((0, 1), (0, 3)),
+    ((1, 0), (1, 1), (1, 3), (0, 2)),
+    ((3, 0), (3, 1), (3, 3)),
     ((2, 0), (2, 1)),
     ((2, 3), (2, 2)),
     ((1, 2), (3, 2)),
@@ -209,31 +206,35 @@
     out[pl.ds(at * BLOCK, BLOCK), :] = table[rows, :]
 
 
-def pick_early_kernel(asked, own, far1, far3, pass1, pass3, out1, out3):
+def pick_early_kernel(asked, wanted, own, far1, far3, near, pass1, pass3, out1, out3):
     pass1[...] = far1[pl.ds(0, HALF_ROWS), :]
     pass3[...] = far3[pl.ds(HALF_ROWS, HALF_ROWS + 16), :]
     for m, out in ((1, out1), (3, out3)):
         for i, (k, table) in enumerate(((0, own), (1, far1), (3, far3))):
             for r in range(CAP):
                 move(table, asked[m - 1, k * CAP + r], out, i * CAP + r)
-
-
-def pick_early(asked, own, far1, far3):
+    for r in range(CAP):
+        move(far1, wanted[CAP + r], near, r)
+        move(far3, wanted[3 * CAP + r], near, CAP + r)
+
+
+def pick_early(asked, wanted, own, far1, far3):
     b16 = jnp.bfloat16
     out = jax.ShapeDtypeStruct((3 * CAP * BLOCK, C), b16)
     return pl.pallas_call(
         pick_early_kernel,
         out_shape=(
+            jax.ShapeDtypeStruct((2 * CAP * BLOCK, C), b16),
             jax.ShapeDtypeStruct((HALF_ROWS, C), b16),
             jax.ShapeDtypeStruct((HALF_ROWS + 16, C), b16),
             out,
             out,
         ),
-        in_specs=[SMEM] + [VMEM] * 3,
-        out_specs=(VMEM,) * 4,
+        in_specs=[SMEM] * 2 + [VMEM] * 3,
+        out_specs=(VMEM,) * 5,
         compiler_params=pltpu.CompilerParams(vmem_limit_bytes=20 << 20),
         name="pick_early",
-    )(asked, own, far1, far3)
+    )(asked, wanted, own, far1, far3)
 
 
 def pick_late_kernel(asked, wanted, own, far1, far3, low2, high2, near, out1, out3, out2a, out2b, line, far2):
@@ -243,12 +244,11 @@
     for r in range(CAP):
         move(far2, asked[0, 2 * CAP + r], out1, r)
         move(far2, asked[2, 2 * CAP + r], out3, r)
+        move(far2, wanted[2 * CAP + r], near, r)
     for i, (k, table) in enumerate(tables):
         for r in range(CAP):
             out, at = (out2a, i) if i < 2 else (out2b, i - 2)
             move(table, asked[1, k * CAP + r], out, at * CAP + r)
-            if k > 0:
-                move(table, wanted[k * CAP + r], near, (k - 1) * CAP + r)
     rows = sum(t[pl.ds(OWN_ROWS, 16), :].astype(jnp.float32) for _, t in tables)
     sums = jnp.sum(rows, axis=0, keepdims=True)
     line[...] = jnp.broadcast_to(sums, (8, C))
@@ -260,7 +260,7 @@
     return pl.pallas_call(
         pick_late_kernel,
         out_shape=(
-            jax.ShapeDtypeStruct((3 * CAP * BLOCK, C), b16),
+            piece,
             piece,
             piece,
             jax.ShapeDtypeStruct((2 * CAP * BLOCK, C), b16),
@@ -438,10 +438,11 @@
     lists = sort_tiles(codes, tile_pattern[0], tile_count)
     for step in range(STEPS):
         far1, far3 = fetch(own, 1, 0), fetch(own, 3, 0)
-        pass1, pass3, out1, out3 = pick_early(asked, own, far1, far3)
+        near, pass1, pass3, out1, out3 = pick_early(asked, requests[0], own, far1, far3)
         low2, high2 = fetch(pass1, 1, 0), fetch(pass3, 3, 0)
         side1, side3 = fetch(out1, 0, 1), fetch(out3, 0, 3)
-        lists, low2, high2 = lax.optimization_barrier((lists, low2, high2))
+        (total,) = run_tiles("near", 0, lists, words, own, (near,))
+        total, low2, high2 = lax.optimization_barrier((total, low2, high2))
         near, out1, out3, out2a, out2b, line = pick_late(asked, requests[0], own, far1, far3, low2, high2)
         lines = tuple(fetch(line, 0, m) for m in (1, 3, 2))
         lines, out2a, out2b, side1, side3 = lax.optimization_barrier(
@@ -449,16 +450,23 @@
         )
         side2a, side2b = fetch(out2a, 0, 2), fetch(out2b, 0, 2)
         late1, late3 = fetch(out1, 0, 1), fetch(out3, 0, 3)
-        col_sums = sum_over_cols(line + lines[0] + lines[1] + lines[2])
-        tables = (side1, side3, near)
-        (total,) = run_tiles("sides", 0, lists, words, own, tables)
-        (total,) = run_tiles("across", 1, lists, words, own, (side2a,), total)
+        sums = line + lines[0] + lines[1] + lines[2]
+        other = swap(sums, "cols_1", 1)
+        (total,) = run_tiles("sides_1", 1, lists, words, own, (side1, near), total)
+        total, other = lax.optimization_barrier((total, other))
+        sums = sums + other
+        other = swap(sums, "cols_0", 1)
+        (total,) = run_tiles("sides_3", 2, lists, words, own, (side3,), total)
+        total, other = lax.optimization_barrier((total, other))
+        sums = sums + other
+        col_sums = sums + swap(sums, "cols_0", 2)
+        (total,) = run_tiles("across", 3, lists, words, own, (side2a,), total)
         total, side2b = lax.optimization_barrier((total, side2b))
-        (total,) = run_tiles("across_more", 2, lists, words, own, (side2b,), total)
+        (total,) = run_tiles("across_more", 4, lists, words, own, (side2b,), total)
         total, late1, late3 = lax.optimization_barrier((total, late1, late3))
         finish = "more" if step < STEPS - 1 else "end"
         current, *own_next = run_tiles(
-            "late", 3, lists, words, own, (late1, late3), total, current, col_sums, finish
+            "late", 5, lists, words, own, (late1, late3), total, current, col_sums, finish
         )
         if own_next:
             (own,) = own_next

time: 174 us -> 172 us (0.989); the launches traced: 173 us -> 173 us
  Pallas kernels: 44.3 us -> 81.1 us
  waiting for transfers between devices: 71.6 us -> 47.5 us
  starting transfers between devices: 54.2 us -> 41.4 us
    pallas_call x8 -> x12, Pallas kernels: 33.4 us -> 64.5 us  [run_tiles(): pl.pallas_call(functools.partial(tile_kernel, part, len(tables), earlier...]
    ppermute x29, waiting for transfers between devices: 61.9 us -> 37 us  [fetch(): return lax.ppermute(value, ALL, pairs(first, second))]
    ppermute x29, starting transfers between devices: 51 us -> 40.9 us  [fetch(): return lax.ppermute(value, ALL, pairs(first, second))]
    pallas_call x1, Pallas kernels: 3.52 us -> 6.57 us  [ask(): pl.pallas_call(ask_kernel, out_shape=(jax.ShapeDtypeStruct((64,), i32), j...]
    ppermute x6, starting transfers between devices: 3.18 us -> 0.43 us  [swap(): lax.ppermute(value, axis, [(i, i ^ step) for i in range(lax.axis_size(axi...]
    pallas_call x1, Pallas kernels: 3.63 us -> 6.33 us  [sort_tiles(): pl.pallas_call(sort_kernel, out_shape=jax.ShapeDtypeStruct((LIST,), i32),...]
  transfers between devices with their start and end apart: 35 -> 35, of which waited for: 19 -> 14; matrix products, arithmetic and copies ran while one was open for 0% -> 0% of each run, Pallas kernels for 20% -> 39%
where the time goes in v2:
time: 172 us; the launch traced here: 173 us
  Pallas kernels  81.1 us (47%)
  waiting for transfers between devices  47.5 us (28%)
  starting transfers between devices  41.4 us (24%)
  local copies, waits for them, and re-layouts  2.06 us (1%)
    pallas_call x12, Pallas kernels, run_tiles(): pl.pallas_call(functools.partial(tile_kernel, part, len(tables), earlier...  64.5 us
    ppermute x29, starting transfers between devices, fetch(): return lax.ppermute(value, ALL, pairs(first, second))  40.9 us
    ppermute x29, waiting for transfers between devices, fetch(): return lax.ppermute(value, ALL, pairs(first, second))  37 us
    ppermute x6, waiting for transfers between devices, swap(): lax.ppermute(value, axis, [(i, i ^ step) for i in range(lax.axis_size(axi...  10.5 us
    pallas_call x1, Pallas kernels, ask(): pl.pallas_call(ask_kernel, out_shape=(jax.ShapeDtypeStruct((64,), i32), j...  6.57 us
    pallas_call x1, Pallas kernels, sort_tiles(): pl.pallas_call(sort_kernel, out_shape=jax.ShapeDtypeStruct((LIST,), i32),...  6.33 us
  transfers between devices with their start and end apart: 35, of which 14 were waited for; matrix products, arithmetic and copies ran while one was open for 0% of the time, Pallas kernels for 39%

profile of v2, /device:TPU:32, one launch (start us, length us, event | category | flops | bytes accessed | tf_op | source)
XLA Modules:
  0.0 173.4 jit_solution(13870044915222836618)
XLA Ops:
  0.0 1.6 copy-done
  1.6 0.1 first.1.own.refs_2_
  1.7 1.6 collective-permute-start.4
  3.3 1.7 %collective-permute-start.3 = (bf16[1040,512]{1,0:T(8,128)(2,1)S(1)}, bf16[1040,512]{1,0:T(8,128)(2,1)S(1)}, u32[]{:S(2)}, u32[]{:S(2)}) collective-permute-start(bf16[1040,512]{1,0:T(8,128)(2,1)S(1)} %first.1.own.refs_2_), channel_id=1, source_target_pairs={{8,0},{33,1},{10,2},{35,3},{12,4},{37,5},{14,6},{39,7},{16,8},{41,... | collective-permute-start | bytes 3194888 | tf_op jit(solution)/shard_map/ppermute | solution.py:55
  5.7 0.1 pad_add_fusion.1.place
  5.8 6.6 %ask.1 = (s32[64]{0:T(128)S(1)}, s32[240]{0:T(256)S(1)}) custom-call(s32[3]{0:T(128)S(1)} %pad_add_fusion.1.place, s32[240]{0:T(256)S(1)} %bitcast.9, s32[240]{0:T(256)S(1)} %bitcast.10, s32[1]{0:T(128)S(6)} %copy.9.count, s32[1024]{0:T(1024)S(1)} %copy-done.2), custom_call_target="tpu_custom_call" | custom-call | tf_op jit(solution)/shard_map/ask/pallas_call | solution.py:115
  12.5 0.8 collective-permute-start.1
  13.3 1.2 collective-permute-start
  14.5 1.6 collective-permute-done.2
  16.0 1.6 collective-permute-done.1
  17.6 1.0 collective-permute-done
  18.7 0.9 pick_early.2
  19.6 2.7 %collective-permute-start.10 = (bf16[1536,512]{1,0:T(8,128)(2,1)S(1)}, bf16[1536,512]{1,0:T(8,128)(2,1)S(1)}, u32[]{:S(2)}, u32[]{:S(2)}) collective-permute-start(bf16[1536,512]{1,0:T(8,128)(2,1)S(1)} %get-tuple-element.79), channel_id=1, source_target_pairs={{32,0},{9,1},{34,2},{11,3},{36,4},{13,5},{38,6},{15,7},{40,8},{17,... | collective-permute-start | bytes 4718600 | tf_op jit(solution)/shard_map/ppermute | solution.py:55
  22.3 1.5 collective-permute-start.6
  23.8 1.7 %collective-permute-start.5 = (bf16[512,512]{1,0:T(8,128)(2,1)S(1)}, bf16[512,512]{1,0:T(8,128)(2,1)S(1)}, u32[]{:S(2)}, u32[]{:S(2)}) collective-permute-start(bf16[512,512]{1,0:T(8,128)(2,1)S(1)} %get-tuple-element.72), channel_id=1, source_target_pairs={{8,0},{33,1},{10,2},{35,3},{12,4},{37,5},{14,6},{39,7},{16,8},{41,... | collective-permute-start | bytes 1572872 | tf_op jit(solution)/shard_map/ppermute | solution.py:55
  25.5 0.3 copy.8
  25.9 6.3 %sort_tiles.1.refs_0_ = s32[680]{0:T(1024)S(1)} custom-call(s32[240]{0:T(256)S(1)} %get-tuple-element.69.codes, s32[240]{0:T(256)S(1)} %bitcast.11, s32[1]{0:T(128)S(6)} %copy.9.count), custom_call_target="tpu_custom_call" | custom-call | tf_op jit(solution)/shard_map/sort_tiles/pallas_call | solution.py:163
  32.3 4.0 %near.2.refs_5_ = f32[1024,512]{1,0:T(8,128)S(1)} custom-call(s32[680]{0:T(1024)S(1)} %sort_tiles.1.refs_0_, s32[193,5,128]{2,1,0:T(8,128)S(1)} %concatenate.3.refs_1_, bf16[1040,512]{1,0:T(8,128)(2,1)S(1)} %first.1.own.refs_2_, bf16[1024,512]{1,0:T(8,128)(2,1)S(1)} %get-tuple-element.71.refs_3_), custom_call_target="tpu_custom_call" | custom-call | tf_op jit(solution)/shard_map/near/pallas_call | solution.py:414
  36.2 2.4 %collective-permute-done.5.low2 = bf16[512,512]{1,0:T(8,128)(2,1)S(1)} collective-permute-done((bf16[512,512]{1,0:T(8,128)(2,1)S(1)}, bf16[512,512]{1,0:T(8,128)(2,1)S(1)}, u32[]{:S(2)}, u32[]{:S(2)}) %collective-permute-start.5) | collective-permute-done | bytes 524320 | tf_op jit(solution)/shard_map/ppermute | solution.py:55
  38.7 0.9 pick_late.2
  39.6 2.3 %collective-permute-start.9 = (f32[8,512]{1,0:T(8,128)S(1)}, f32[8,512]{1,0:T(8,128)S(1)}, u32[]{:S(2)}, u32[]{:S(2)}) collective-permute-start(f32[8,512]{1,0:T(8,128)S(1)} %get-tuple-element.76), channel_id=1, source_target_pairs={{64,0},{17,1},{66,2},{19,3},{68,4},{21,5},{70,6},{23,7},{72,8},{25... | collective-permute-start | bytes 49160 | tf_op jit(solution)/shard_map/ppermute | solution.py:55
  41.9 1.9 %collective-permute-start.8 = (f32[8,512]{1,0:T(8,128)S(1)}, f32[8,512]{1,0:T(8,128)S(1)}, u32[]{:S(2)}, u32[]{:S(2)}) collective-permute-start(f32[8,512]{1,0:T(8,128)S(1)} %get-tuple-element.76), channel_id=1, source_target_pairs={{96,0},{25,1},{98,2},{27,3},{100,4},{29,5},{102,6},{31,7},{104,8},... | collective-permute-start | bytes 49160 | tf_op jit(solution)/shard_map/ppermute | solution.py:55
  43.8 1.3 collective-permute-start.7
  45.1 3.3 %collective-permute-done.9 = f32[8,512]{1,0:T(8,128)S(1)} collective-permute-done((f32[8,512]{1,0:T(8,128)S(1)}, f32[8,512]{1,0:T(8,128)S(1)}, u32[]{:S(2)}, u32[]{:S(2)}) %collective-permute-start.9) | collective-permute-done | bytes 16416 | tf_op jit(solution)/shard_map/ppermute | solution.py:55
  48.4 0.7 collective-permute-start.12
  49.1 2.9 %collective-permute-start.15 = (bf16[1024,512]{1,0:T(8,128)(2,1)S(1)}, bf16[1024,512]{1,0:T(8,128)(2,1)S(1)}, u32[]{:S(2)}, u32[]{:S(2)}) collective-permute-start(bf16[1024,512]{1,0:T(8,128)(2,1)S(1)} %get-tuple-element.92), channel_id=1, source_target_pairs={{64,0},{17,1},{66,2},{19,3},{68,4},{21,5},{70,6},{23,7},{72,8},{25... | collective-permute-start | bytes 3145736 | tf_op jit(solution)/shard_map/ppermute | solution.py:55
  52.0 1.6 collective-permute-start.16
  53.6 0.4 collective-permute-start.17
  54.1 7.1 %sides_1.2.refs_4_ = f32[1024,512]{1,0:T(8,128)S(1)} custom-call(s32[680]{0:T(1024)S(1)} %sort_tiles.1.refs_0_, s32[193,5,128]{2,1,0:T(8,128)S(1)} %concatenate.3.refs_1_, bf16[1040,512]{1,0:T(8,128)(2,1)S(1)} %first.1.own.refs_2_, bf16[1536,512]{1,0:T(8,128)(2,1)S(1)} %collective-permute-done.10.refs_3_, bf16[512,512]{1,0:T(8,128)(2,1)S(1)} %get-tuple-element.84.refs_4_, ...), custom_call_target="tpu_custom_call" | custom-call | tf_op jit(solution)/shard_map/sides_1/pallas_call | solution.py:414
  61.3 0.1 collective-permute-start.14
  61.3 6.1 %sides_3.2.refs_4_ = f32[1024,512]{1,0:T(8,128)S(1)} custom-call(s32[680]{0:T(1024)S(1)} %sort_tiles.1.refs_0_, s32[193,5,128]{2,1,0:T(8,128)S(1)} %concatenate.3.refs_1_, bf16[1040,512]{1,0:T(8,128)(2,1)S(1)} %first.1.own.refs_2_, bf16[1536,512]{1,0:T(8,128)(2,1)S(1)} %collective-permute-done.11.refs_3_, f32[1024,512]{1,0:T(8,128)S(1)} %sides_1.2.refs_4_), custom_call_target="tpu_custom_call" | custom-call | tf_op jit(solution)/shard_map/sides_3/pallas_call | solution.py:414
  67.5 0.1 collective-permute-start.18
  67.6 5.2 %collective-permute-done.18 = f32[8,512]{1,0:T(8,128)S(1)} collective-permute-done((f32[8,512]{1,0:T(8,128)S(1)}, f32[8,512]{1,0:T(8,128)S(1)}, u32[]{:S(2)}, u32[]{:S(2)}) %collective-permute-start.18) | collective-permute-done | bytes 16416 | tf_op jit(solution)/shard_map/ppermute | solution.py:59
  72.8 4.8 %across.2.refs_4_ = f32[1024,512]{1,0:T(8,128)S(1)} custom-call(s32[680]{0:T(1024)S(1)} %sort_tiles.1.refs_0_, s32[193,5,128]{2,1,0:T(8,128)S(1)} %concatenate.3.refs_1_, bf16[1040,512]{1,0:T(8,128)(2,1)S(1)} %first.1.own.refs_2_, bf16[1024,512]{1,0:T(8,128)(2,1)S(1)} %collective-permute-done.12.refs_3_, f32[1024,512]{1,0:T(8,128)S(1)} %sides_3.2.refs_4_), custom_call_target="tpu_custom_call" | custom-call | tf_op jit(solution)/shard_map/across/pallas_call | solution.py:414
  77.7 5.0 %across_more.2.refs_5_ = f32[1024,512]{1,0:T(8,128)S(1)} custom-call(s32[680]{0:T(1024)S(1)} %sort_tiles.1.refs_0_, s32[193,5,128]{2,1,0:T(8,128)S(1)} %concatenate.3.refs_1_, bf16[1040,512]{1,0:T(8,128)(2,1)S(1)} %first.1.own.refs_2_, bf16[1024,512]{1,0:T(8,128)(2,1)S(1)} %collective-permute-done.15.refs_3_, f32[1024,512]{1,0:T(8,128)S(1)} %across.2.refs_4_), custom_call_target="tpu_custom_call" | custom-call | tf_op jit(solution)/shard_map/across_more/pallas_call | solution.py:414
  82.7 5.1 %late.2 = (f32[1024,512]{1,0:T(8,128)S(1)}, bf16[1040,512]{1,0:T(8,128)(2,1)S(1)}) custom-call(s32[680]{0:T(1024)S(1)} %sort_tiles.1.refs_0_, s32[193,5,128]{2,1,0:T(8,128)S(1)} %concatenate.3.refs_1_, bf16[1040,512]{1,0:T(8,128)(2,1)S(1)} %first.1.own.refs_2_, bf16[512,512]{1,0:T(8,128)(2,1)S(1)} %collective-permute-done.16.refs_3_, ...), custom_call_target="tpu_custom_call" | custom-call | tf_op jit(solution)/shard_map/late/pallas_call | solution.py:414
  87.8 0.1 collective-permute-start.20
  87.9 3.2 %collective-permute-start.19 = (bf16[1040,512]{1,0:T(8,128)(2,1)S(1)}, bf16[1040,512]{1,0:T(8,128)(2,1)S(1)}, u32[]{:S(2)}, u32[]{:S(2)}) collective-permute-start(bf16[1040,512]{1,0:T(8,128)(2,1)S(1)} %get-tuple-element.101.own.refs_2_), channel_id=1, source_target_pairs={{8,0},{33,1},{10,2},{35,3},{12,4},{37,5},{14,6},{39,7},{16,8},{41,... | collective-permute-start | bytes 3194888 | tf_op jit(solution)/shard_map/ppermute | solution.py:55
  91.1 12.9 %collective-permute-done.20.far3 = bf16[1040,512]{1,0:T(8,128)(2,1)S(1)} collective-permute-done((bf16[1040,512]{1,0:T(8,128)(2,1)S(1)}, bf16[1040,512]{1,0:T(8,128)(2,1)S(1)}, u32[]{:S(2)}, u32[]{:S(2)}) %collective-permute-start.20) | collective-permute-done | bytes 1064992 | tf_op jit(solution)/shard_map/ppermute | solution.py:55
  104.1 2.3 %collective-permute-done.19.far1 = bf16[1040,512]{1,0:T(8,128)(2,1)S(1)} collective-permute-done((bf16[1040,512]{1,0:T(8,128)(2,1)S(1)}, bf16[1040,512]{1,0:T(8,128)(2,1)S(1)}, u32[]{:S(2)}, u32[]{:S(2)}) %collective-permute-start.19) | collective-permute-done | bytes 1064992 | tf_op jit(solution)/shard_map/ppermute | solution.py:55
  106.3 0.9 pick_early.3
  107.3 2.0 %collective-permute-start.27 = (bf16[1536,512]{1,0:T(8,128)(2,1)S(1)}, bf16[1536,512]{1,0:T(8,128)(2,1)S(1)}, u32[]{:S(2)}, u32[]{:S(2)}) collective-permute-start(bf16[1536,512]{1,0:T(8,128)(2,1)S(1)} %get-tuple-element.111), channel_id=1, source_target_pairs={{96,0},{25,1},{98,2},{27,3},{100,4},{29,5},{102,6},{31,7},{104,8},... | collective-permute-start | bytes 4718600 | tf_op jit(solution)/shard_map/ppermute | solution.py:55
  109.4 3.7 %collective-permute-start.21 = (bf16[512,512]{1,0:T(8,128)(2,1)S(1)}, bf16[512,512]{1,0:T(8,128)(2,1)S(1)}, u32[]{:S(2)}, u32[]{:S(2)}) collective-permute-start(bf16[512,512]{1,0:T(8,128)(2,1)S(1)} %get-tuple-element.103), channel_id=1, source_target_pairs={{8,0},{33,1},{10,2},{35,3},{12,4},{37,5},{14,6},{39,7},{16,8},{41,... | collective-permute-start | bytes 1572872 | tf_op jit(solution)/shard_map/ppermute | solution.py:55
  113.1 4.0 %near.3.refs_5_ = f32[1024,512]{1,0:T(8,128)S(1)} custom-call(s32[680]{0:T(1024)S(1)} %sort_tiles.1.refs_0_, s32[193,5,128]{2,1,0:T(8,128)S(1)} %concatenate.3.refs_1_, bf16[1040,512]{1,0:T(8,128)(2,1)S(1)} %get-tuple-element.101.own.refs_2_, bf16[1024,512]{1,0:T(8,128)(2,1)S(1)} %get-tuple-element.102.refs_3_), custom_call_target="tpu_custom_call" | custom-call | tf_op jit(solution)/shard_map/near/pallas_call | solution.py:414
  117.1 8.4 %collective-permute-done.21.low2 = bf16[512,512]{1,0:T(8,128)(2,1)S(1)} collective-permute-done((bf16[512,512]{1,0:T(8,128)(2,1)S(1)}, bf16[512,512]{1,0:T(8,128)(2,1)S(1)}, u32[]{:S(2)}, u32[]{:S(2)}) %collective-permute-start.21) | collective-permute-done | bytes 524320 | tf_op jit(solution)/shard_map/ppermute | solution.py:55
  125.5 0.9 collective-permute-done.22.high2
  126.4 0.9 pick_late.3
  127.3 0.1 collective-permute-start.25
  127.4 2.0 %collective-permute-start.24 = (f32[8,512]{1,0:T(8,128)S(1)}, f32[8,512]{1,0:T(8,128)S(1)}, u32[]{:S(2)}, u32[]{:S(2)}) collective-permute-start(f32[8,512]{1,0:T(8,128)S(1)} %get-tuple-element.107), channel_id=1, source_target_pairs={{96,0},{25,1},{98,2},{27,3},{100,4},{29,5},{102,6},{31,7},{104,8},... | collective-permute-start | bytes 49160 | tf_op jit(solution)/shard_map/ppermute | solution.py:55
  129.4 1.3 collective-permute-start.23
  130.7 1.9 %collective-permute-done.25 = f32[8,512]{1,0:T(8,128)S(1)} collective-permute-done((f32[8,512]{1,0:T(8,128)S(1)}, f32[8,512]{1,0:T(8,128)S(1)}, u32[]{:S(2)}, u32[]{:S(2)}) %collective-permute-start.25) | collective-permute-done | bytes 16416 | tf_op jit(solution)/shard_map/ppermute | solution.py:55
  132.6 0.5 collective-permute-done.23
  133.1 2.2 %collective-permute-start.28 = (bf16[1024,512]{1,0:T(8,128)(2,1)S(1)}, bf16[1024,512]{1,0:T(8,128)(2,1)S(1)}, u32[]{:S(2)}, u32[]{:S(2)}) collective-permute-start(bf16[1024,512]{1,0:T(8,128)(2,1)S(1)} %get-tuple-element.112), channel_id=1, source_target_pairs={{64,0},{17,1},{66,2},{19,3},{68,4},{21,5},{70,6},{23,7},{72,8},{25... | collective-permute-start | bytes 3145736 | tf_op jit(solution)/shard_map/ppermute | solution.py:55
  135.3 1.4 collective-permute-start.31
  136.7 2.6 %collective-permute-start.32 = (bf16[512,512]{1,0:T(8,128)(2,1)S(1)}, bf16[512,512]{1,0:T(8,128)(2,1)S(1)}, u32[]{:S(2)}, u32[]{:S(2)}) collective-permute-start(bf16[512,512]{1,0:T(8,128)(2,1)S(1)} %get-tuple-element.126), channel_id=1, source_target_pairs={{32,0},{9,1},{34,2},{11,3},{36,4},{13,5},{38,6},{15,7},{40,8},{17,... | collective-permute-start | bytes 1572872 | tf_op jit(solution)/shard_map/ppermute | solution.py:55
  139.2 0.1 collective-permute-start.29
  139.3 7.1 %sides_1.3.refs_4_ = f32[1024,512]{1,0:T(8,128)S(1)} custom-call(s32[680]{0:T(1024)S(1)} %sort_tiles.1.refs_0_, s32[193,5,128]{2,1,0:T(8,128)S(1)} %concatenate.3.refs_1_, bf16[1040,512]{1,0:T(8,128)(2,1)S(1)} %get-tuple-element.101.own.refs_2_, bf16[1536,512]{1,0:T(8,128)(2,1)S(1)} %collective-permute-done.26.refs_3_, ...), custom_call_target="tpu_custom_call" | custom-call | tf_op jit(solution)/shard_map/sides_1/pallas_call | solution.py:414
  146.5 0.1 collective-permute-start.30
  146.6 6.1 %sides_3.3.refs_4_ = f32[1024,512]{1,0:T(8,128)S(1)} custom-call(s32[680]{0:T(1024)S(1)} %sort_tiles.1.refs_0_, s32[193,5,128]{2,1,0:T(8,128)S(1)} %concatenate.3.refs_1_, bf16[1040,512]{1,0:T(8,128)(2,1)S(1)} %get-tuple-element.101.own.refs_2_, bf16[1536,512]{1,0:T(8,128)(2,1)S(1)} %collective-permute-done.27.refs_3_, f32[1024,512]{1,0:T(8,128)S(1)} %sides_1.3.refs_4_), custom_call_target="tpu_custom_call" | custom-call | tf_op jit(solution)/shard_map/sides_3/pallas_call | solution.py:414
  152.7 0.1 collective-permute-start.34
  152.8 5.2 %collective-permute-done.34 = f32[8,512]{1,0:T(8,128)S(1)} collective-permute-done((f32[8,512]{1,0:T(8,128)S(1)}, f32[8,512]{1,0:T(8,128)S(1)}, u32[]{:S(2)}, u32[]{:S(2)}) %collective-permute-start.34) | collective-permute-done | bytes 16416 | tf_op jit(solution)/shard_map/ppermute | solution.py:59
  158.0 4.6 %across.3.refs_4_ = f32[1024,512]{1,0:T(8,128)S(1)} custom-call(s32[680]{0:T(1024)S(1)} %sort_tiles.1.refs_0_, s32[193,5,128]{2,1,0:T(8,128)S(1)} %concatenate.3.refs_1_, bf16[1040,512]{1,0:T(8,128)(2,1)S(1)} %get-tuple-element.101.own.refs_2_, bf16[1024,512]{1,0:T(8,128)(2,1)S(1)} %collective-permute-done.28.refs_3_, f32[1024,512]{1,0:T(8,128)S(1)} %sides_3.3.refs_4_), custom_call_target="tpu_custom_call" | custom-call | tf_op jit(solution)/shard_map/across/pallas_call | solution.py:414
  162.6 4.6 %across_more.3.refs_5_ = f32[1024,512]{1,0:T(8,128)S(1)} custom-call(s32[680]{0:T(1024)S(1)} %sort_tiles.1.refs_0_, s32[193,5,128]{2,1,0:T(8,128)S(1)} %concatenate.3.refs_1_, bf16[1040,512]{1,0:T(8,128)(2,1)S(1)} %get-tuple-element.101.own.refs_2_, bf16[1024,512]{1,0:T(8,128)(2,1)S(1)} %collective-permute-done.31.refs_3_, f32[1024,512]{1,0:T(8,128)S(1)} %across.3.refs_4_), custom_call_target="tpu_custom_call" | custom-call | tf_op jit(solution)/shard_map/across_more/pallas_call | solution.py:414
  167.1 6.1 %late.3 = f32[1024,512]{1,0:T(8,128)} custom-call(s32[680]{0:T(1024)S(1)} %sort_tiles.1.refs_0_, s32[193,5,128]{2,1,0:T(8,128)S(1)} %concatenate.3.refs_1_, bf16[1040,512]{1,0:T(8,128)(2,1)S(1)} %get-tuple-element.101.own.refs_2_, bf16[512,512]{1,0:T(8,128)(2,1)S(1)} %collective-permute-done.32.refs_3_, ...), custom_call_target="tpu_custom_call" | custom-call | tf_op jit(solution)/shard_map/late/pallas_call | solution.py:414
  (52 shorter events, 0.4 us)
Async XLA Ops:
  0.0 1.6 copy-start
  1.6 4.2 %copy-start.2 = (s32[1024]{0:T(1024)S(1)}, s32[1024]{0:T(1024)}, u32[]{:S(2)}) copy-start(s32[1024]{0:T(1024)} %home.1) | copy-start | bytes 12292
  1.6 4.2 %copy-start.3 = (s32[1,240]{1,0:T(1,128)S(1)}, s32[1,240]{1,0:T(1,128)}, u32[]{:S(2)}) copy-start(s32[1,240]{1,0:T(1,128)} %param.8) | copy-start | bytes 2884
  1.6 4.2 %copy-start.4 = (s32[1,240]{1,0:T(1,128)S(1)}, s32[1,240]{1,0:T(1,128)}, u32[]{:S(2)}) copy-start(s32[1,240]{1,0:T(1,128)} %param.9) | copy-start | bytes 2884
  1.7 16.9 %collective-permute-start.4 = (bf16[1040,512]{1,0:T(8,128)(2,1)S(1)}, bf16[1040,512]{1,0:T(8,128)(2,1)S(1)}, u32[]{:S(2)}, u32[]{:S(2)}) collective-permute-start(bf16[1040,512]{1,0:T(8,128)(2,1)S(1)} %first.1.own.refs_2_), channel_id=1, source_target_pairs={{24,0},{97,1},{26,2},{99,3},{28,4},{101,5},{30,6},{103,7},{0,8},{1... | collective-permute-start | bytes 3194888 | tf_op jit(solution)/shard_map/ppermute | solution.py:55
  3.3 15.4 %collective-permute-start.3 = (bf16[1040,512]{1,0:T(8,128)(2,1)S(1)}, bf16[1040,512]{1,0:T(8,128)(2,1)S(1)}, u32[]{:S(2)}, u32[]{:S(2)}) collective-permute-start(bf16[1040,512]{1,0:T(8,128)(2,1)S(1)} %first.1.own.refs_2_), channel_id=1, source_target_pairs={{8,0},{33,1},{10,2},{35,3},{12,4},{37,5},{14,6},{39,7},{16,8},{41,... | collective-permute-start | bytes 3194888 | tf_op jit(solution)/shard_map/ppermute | solution.py:55
  12.4 3.6 %collective-permute-start.2 = (s32[16]{0:T(128)S(1)}, s32[16]{0:T(128)S(1)}, u32[]{:S(2)}, u32[]{:S(2)}) collective-permute-start(s32[16]{0:T(128)S(1)} %get-tuple-element.134), channel_id=1, source_target_pairs={{32,0},{9,1},{34,2},{11,3},{36,4},{13,5},{38,6},{15,7},{40,8},{17,... | collective-permute-start | bytes 200 | tf_op jit(solution)/shard_map/ppermute | solution.py:55
  12.5 5.2 %collective-permute-start.1 = (s32[16]{0:T(128)S(1)}, s32[16]{0:T(128)S(1)}, u32[]{:S(2)}, u32[]{:S(2)}) collective-permute-start(s32[16]{0:T(128)S(1)} %get-tuple-element.135), channel_id=1, source_target_pairs={{64,0},{17,1},{66,2},{19,3},{68,4},{21,5},{70,6},{23,7},{72,8},{25... | collective-permute-start | bytes 200 | tf_op jit(solution)/shard_map/ppermute | solution.py:55
  13.3 5.4 %collective-permute-start = (s32[16]{0:T(128)S(1)}, s32[16]{0:T(128)S(1)}, u32[]{:S(2)}, u32[]{:S(2)}) collective-permute-start(s32[16]{0:T(128)S(1)} %get-tuple-element.136), channel_id=1, source_target_pairs={{96,0},{25,1},{98,2},{27,3},{100,4},{29,5},{102,6},{31,7},{104,8},... | collective-permute-start | bytes 200 | tf_op jit(solution)/shard_map/ppermute | solution.py:55
  18.7 6.8 %copy-start.6 = (s32[192,5,128]{2,0,1:T(8,128)S(1)}, s32[192,5,128]{2,0,1:T(8,128)}, u32[]{:S(2)}) copy-start(s32[192,5,128]{2,0,1:T(8,128)} %param.13) | copy-start | bytes 1474564
  19.6 6.3 %copy-start.5 = (s32[1,240]{1,0:T(1,128)S(1)}, s32[1,240]{1,0:T(1,128)}, u32[]{:S(2)}) copy-start(s32[1,240]{1,0:T(1,128)} %param.10) | copy-start | bytes 2884
  19.6 28.8 %collective-permute-start.10 = (bf16[1536,512]{1,0:T(8,128)(2,1)S(1)}, bf16[1536,512]{1,0:T(8,128)(2,1)S(1)}, u32[]{:S(2)}, u32[]{:S(2)}) collective-permute-start(bf16[1536,512]{1,0:T(8,128)(2,1)S(1)} %get-tuple-element.79), channel_id=1, source_target_pairs={{32,0},{9,1},{34,2},{11,3},{36,4},{13,5},{38,6},{15,7},{40,8},{17,... | collective-permute-start | bytes 4718600 | tf_op jit(solution)/shard_map/ppermute | solution.py:55
  22.3 26.1 %collective-permute-start.11 = (bf16[1536,512]{1,0:T(8,128)(2,1)S(1)}, bf16[1536,512]{1,0:T(8,128)(2,1)S(1)}, u32[]{:S(2)}, u32[]{:S(2)}) collective-permute-start(bf16[1536,512]{1,0:T(8,128)(2,1)S(1)} %get-tuple-element.80), channel_id=1, source_target_pairs={{96,0},{25,1},{98,2},{27,3},{100,4},{29,5},{102,6},{31,7},{104,8},... | collective-permute-start | bytes 4718600 | tf_op jit(solution)/shard_map/ppermute | solution.py:55
  22.3 16.4 %collective-permute-start.6 = (bf16[528,512]{1,0:T(8,128)(2,1)S(1)}, bf16[528,512]{1,0:T(8,128)(2,1)S(1)}, u32[]{:S(2)}, u32[]{:S(2)}) collective-permute-start(bf16[528,512]{1,0:T(8,128)(2,1)S(1)} %get-tuple-element.73), channel_id=1, source_target_pairs={{24,0},{97,1},{26,2},{99,3},{28,4},{101,5},{30,6},{103,7},{0,8},{1... | collective-permute-start | bytes 1622024 | tf_op jit(solution)/shard_map/ppermute | solution.py:55
  23.8 14.9 %collective-permute-start.5 = (bf16[512,512]{1,0:T(8,128)(2,1)S(1)}, bf16[512,512]{1,0:T(8,128)(2,1)S(1)}, u32[]{:S(2)}, u32[]{:S(2)}) collective-permute-start(bf16[512,512]{1,0:T(8,128)(2,1)S(1)} %get-tuple-element.72), channel_id=1, source_target_pairs={{8,0},{33,1},{10,2},{35,3},{12,4},{37,5},{14,6},{39,7},{16,8},{41,... | collective-permute-start | bytes 1572872 | tf_op jit(solution)/shard_map/ppermute | solution.py:55
  39.6 8.8 %collective-permute-start.9 = (f32[8,512]{1,0:T(8,128)S(1)}, f32[8,512]{1,0:T(8,128)S(1)}, u32[]{:S(2)}, u32[]{:S(2)}) collective-permute-start(f32[8,512]{1,0:T(8,128)S(1)} %get-tuple-element.76), channel_id=1, source_target_pairs={{64,0},{17,1},{66,2},{19,3},{68,4},{21,5},{70,6},{23,7},{72,8},{25... | collective-permute-start | bytes 49160 | tf_op jit(solution)/shard_map/ppermute | solution.py:55
  41.9 6.5 %collective-permute-start.8 = (f32[8,512]{1,0:T(8,128)S(1)}, f32[8,512]{1,0:T(8,128)S(1)}, u32[]{:S(2)}, u32[]{:S(2)}) collective-permute-start(f32[8,512]{1,0:T(8,128)S(1)} %get-tuple-element.76), channel_id=1, source_target_pairs={{96,0},{25,1},{98,2},{27,3},{100,4},{29,5},{102,6},{31,7},{104,8},... | collective-permute-start | bytes 49160 | tf_op jit(solution)/shard_map/ppermute | solution.py:55
  43.8 4.6 %collective-permute-start.7 = (f32[8,512]{1,0:T(8,128)S(1)}, f32[8,512]{1,0:T(8,128)S(1)}, u32[]{:S(2)}, u32[]{:S(2)}) collective-permute-start(f32[8,512]{1,0:T(8,128)S(1)} %get-tuple-element.76), channel_id=1, source_target_pairs={{32,0},{9,1},{34,2},{11,3},{36,4},{13,5},{38,6},{15,7},{40,8},{17,... | collective-permute-start | bytes 49160 | tf_op jit(solution)/shard_map/ppermute | solution.py:55
  48.4 24.4 %collective-permute-start.12 = (bf16[1024,512]{1,0:T(8,128)(2,1)S(1)}, bf16[1024,512]{1,0:T(8,128)(2,1)S(1)}, u32[]{:S(2)}, u32[]{:S(2)}) collective-permute-start(bf16[1024,512]{1,0:T(8,128)(2,1)S(1)} %get-tuple-element.81), channel_id=1, source_target_pairs={{64,0},{17,1},{66,2},{19,3},{68,4},{21,5},{70,6},{23,7},{72,8},{25... | collective-permute-start | bytes 3145736 | tf_op jit(solution)/shard_map/ppermute | solution.py:55
  49.1 28.5 %collective-permute-start.15 = (bf16[1024,512]{1,0:T(8,128)(2,1)S(1)}, bf16[1024,512]{1,0:T(8,128)(2,1)S(1)}, u32[]{:S(2)}, u32[]{:S(2)}) collective-permute-start(bf16[1024,512]{1,0:T(8,128)(2,1)S(1)} %get-tuple-element.92), channel_id=1, source_target_pairs={{64,0},{17,1},{66,2},{19,3},{68,4},{21,5},{70,6},{23,7},{72,8},{25... | collective-permute-start | bytes 3145736 | tf_op jit(solution)/shard_map/ppermute | solution.py:55
  52.0 30.6 %collective-permute-start.16 = (bf16[512,512]{1,0:T(8,128)(2,1)S(1)}, bf16[512,512]{1,0:T(8,128)(2,1)S(1)}, u32[]{:S(2)}, u32[]{:S(2)}) collective-permute-start(bf16[512,512]{1,0:T(8,128)(2,1)S(1)} %get-tuple-element.95), channel_id=1, source_target_pairs={{32,0},{9,1},{34,2},{11,3},{36,4},{13,5},{38,6},{15,7},{40,8},{17,... | collective-permute-start | bytes 1572872 | tf_op jit(solution)/shard_map/ppermute | solution.py:55
  53.6 29.0 %collective-permute-start.17 = (bf16[512,512]{1,0:T(8,128)(2,1)S(1)}, bf16[512,512]{1,0:T(8,128)(2,1)S(1)}, u32[]{:S(2)}, u32[]{:S(2)}) collective-permute-start(bf16[512,512]{1,0:T(8,128)(2,1)S(1)} %get-tuple-element.96), channel_id=1, source_target_pairs={{96,0},{25,1},{98,2},{27,3},{100,4},{29,5},{102,6},{31,7},{104,8},... | collective-permute-start | bytes 1572872 | tf_op jit(solution)/shard_map/ppermute | solution.py:55
  54.1 7.2 %collective-permute-start.13 = (f32[8,512]{1,0:T(8,128)S(1)}, f32[8,512]{1,0:T(8,128)S(1)}, u32[]{:S(2)}, u32[]{:S(2)}) collective-permute-start(f32[8,512]{1,0:T(8,128)S(1)} %add_add_fusion.1), channel_id=1, source_target_pairs={{0,1},{1,0},{2,3},{3,2},{4,5},{5,4},{6,7},{7,6},{8,9},{9,8},{10,11... | collective-permute-start | bytes 49160 | tf_op jit(solution)/shard_map/ppermute | solution.py:59
  61.3 6.2 %collective-permute-start.14 = (f32[8,512]{1,0:T(8,128)S(1)}, f32[8,512]{1,0:T(8,128)S(1)}, u32[]{:S(2)}, u32[]{:S(2)}) collective-permute-start(f32[8,512]{1,0:T(8,128)S(1)} %add.41), channel_id=1, source_target_pairs={{0,2},{2,0},{4,6},{6,4},{1,3},{3,1},{5,7},{7,5},{8,10},{10,8},{12,... | collective-permute-start | bytes 49160 | tf_op jit(solution)/shard_map/ppermute | solution.py:59
  67.5 5.3 %collective-permute-start.18 = (f32[8,512]{1,0:T(8,128)S(1)}, f32[8,512]{1,0:T(8,128)S(1)}, u32[]{:S(2)}, u32[]{:S(2)}) collective-permute-start(f32[8,512]{1,0:T(8,128)S(1)} %add.42), channel_id=1, source_target_pairs={{0,4},{2,6},{4,0},{6,2},{1,5},{3,7},{5,1},{7,3},{8,12},{10,14},{12... | collective-permute-start | bytes 49160 | tf_op jit(solution)/shard_map/ppermute | solution.py:59
  77.6 5.0 %copy-start.1 = (f32[1024,512]{1,0:T(8,128)S(1)}, f32[1024,512]{1,0:T(8,128)}, u32[]{:S(2)}) copy-start(f32[1024,512]{1,0:T(8,128)} %refs_6_.1) | copy-start | bytes 6291460
  87.8 16.3 %collective-permute-start.20 = (bf16[1040,512]{1,0:T(8,128)(2,1)S(1)}, bf16[1040,512]{1,0:T(8,128)(2,1)S(1)}, u32[]{:S(2)}, u32[]{:S(2)}) collective-permute-start(bf16[1040,512]{1,0:T(8,128)(2,1)S(1)} %get-tuple-element.101.own.refs_2_), channel_id=1, source_target_pairs={{24,0},{97,1},{26,2},{99,3},{28,4},{101,5},{30,6},{103,7},{0,8},{1... | collective-permute-start | bytes 3194888 | tf_op jit(solution)/shard_map/ppermute | solution.py:55
  87.9 18.5 %collective-permute-start.19 = (bf16[1040,512]{1,0:T(8,128)(2,1)S(1)}, bf16[1040,512]{1,0:T(8,128)(2,1)S(1)}, u32[]{:S(2)}, u32[]{:S(2)}) collective-permute-start(bf16[1040,512]{1,0:T(8,128)(2,1)S(1)} %get-tuple-element.101.own.refs_2_), channel_id=1, source_target_pairs={{8,0},{33,1},{10,2},{35,3},{12,4},{37,5},{14,6},{39,7},{16,8},{41,... | collective-permute-start | bytes 3194888 | tf_op jit(solution)/shard_map/ppermute | solution.py:55
  107.3 25.9 %collective-permute-start.26 = (bf16[1536,512]{1,0:T(8,128)(2,1)S(1)}, bf16[1536,512]{1,0:T(8,128)(2,1)S(1)}, u32[]{:S(2)}, u32[]{:S(2)}) collective-permute-start(bf16[1536,512]{1,0:T(8,128)(2,1)S(1)} %get-tuple-element.110), channel_id=1, source_target_pairs={{32,0},{9,1},{34,2},{11,3},{36,4},{13,5},{38,6},{15,7},{40,8},{17,... | collective-permute-start | bytes 4718600 | tf_op jit(solution)/shard_map/ppermute | solution.py:55
  107.3 25.8 %collective-permute-start.27 = (bf16[1536,512]{1,0:T(8,128)(2,1)S(1)}, bf16[1536,512]{1,0:T(8,128)(2,1)S(1)}, u32[]{:S(2)}, u32[]{:S(2)}) collective-permute-start(bf16[1536,512]{1,0:T(8,128)(2,1)S(1)} %get-tuple-element.111), channel_id=1, source_target_pairs={{96,0},{25,1},{98,2},{27,3},{100,4},{29,5},{102,6},{31,7},{104,8},... | collective-permute-start | bytes 4718600 | tf_op jit(solution)/shard_map/ppermute | solution.py:55
  109.4 17.1 %collective-permute-start.22 = (bf16[528,512]{1,0:T(8,128)(2,1)S(1)}, bf16[528,512]{1,0:T(8,128)(2,1)S(1)}, u32[]{:S(2)}, u32[]{:S(2)}) collective-permute-start(bf16[528,512]{1,0:T(8,128)(2,1)S(1)} %get-tuple-element.104), channel_id=1, source_target_pairs={{24,0},{97,1},{26,2},{99,3},{28,4},{101,5},{30,6},{103,7},{0,8},{1... | collective-permute-start | bytes 1622024 | tf_op jit(solution)/shard_map/ppermute | solution.py:55
  109.4 16.1 %collective-permute-start.21 = (bf16[512,512]{1,0:T(8,128)(2,1)S(1)}, bf16[512,512]{1,0:T(8,128)(2,1)S(1)}, u32[]{:S(2)}, u32[]{:S(2)}) collective-permute-start(bf16[512,512]{1,0:T(8,128)(2,1)S(1)} %get-tuple-element.103), channel_id=1, source_target_pairs={{8,0},{33,1},{10,2},{35,3},{12,4},{37,5},{14,6},{39,7},{16,8},{41,... | collective-permute-start | bytes 1572872 | tf_op jit(solution)/shard_map/ppermute | solution.py:55
  127.3 5.3 %collective-permute-start.25 = (f32[8,512]{1,0:T(8,128)S(1)}, f32[8,512]{1,0:T(8,128)S(1)}, u32[]{:S(2)}, u32[]{:S(2)}) collective-permute-start(f32[8,512]{1,0:T(8,128)S(1)} %get-tuple-element.107), channel_id=1, source_target_pairs={{64,0},{17,1},{66,2},{19,3},{68,4},{21,5},{70,6},{23,7},{72,8},{25... | collective-permute-start | bytes 49160 | tf_op jit(solution)/shard_map/ppermute | solution.py:55
  127.4 5.2 %collective-permute-start.24 = (f32[8,512]{1,0:T(8,128)S(1)}, f32[8,512]{1,0:T(8,128)S(1)}, u32[]{:S(2)}, u32[]{:S(2)}) collective-permute-start(f32[8,512]{1,0:T(8,128)S(1)} %get-tuple-element.107), channel_id=1, source_target_pairs={{96,0},{25,1},{98,2},{27,3},{100,4},{29,5},{102,6},{31,7},{104,8},... | collective-permute-start | bytes 49160 | tf_op jit(solution)/shard_map/ppermute | solution.py:55
  129.4 3.7 %collective-permute-start.23 = (f32[8,512]{1,0:T(8,128)S(1)}, f32[8,512]{1,0:T(8,128)S(1)}, u32[]{:S(2)}, u32[]{:S(2)}) collective-permute-start(f32[8,512]{1,0:T(8,128)S(1)} %get-tuple-element.107), channel_id=1, source_target_pairs={{32,0},{9,1},{34,2},{11,3},{36,4},{13,5},{38,6},{15,7},{40,8},{17,... | collective-permute-start | bytes 49160 | tf_op jit(solution)/shard_map/ppermute | solution.py:55
  133.1 24.9 %collective-permute-start.28 = (bf16[1024,512]{1,0:T(8,128)(2,1)S(1)}, bf16[1024,512]{1,0:T(8,128)(2,1)S(1)}, u32[]{:S(2)}, u32[]{:S(2)}) collective-permute-start(bf16[1024,512]{1,0:T(8,128)(2,1)S(1)} %get-tuple-element.112), channel_id=1, source_target_pairs={{64,0},{17,1},{66,2},{19,3},{68,4},{21,5},{70,6},{23,7},{72,8},{25... | collective-permute-start | bytes 3145736 | tf_op jit(solution)/shard_map/ppermute | solution.py:55
  135.3 27.3 %collective-permute-start.31 = (bf16[1024,512]{1,0:T(8,128)(2,1)S(1)}, bf16[1024,512]{1,0:T(8,128)(2,1)S(1)}, u32[]{:S(2)}, u32[]{:S(2)}) collective-permute-start(bf16[1024,512]{1,0:T(8,128)(2,1)S(1)} %get-tuple-element.123), channel_id=1, source_target_pairs={{64,0},{17,1},{66,2},{19,3},{68,4},{21,5},{70,6},{23,7},{72,8},{25... | collective-permute-start | bytes 3145736 | tf_op jit(solution)/shard_map/ppermute | solution.py:55
  136.7 30.5 %collective-permute-start.32 = (bf16[512,512]{1,0:T(8,128)(2,1)S(1)}, bf16[512,512]{1,0:T(8,128)(2,1)S(1)}, u32[]{:S(2)}, u32[]{:S(2)}) collective-permute-start(bf16[512,512]{1,0:T(8,128)(2,1)S(1)} %get-tuple-element.126), channel_id=1, source_target_pairs={{32,0},{9,1},{34,2},{11,3},{36,4},{13,5},{38,6},{15,7},{40,8},{17,... | collective-permute-start | bytes 1572872 | tf_op jit(solution)/shard_map/ppermute | solution.py:55
  139.2 27.9 %collective-permute-start.33 = (bf16[512,512]{1,0:T(8,128)(2,1)S(1)}, bf16[512,512]{1,0:T(8,128)(2,1)S(1)}, u32[]{:S(2)}, u32[]{:S(2)}) collective-permute-start(bf16[512,512]{1,0:T(8,128)(2,1)S(1)} %get-tuple-element.127), channel_id=1, source_target_pairs={{96,0},{25,1},{98,2},{27,3},{100,4},{29,5},{102,6},{31,7},{104,8},... | collective-permute-start | bytes 1572872 | tf_op jit(solution)/shard_map/ppermute | solution.py:55
  139.2 7.2 %collective-permute-start.29 = (f32[8,512]{1,0:T(8,128)S(1)}, f32[8,512]{1,0:T(8,128)S(1)}, u32[]{:S(2)}, u32[]{:S(2)}) collective-permute-start(f32[8,512]{1,0:T(8,128)S(1)} %add_add_fusion), channel_id=1, source_target_pairs={{0,1},{1,0},{2,3},{3,2},{4,5},{5,4},{6,7},{7,6},{8,9},{9,8},{10,11... | collective-permute-start | bytes 49160 | tf_op jit(solution)/shard_map/ppermute | solution.py:59
  146.5 6.2 %collective-permute-start.30 = (f32[8,512]{1,0:T(8,128)S(1)}, f32[8,512]{1,0:T(8,128)S(1)}, u32[]{:S(2)}, u32[]{:S(2)}) collective-permute-start(f32[8,512]{1,0:T(8,128)S(1)} %add.47), channel_id=1, source_target_pairs={{0,2},{2,0},{4,6},{6,4},{1,3},{3,1},{5,7},{7,5},{8,10},{10,8},{12,... | collective-permute-start | bytes 49160 | tf_op jit(solution)/shard_map/ppermute | solution.py:59
  152.7 5.3 %collective-permute-start.34 = (f32[8,512]{1,0:T(8,128)S(1)}, f32[8,512]{1,0:T(8,128)S(1)}, u32[]{:S(2)}, u32[]{:S(2)}) collective-permute-start(f32[8,512]{1,0:T(8,128)S(1)} %add.48), channel_id=1, source_target_pairs={{0,4},{2,6},{4,0},{6,2},{1,5},{3,7},{5,1},{7,3},{8,12},{10,14},{12... | collective-permute-start | bytes 49160 | tf_op jit(solution)/shard_map/ppermute | solution.py:59

commit v3 on v2

--- a/solution.py
+++ b/solution.py
@@ -19,8 +19,8 @@
 UNIT = 1572864
 PATTERNS = 192
 TILES = 240
-PARTS = 6
-GROUP = (4, 4, 4, 4, 4, 4)
+PARTS = 5
+GROUP = (4, 4, 4, 4, 4)
 KEYS = PARTS * BPD
 SLOTS = TILES + sum(BPD * (g - 1) + 2 * g for g in GROUP) // 16 * 16 + 16
 STARTS = SLOTS + SLOTS // 2
@@ -62,10 +62,9 @@
 OWNERS = (
     ((0, 1), (0, 3)),
     ((1, 0), (1, 1), (1, 3), (0, 2)),
-    ((3, 0), (3, 1), (3, 3)),
+    ((3, 0), (3, 1), (3, 3), (1, 2), (3, 2)),
     ((2, 0), (2, 1)),
     ((2, 3), (2, 2)),
-    ((1, 2), (3, 2)),
 )
 
 
@@ -252,21 +251,18 @@
     rows = sum(t[pl.ds(OWN_ROWS, 16), :].astype(jnp.float32) for _, t in tables)
     sums = jnp.sum(rows, axis=0, keepdims=True)
     line[...] = jnp.broadcast_to(sums, (8, C))
+    for out in (out1, out3):
+        out[pl.ds(CAP * BLOCK, 16), :] = sum_rows(sums)
 
 
 def pick_late(asked, wanted, own, far1, far3, low2, high2):
     b16 = jnp.bfloat16
     piece = jax.ShapeDtypeStruct((CAP * BLOCK, C), b16)
+    with_sums = jax.ShapeDtypeStruct((CAP * BLOCK + 16, C), b16)
+    double = jax.ShapeDtypeStruct((2 * CAP * BLOCK, C), b16)
     return pl.pallas_call(
         pick_late_kernel,
-        out_shape=(
-            piece,
-            piece,
-            piece,
-            jax.ShapeDtypeStruct((2 * CAP * BLOCK, C), b16),
-            jax.ShapeDtypeStruct((2 * CAP * BLOCK, C), b16),
-            jax.ShapeDtypeStruct((8, C), jnp.float32),
-        ),
+        out_shape=(piece, with_sums, with_sums, double, double, jax.ShapeDtypeStruct((8, C), jnp.float32)),
         in_specs=[SMEM] * 2 + [VMEM] * 5,
         out_specs=(VMEM,) * 6,
         scratch_shapes=[pltpu.VMEM((SENT_ROWS, C), b16)],
@@ -283,8 +279,8 @@
     if resume:
         earlier = refs.pop(0)
     if finish:
-        current, all_sums, fresh = refs[:3]
-        refs = refs[3:]
+        current, chain, cross, fresh = refs[:4]
+        refs = refs[4:]
         if finish == "more":
             sent = refs.pop(0)
     if finish == "end":
@@ -302,8 +298,9 @@
         held = refs[4]
         at = 0
         for table in tables:
-            held[pl.ds(at, table.shape[0]), :] = table[...]
-            at += table.shape[0]
+            rows = table.shape[0] // BLOCK * BLOCK
+            held[pl.ds(at, rows), :] = table[pl.ds(0, rows), :]
+            at += rows
 
     def rows_of(index):
         return pl.ds(pl.multiple_of(index * BLOCK, BLOCK), BLOCK)
@@ -366,7 +363,7 @@
 
     if not finish:
         return
-    col_sums = all_sums[0:1, :]
+    col_sums = chain[0:1, :] + cross[4:5, :]
     moved_sums = jnp.zeros((8, C), jnp.float32)
     copies = []
     for j in range(BPD):
@@ -386,7 +383,7 @@
         copy.wait()
 
 
-def run_tiles(name, part, lists, words, own, tables, earlier=None, current=None, sums=None, finish=""):
+def run_tiles(name, part, lists, words, own, tables, earlier=None, current=None, sums=(), finish=""):
     f32 = jnp.float32
     blocks = jax.ShapeDtypeStruct((OWN_ROWS, C), f32)
     args = [lists, words, own, *tables]
@@ -397,8 +394,8 @@
         args.append(earlier)
         specs.append(VMEM)
     if finish:
-        args += [current, sums]
-        specs += [VMEM] * 2
+        args += [current, *sums]
+        specs += [VMEM] * 3
         if finish == "end":
             scratch += [pltpu.VMEM((OWN_ROWS, C), f32), pltpu.SemaphoreType.DMA((BPD,))]
         scratch.append(pltpu.VMEM((OWN_ROWS, C), f32))
@@ -422,6 +419,12 @@
     )(*args)
 
 
+def line_sums(line, side1, side3):
+    rows = sum(t[CAP * BLOCK :].astype(jnp.float32) for t in (side1, side3))
+    beside = jnp.sum(rows, axis=0, keepdims=True)
+    return line + jnp.where(jnp.arange(8)[:, None] < 4, beside, 0.0)
+
+
 def per_device(affiliations, tile_block, tile_target, tile_pattern, tile_count, block_home, patterns):
     y, x = lax.axis_index("rows_0"), lax.axis_index("rows_1")
     core = lax.axis_index("cols_1")
@@ -443,30 +446,27 @@
         side1, side3 = fetch(out1, 0, 1), fetch(out3, 0, 3)
         (total,) = run_tiles("near", 0, lists, words, own, (near,))
         total, low2, high2 = lax.optimization_barrier((total, low2, high2))
-        near, out1, out3, out2a, out2b, line = pick_late(asked, requests[0], own, far1, far3, low2, high2)
-        lines = tuple(fetch(line, 0, m) for m in (1, 3, 2))
-        lines, out2a, out2b, side1, side3 = lax.optimization_barrier(
-            (lines, out2a, out2b, side1, side3)
+        near, out1, out3, *out2, line = pick_late(
+            asked, requests[0], own, far1, far3, low2, high2
         )
-        side2a, side2b = fetch(out2a, 0, 2), fetch(out2b, 0, 2)
         late1, late3 = fetch(out1, 0, 1), fetch(out3, 0, 3)
-        sums = line + lines[0] + lines[1] + lines[2]
+        out2, side1, side3 = lax.optimization_barrier((out2, side1, side3))
+        side2 = [fetch(piece, 0, 2) for piece in out2]
+        (total,) = run_tiles("sides_1", 1, lists, words, own, (side1, near), total)
+        total, late1, late3 = lax.optimization_barrier((total, late1, late3))
+        sums = line_sums(line, late1, late3)
         other = swap(sums, "cols_1", 1)
-        (total,) = run_tiles("sides_1", 1, lists, words, own, (side1, near), total)
+        (total,) = run_tiles("sides_3", 2, lists, words, own, (side3, late1, late3), total)
         total, other = lax.optimization_barrier((total, other))
         sums = sums + other
-        other = swap(sums, "cols_0", 1)
-        (total,) = run_tiles("sides_3", 2, lists, words, own, (side3,), total)
-        total, other = lax.optimization_barrier((total, other))
-        sums = sums + other
-        col_sums = sums + swap(sums, "cols_0", 2)
-        (total,) = run_tiles("across", 3, lists, words, own, (side2a,), total)
-        total, side2b = lax.optimization_barrier((total, side2b))
-        (total,) = run_tiles("across_more", 4, lists, words, own, (side2b,), total)
-        total, late1, late3 = lax.optimization_barrier((total, late1, late3))
+        sums = sums + swap(sums, "cols_0", 1)
+        sums = sums + swap(sums, "cols_0", 2)
+        cross = fetch(sums, 2, 2)
+        (total,) = run_tiles("across", 3, lists, words, own, side2[:1], total)
+        total, last = lax.optimization_barrier((total, side2[1:]))
         finish = "more" if step < STEPS - 1 else "end"
         current, *own_next = run_tiles(
-            "late", 5, lists, words, own, (late1, late3), total, current, col_sums, finish
+            "late", 4, lists, words, own, last, total, current, (sums, cross), finish
         )
         if own_next:
             (own,) = own_next

time: 172 us -> 204 us (1.19); the launches traced: 173 us -> 200 us
  waiting for transfers between devices: 47.5 us -> 103 us
  Pallas kernels: 81.1 us -> 45.9 us
  starting transfers between devices: 41.4 us -> 47.8 us
    ppermute x29 -> x25, waiting for transfers between devices: 37 us -> 94.5 us  [fetch(): return lax.ppermute(value, ALL, pairs(first, second))]
    pallas_call x12 -> x10, Pallas kernels: 64.5 us -> 35.8 us  [run_tiles(): pl.pallas_call(functools.partial(tile_kernel, part, len(tables), earlier...]
    ppermute x6, starting transfers between devices: 0.43 us -> 11.8 us  [swap(): lax.ppermute(value, axis, [(i, i ^ step) for i in range(lax.axis_size(axi...]
    ppermute x29 -> x25, starting transfers between devices: 40.9 us -> 36 us  [fetch(): return lax.ppermute(value, ALL, pairs(first, second))]
    pallas_call x1, Pallas kernels: 6.57 us -> 3.07 us  [ask(): pl.pallas_call(ask_kernel, out_shape=(jax.ShapeDtypeStruct((64,), i32), j...]
    pallas_call x1, Pallas kernels: 6.33 us -> 3.36 us  [sort_tiles(): pl.pallas_call(sort_kernel, out_shape=jax.ShapeDtypeStruct((LIST,), i32),...]
  transfers between devices with their start and end apart: 35 -> 31, of which waited for: 14 -> 22; matrix products, arithmetic and copies ran while one was open for 0% -> 0% of each run, Pallas kernels for 39% -> 18%
where the time goes in v3:
time: 204 us; the launch traced here: 200 us
  waiting for transfers between devices  103 us (50%)
  starting transfers between devices  47.8 us (23%)
  Pallas kernels  45.9 us (22%)
  local copies, waits for them, and re-layouts  2.05 us (1%)
    ppermute x25, waiting for transfers between devices, fetch(): return lax.ppermute(value, ALL, pairs(first, second))  94.5 us
    ppermute x25, starting transfers between devices, fetch(): return lax.ppermute(value, ALL, pairs(first, second))  36 us
    pallas_call x10, Pallas kernels, run_tiles(): pl.pallas_call(functools.partial(tile_kernel, part, len(tables), earlier...  35.8 us
    ppermute x6, starting transfers between devices, swap(): lax.ppermute(value, axis, [(i, i ^ step) for i in range(lax.axis_size(axi...  11.8 us
    ppermute x6, waiting for transfers between devices, swap(): lax.ppermute(value, axis, [(i, i ^ step) for i in range(lax.axis_size(axi...  8.68 us
  transfers between devices with their start and end apart: 31, of which 22 were waited for; matrix products, arithmetic and copies ran while one was open for 0% of the time, Pallas kernels for 18%

profile of v3, /device:TPU:32, one launch (start us, length us, event | category | flops | bytes accessed | tf_op | source)
XLA Modules:
  0.0 200.5 jit_solution(5377596682363713802)
XLA Ops:
  0.0 1.6 copy-done
  1.7 1.6 collective-permute-start.4
  3.3 1.7 collective-permute-start.3
  5.8 3.1 %ask.1 = (s32[64]{0:T(128)S(1)}, s32[240]{0:T(256)S(1)}) custom-call(s32[3]{0:T(128)S(1)} %pad_add_fusion.1.place, s32[240]{0:T(256)S(1)} %bitcast.9, s32[240]{0:T(256)S(1)} %bitcast.10, s32[1]{0:T(128)S(6)} %copy.9.count, s32[1024]{0:T(1024)S(1)} %copy-done.2), custom_call_target="tpu_custom_call" | custom-call | tf_op jit(solution)/shard_map/ask/pallas_call | solution.py:114
  8.9 3.2 %collective-permute-start.2 = (s32[16]{0:T(128)S(1)}, s32[16]{0:T(128)S(1)}, u32[]{:S(2)}, u32[]{:S(2)}) collective-permute-start(s32[16]{0:T(128)S(1)} %get-tuple-element.114), channel_id=1, source_target_pairs={{32,0},{9,1},{34,2},{11,3},{36,4},{13,5},{38,6},{15,7},{40,8},{17,... | collective-permute-start | bytes 200 | tf_op jit(solution)/shard_map/ppermute | solution.py:55
  12.1 0.8 collective-permute-start.1
  12.9 1.3 collective-permute-start
  14.2 3.0 %collective-permute-done.1 = s32[16]{0:T(128)S(1)} collective-permute-done((s32[16]{0:T(128)S(1)}, s32[16]{0:T(128)S(1)}, u32[]{:S(2)}, u32[]{:S(2)}) %collective-permute-start.1) | collective-permute-done | bytes 96 | tf_op jit(solution)/shard_map/ppermute | solution.py:55
  17.2 0.4 collective-permute-done
  17.7 0.3 collective-permute-done.4.far3
  18.3 0.9 pick_early.2
  19.2 3.1 %collective-permute-start.7 = (bf16[1536,512]{1,0:T(8,128)(2,1)S(1)}, bf16[1536,512]{1,0:T(8,128)(2,1)S(1)}, u32[]{:S(2)}, u32[]{:S(2)}) collective-permute-start(bf16[1536,512]{1,0:T(8,128)(2,1)S(1)} %get-tuple-element.68), channel_id=1, source_target_pairs={{32,0},{9,1},{34,2},{11,3},{36,4},{13,5},{38,6},{15,7},{40,8},{17,... | collective-permute-start | bytes 4718600 | tf_op jit(solution)/shard_map/ppermute | solution.py:55
  22.3 1.5 collective-permute-start.6
  23.8 1.7 collective-permute-start.5
  25.5 0.3 copy.8
  25.9 3.4 %sort_tiles.1.refs_0_ = s32[632]{0:T(1024)S(1)} custom-call(s32[240]{0:T(256)S(1)} %get-tuple-element.59.codes, s32[240]{0:T(256)S(1)} %bitcast.11, s32[1]{0:T(128)S(6)} %copy.9.count), custom_call_target="tpu_custom_call" | custom-call | tf_op jit(solution)/shard_map/sort_tiles/pallas_call | solution.py:162
  29.3 3.4 %near.2.refs_5_ = f32[1024,512]{1,0:T(8,128)S(1)} custom-call(s32[632]{0:T(1024)S(1)} %sort_tiles.1.refs_0_, s32[193,5,128]{2,1,0:T(8,128)S(1)} %concatenate.3.refs_1_, bf16[1040,512]{1,0:T(8,128)(2,1)S(1)} %first.1.own.refs_2_, bf16[1024,512]{1,0:T(8,128)(2,1)S(1)} %get-tuple-element.61.refs_3_), custom_call_target="tpu_custom_call" | custom-call | tf_op jit(solution)/shard_map/near/pallas_call | solution.py:411
  32.7 6.0 %collective-permute-done.5.low2 = bf16[512,512]{1,0:T(8,128)(2,1)S(1)} collective-permute-done((bf16[512,512]{1,0:T(8,128)(2,1)S(1)}, bf16[512,512]{1,0:T(8,128)(2,1)S(1)}, u32[]{:S(2)}, u32[]{:S(2)}) %collective-permute-start.5) | collective-permute-done | bytes 524320 | tf_op jit(solution)/shard_map/ppermute | solution.py:55
  38.7 0.9 pick_late.2
  39.6 3.3 %collective-permute-start.10 = (bf16[528,512]{1,0:T(8,128)(2,1)S(1)}, bf16[528,512]{1,0:T(8,128)(2,1)S(1)}, u32[]{:S(2)}, u32[]{:S(2)}) collective-permute-start(bf16[528,512]{1,0:T(8,128)(2,1)S(1)} %get-tuple-element.75), channel_id=1, source_target_pairs={{32,0},{9,1},{34,2},{11,3},{36,4},{13,5},{38,6},{15,7},{40,8},{17,... | collective-permute-start | bytes 1622024 | tf_op jit(solution)/shard_map/ppermute | solution.py:55
  42.9 2.9 %collective-permute-done.7.refs_3_ = bf16[1536,512]{1,0:T(8,128)(2,1)S(1)} collective-permute-done((bf16[1536,512]{1,0:T(8,128)(2,1)S(1)}, bf16[1536,512]{1,0:T(8,128)(2,1)S(1)}, u32[]{:S(2)}, u32[]{:S(2)}) %collective-permute-start.7) | collective-permute-done | bytes 1572896 | tf_op jit(solution)/shard_map/ppermute | solution.py:55
  45.8 1.2 collective-permute-done.8.refs_3_
  47.1 1.6 collective-permute-start.9
  48.7 1.9 collective-permute-start.13
  50.6 3.5 %sides_1.2.refs_6_ = f32[1024,512]{1,0:T(8,128)S(1)} custom-call(s32[632]{0:T(1024)S(1)} %sort_tiles.1.refs_0_, s32[193,5,128]{2,1,0:T(8,128)S(1)} %concatenate.3.refs_1_, bf16[1040,512]{1,0:T(8,128)(2,1)S(1)} %first.1.own.refs_2_, bf16[1536,512]{1,0:T(8,128)(2,1)S(1)} %collective-permute-done.7.refs_3_, bf16[512,512]{1,0:T(8,128)(2,1)S(1)} %get-tuple-element.73.refs_4_, ...), custom_call_target="tpu_custom_call" | custom-call | tf_op jit(solution)/shard_map/sides_1/pallas_call | solution.py:411
  54.1 20.0 %collective-permute-done.10.refs_4_ = bf16[528,512]{1,0:T(8,128)(2,1)S(1)} collective-permute-done((bf16[528,512]{1,0:T(8,128)(2,1)S(1)}, bf16[528,512]{1,0:T(8,128)(2,1)S(1)}, u32[]{:S(2)}, u32[]{:S(2)}) %collective-permute-start.10) | collective-permute-done | bytes 540704 | tf_op jit(solution)/shard_map/ppermute | solution.py:55
  74.2 1.2 collective-permute-start.12
  75.5 3.5 %sides_3.2.refs_4_ = f32[1024,512]{1,0:T(8,128)S(1)} custom-call(s32[632]{0:T(1024)S(1)} %sort_tiles.1.refs_0_, s32[193,5,128]{2,1,0:T(8,128)S(1)} %concatenate.3.refs_1_, bf16[1040,512]{1,0:T(8,128)(2,1)S(1)} %first.1.own.refs_2_, bf16[1536,512]{1,0:T(8,128)(2,1)S(1)} %collective-permute-done.8.refs_3_, ...), custom_call_target="tpu_custom_call" | custom-call | tf_op jit(solution)/shard_map/sides_3/pallas_call | solution.py:411
  79.1 0.7 collective-permute-start.14
  79.8 3.0 %collective-permute-done.14 = f32[8,512]{1,0:T(8,128)S(1)} collective-permute-done((f32[8,512]{1,0:T(8,128)S(1)}, f32[8,512]{1,0:T(8,128)S(1)}, u32[]{:S(2)}, u32[]{:S(2)}) %collective-permute-start.14) | collective-permute-done | bytes 16416 | tf_op jit(solution)/shard_map/ppermute | solution.py:59
  82.9 3.6 %collective-permute-start.15 = (f32[8,512]{1,0:T(8,128)S(1)}, f32[8,512]{1,0:T(8,128)S(1)}, u32[]{:S(2)}, u32[]{:S(2)}) collective-permute-start(f32[8,512]{1,0:T(8,128)S(1)} %add.35), channel_id=1, source_target_pairs={{0,4},{2,6},{4,0},{6,2},{1,5},{3,7},{5,1},{7,3},{8,12},{10,14},{12... | collective-permute-start | bytes 49160 | tf_op jit(solution)/shard_map/ppermute | solution.py:59
  86.5 1.7 collective-permute-done.15
  88.2 3.5 %across.2.refs_4_ = f32[1024,512]{1,0:T(8,128)S(1)} custom-call(s32[632]{0:T(1024)S(1)} %sort_tiles.1.refs_0_, s32[193,5,128]{2,1,0:T(8,128)S(1)} %concatenate.3.refs_1_, bf16[1040,512]{1,0:T(8,128)(2,1)S(1)} %first.1.own.refs_2_, bf16[1024,512]{1,0:T(8,128)(2,1)S(1)} %collective-permute-done.9.refs_3_, f32[1024,512]{1,0:T(8,128)S(1)} %sides_3.2.refs_4_), custom_call_target="tpu_custom_call" | custom-call | tf_op jit(solution)/shard_map/across/pallas_call | solution.py:411
  91.7 4.1 %collective-permute-done.16.refs_7_ = f32[8,512]{1,0:T(8,128)S(1)} collective-permute-done((f32[8,512]{1,0:T(8,128)S(1)}, f32[8,512]{1,0:T(8,128)S(1)}, u32[]{:S(2)}, u32[]{:S(2)}) %collective-permute-start.16) | collective-permute-done | bytes 16416 | tf_op jit(solution)/shard_map/ppermute | solution.py:55
  95.8 3.6 %late.2 = (f32[1024,512]{1,0:T(8,128)S(1)}, bf16[1040,512]{1,0:T(8,128)(2,1)S(1)}) custom-call(s32[632]{0:T(1024)S(1)} %sort_tiles.1.refs_0_, s32[193,5,128]{2,1,0:T(8,128)S(1)} %concatenate.3.refs_1_, bf16[1040,512]{1,0:T(8,128)(2,1)S(1)} %first.1.own.refs_2_, bf16[1024,512]{1,0:T(8,128)(2,1)S(1)} %collective-permute-done.13.refs_3_, ...), custom_call_target="tpu_custom_call" | custom-call | tf_op jit(solution)/shard_map/late/pallas_call | solution.py:411
  99.4 2.5 %collective-permute-start.18 = (bf16[1040,512]{1,0:T(8,128)(2,1)S(1)}, bf16[1040,512]{1,0:T(8,128)(2,1)S(1)}, u32[]{:S(2)}, u32[]{:S(2)}) collective-permute-start(bf16[1040,512]{1,0:T(8,128)(2,1)S(1)} %get-tuple-element.86.own.refs_2_), channel_id=1, source_target_pairs={{24,0},{97,1},{26,2},{99,3},{28,4},{101,5},{30,6},{103,7},{0,8},{1... | collective-permute-start | bytes 3194888 | tf_op jit(solution)/shard_map/ppermute | solution.py:55
  101.9 0.8 collective-permute-start.17
  102.7 12.9 %collective-permute-done.18.far3 = bf16[1040,512]{1,0:T(8,128)(2,1)S(1)} collective-permute-done((bf16[1040,512]{1,0:T(8,128)(2,1)S(1)}, bf16[1040,512]{1,0:T(8,128)(2,1)S(1)}, u32[]{:S(2)}, u32[]{:S(2)}) %collective-permute-start.18) | collective-permute-done | bytes 1064992 | tf_op jit(solution)/shard_map/ppermute | solution.py:55
  115.6 3.3 %collective-permute-done.17.far1 = bf16[1040,512]{1,0:T(8,128)(2,1)S(1)} collective-permute-done((bf16[1040,512]{1,0:T(8,128)(2,1)S(1)}, bf16[1040,512]{1,0:T(8,128)(2,1)S(1)}, u32[]{:S(2)}, u32[]{:S(2)}) %collective-permute-start.17) | collective-permute-done | bytes 1064992 | tf_op jit(solution)/shard_map/ppermute | solution.py:55
  118.9 0.9 pick_early.3
  119.8 0.7 collective-permute-start.21
  120.5 1.4 collective-permute-start.22
  121.9 2.3 %collective-permute-start.20 = (bf16[528,512]{1,0:T(8,128)(2,1)S(1)}, bf16[528,512]{1,0:T(8,128)(2,1)S(1)}, u32[]{:S(2)}, u32[]{:S(2)}) collective-permute-start(bf16[528,512]{1,0:T(8,128)(2,1)S(1)} %get-tuple-element.89), channel_id=1, source_target_pairs={{24,0},{97,1},{26,2},{99,3},{28,4},{101,5},{30,6},{103,7},{0,8},{1... | collective-permute-start | bytes 1622024 | tf_op jit(solution)/shard_map/ppermute | solution.py:55
  124.2 0.9 collective-permute-start.19
  125.2 3.4 %near.3.refs_5_ = f32[1024,512]{1,0:T(8,128)S(1)} custom-call(s32[632]{0:T(1024)S(1)} %sort_tiles.1.refs_0_, s32[193,5,128]{2,1,0:T(8,128)S(1)} %concatenate.3.refs_1_, bf16[1040,512]{1,0:T(8,128)(2,1)S(1)} %get-tuple-element.86.own.refs_2_, bf16[1024,512]{1,0:T(8,128)(2,1)S(1)} %get-tuple-element.87.refs_3_), custom_call_target="tpu_custom_call" | custom-call | tf_op jit(solution)/shard_map/near/pallas_call | solution.py:411
  128.6 10.5 %collective-permute-done.19.low2 = bf16[512,512]{1,0:T(8,128)(2,1)S(1)} collective-permute-done((bf16[512,512]{1,0:T(8,128)(2,1)S(1)}, bf16[512,512]{1,0:T(8,128)(2,1)S(1)}, u32[]{:S(2)}, u32[]{:S(2)}) %collective-permute-start.19) | collective-permute-done | bytes 524320 | tf_op jit(solution)/shard_map/ppermute | solution.py:55
  139.1 0.9 pick_late.3
  140.0 1.4 collective-permute-start.24
  141.4 0.7 collective-permute-start.25
  142.1 1.0 collective-permute-done.21.refs_3_
  143.1 0.9 collective-permute-done.22.refs_3_
  144.0 1.8 collective-permute-start.23
  145.8 1.7 collective-permute-start.27
  147.5 3.5 %sides_1.3.refs_6_ = f32[1024,512]{1,0:T(8,128)S(1)} custom-call(s32[632]{0:T(1024)S(1)} %sort_tiles.1.refs_0_, s32[193,5,128]{2,1,0:T(8,128)S(1)} %concatenate.3.refs_1_, bf16[1040,512]{1,0:T(8,128)(2,1)S(1)} %get-tuple-element.86.own.refs_2_, bf16[1536,512]{1,0:T(8,128)(2,1)S(1)} %collective-permute-done.21.refs_3_, ...), custom_call_target="tpu_custom_call" | custom-call | tf_op jit(solution)/shard_map/sides_1/pallas_call | solution.py:411
  151.1 20.3 %collective-permute-done.24.refs_4_ = bf16[528,512]{1,0:T(8,128)(2,1)S(1)} collective-permute-done((bf16[528,512]{1,0:T(8,128)(2,1)S(1)}, bf16[528,512]{1,0:T(8,128)(2,1)S(1)}, u32[]{:S(2)}, u32[]{:S(2)}) %collective-permute-start.24) | collective-permute-done | bytes 540704 | tf_op jit(solution)/shard_map/ppermute | solution.py:55
  171.4 3.0 %collective-permute-done.25.refs_5_ = bf16[528,512]{1,0:T(8,128)(2,1)S(1)} collective-permute-done((bf16[528,512]{1,0:T(8,128)(2,1)S(1)}, bf16[528,512]{1,0:T(8,128)(2,1)S(1)}, u32[]{:S(2)}, u32[]{:S(2)}) %collective-permute-start.25) | collective-permute-done | bytes 540704 | tf_op jit(solution)/shard_map/ppermute | solution.py:55
  174.5 3.6 %sides_3.3.refs_4_ = f32[1024,512]{1,0:T(8,128)S(1)} custom-call(s32[632]{0:T(1024)S(1)} %sort_tiles.1.refs_0_, s32[193,5,128]{2,1,0:T(8,128)S(1)} %concatenate.3.refs_1_, bf16[1040,512]{1,0:T(8,128)(2,1)S(1)} %get-tuple-element.86.own.refs_2_, bf16[1536,512]{1,0:T(8,128)(2,1)S(1)} %collective-permute-done.22.refs_3_, ...), custom_call_target="tpu_custom_call" | custom-call | tf_op jit(solution)/shard_map/sides_3/pallas_call | solution.py:411
  178.2 3.2 %collective-permute-start.28 = (f32[8,512]{1,0:T(8,128)S(1)}, f32[8,512]{1,0:T(8,128)S(1)}, u32[]{:S(2)}, u32[]{:S(2)}) collective-permute-start(f32[8,512]{1,0:T(8,128)S(1)} %fusion.1), channel_id=1, source_target_pairs={{0,2},{2,0},{4,6},{6,4},{1,3},{3,1},{5,7},{7,5},{8,10},{10,8},{12,... | collective-permute-start | bytes 49160 | tf_op jit(solution)/shard_map/ppermute | solution.py:59
  181.4 1.7 collective-permute-done.28
  183.1 3.0 %collective-permute-start.29 = (f32[8,512]{1,0:T(8,128)S(1)}, f32[8,512]{1,0:T(8,128)S(1)}, u32[]{:S(2)}, u32[]{:S(2)}) collective-permute-start(f32[8,512]{1,0:T(8,128)S(1)} %add.40), channel_id=1, source_target_pairs={{0,4},{2,6},{4,0},{6,2},{1,5},{3,7},{5,1},{7,3},{8,12},{10,14},{12... | collective-permute-start | bytes 49160 | tf_op jit(solution)/shard_map/ppermute | solution.py:59
  186.1 2.2 %collective-permute-done.29 = f32[8,512]{1,0:T(8,128)S(1)} collective-permute-done((f32[8,512]{1,0:T(8,128)S(1)}, f32[8,512]{1,0:T(8,128)S(1)}, u32[]{:S(2)}, u32[]{:S(2)}) %collective-permute-start.29) | collective-permute-done | bytes 16416 | tf_op jit(solution)/shard_map/ppermute | solution.py:59
  188.3 3.4 %across.3.refs_4_ = f32[1024,512]{1,0:T(8,128)S(1)} custom-call(s32[632]{0:T(1024)S(1)} %sort_tiles.1.refs_0_, s32[193,5,128]{2,1,0:T(8,128)S(1)} %concatenate.3.refs_1_, bf16[1040,512]{1,0:T(8,128)(2,1)S(1)} %get-tuple-element.86.own.refs_2_, bf16[1024,512]{1,0:T(8,128)(2,1)S(1)} %collective-permute-done.23.refs_3_, f32[1024,512]{1,0:T(8,128)S(1)} %sides_3.3.refs_4_), custom_call_target="tpu_custom_call" | custom-call | tf_op jit(solution)/shard_map/across/pallas_call | solution.py:411
  191.7 4.2 %collective-permute-done.30.refs_7_ = f32[8,512]{1,0:T(8,128)S(1)} collective-permute-done((f32[8,512]{1,0:T(8,128)S(1)}, f32[8,512]{1,0:T(8,128)S(1)}, u32[]{:S(2)}, u32[]{:S(2)}) %collective-permute-start.30) | collective-permute-done | bytes 16416 | tf_op jit(solution)/shard_map/ppermute | solution.py:55
  196.0 4.4 %late.3 = f32[1024,512]{1,0:T(8,128)} custom-call(s32[632]{0:T(1024)S(1)} %sort_tiles.1.refs_0_, s32[193,5,128]{2,1,0:T(8,128)S(1)} %concatenate.3.refs_1_, bf16[1040,512]{1,0:T(8,128)(2,1)S(1)} %get-tuple-element.86.own.refs_2_, bf16[1024,512]{1,0:T(8,128)(2,1)S(1)} %collective-permute-done.27.refs_3_, f32[1024,512]{1,0:T(8,128)S(1)} %across.3.refs_4_, ...), custom_call_target="tpu_custom_call" | custom-call | tf_op jit(solution)/shard_map/late/pallas_call | solution.py:411
  (45 shorter events, 1.1 us)
Async XLA Ops:
  0.0 1.6 copy-start
  1.6 4.2 %copy-start.2 = (s32[1024]{0:T(1024)S(1)}, s32[1024]{0:T(1024)}, u32[]{:S(2)}) copy-start(s32[1024]{0:T(1024)} %home.1) | copy-start | bytes 12292
  1.6 4.2 %copy-start.3 = (s32[1,240]{1,0:T(1,128)S(1)}, s32[1,240]{1,0:T(1,128)}, u32[]{:S(2)}) copy-start(s32[1,240]{1,0:T(1,128)} %param.8) | copy-start | bytes 2884
  1.6 4.2 %copy-start.4 = (s32[1,240]{1,0:T(1,128)S(1)}, s32[1,240]{1,0:T(1,128)}, u32[]{:S(2)}) copy-start(s32[1,240]{1,0:T(1,128)} %param.9) | copy-start | bytes 2884
  1.7 16.3 %collective-permute-start.4 = (bf16[1040,512]{1,0:T(8,128)(2,1)S(1)}, bf16[1040,512]{1,0:T(8,128)(2,1)S(1)}, u32[]{:S(2)}, u32[]{:S(2)}) collective-permute-start(bf16[1040,512]{1,0:T(8,128)(2,1)S(1)} %first.1.own.refs_2_), channel_id=1, source_target_pairs={{24,0},{97,1},{26,2},{99,3},{28,4},{101,5},{30,6},{103,7},{0,8},{1... | collective-permute-start | bytes 3194888 | tf_op jit(solution)/shard_map/ppermute | solution.py:55
  3.3 15.0 %collective-permute-start.3 = (bf16[1040,512]{1,0:T(8,128)(2,1)S(1)}, bf16[1040,512]{1,0:T(8,128)(2,1)S(1)}, u32[]{:S(2)}, u32[]{:S(2)}) collective-permute-start(bf16[1040,512]{1,0:T(8,128)(2,1)S(1)} %first.1.own.refs_2_), channel_id=1, source_target_pairs={{8,0},{33,1},{10,2},{35,3},{12,4},{37,5},{14,6},{39,7},{16,8},{41,... | collective-permute-start | bytes 3194888 | tf_op jit(solution)/shard_map/ppermute | solution.py:55
  8.9 5.3 %collective-permute-start.2 = (s32[16]{0:T(128)S(1)}, s32[16]{0:T(128)S(1)}, u32[]{:S(2)}, u32[]{:S(2)}) collective-permute-start(s32[16]{0:T(128)S(1)} %get-tuple-element.114), channel_id=1, source_target_pairs={{32,0},{9,1},{34,2},{11,3},{36,4},{13,5},{38,6},{15,7},{40,8},{17,... | collective-permute-start | bytes 200 | tf_op jit(solution)/shard_map/ppermute | solution.py:55
  12.1 5.1 %collective-permute-start.1 = (s32[16]{0:T(128)S(1)}, s32[16]{0:T(128)S(1)}, u32[]{:S(2)}, u32[]{:S(2)}) collective-permute-start(s32[16]{0:T(128)S(1)} %get-tuple-element.115), channel_id=1, source_target_pairs={{64,0},{17,1},{66,2},{19,3},{68,4},{21,5},{70,6},{23,7},{72,8},{25... | collective-permute-start | bytes 200 | tf_op jit(solution)/shard_map/ppermute | solution.py:55
  12.9 4.8 %collective-permute-start = (s32[16]{0:T(128)S(1)}, s32[16]{0:T(128)S(1)}, u32[]{:S(2)}, u32[]{:S(2)}) collective-permute-start(s32[16]{0:T(128)S(1)} %get-tuple-element.116), channel_id=1, source_target_pairs={{96,0},{25,1},{98,2},{27,3},{100,4},{29,5},{102,6},{31,7},{104,8},... | collective-permute-start | bytes 200 | tf_op jit(solution)/shard_map/ppermute | solution.py:55
  18.3 7.3 %copy-start.6 = (s32[192,5,128]{2,0,1:T(8,128)S(1)}, s32[192,5,128]{2,0,1:T(8,128)}, u32[]{:S(2)}) copy-start(s32[192,5,128]{2,0,1:T(8,128)} %param.13) | copy-start | bytes 1474564
  19.2 6.7 %copy-start.5 = (s32[1,240]{1,0:T(1,128)S(1)}, s32[1,240]{1,0:T(1,128)}, u32[]{:S(2)}) copy-start(s32[1,240]{1,0:T(1,128)} %param.10) | copy-start | bytes 2884
  19.2 26.6 %collective-permute-start.7 = (bf16[1536,512]{1,0:T(8,128)(2,1)S(1)}, bf16[1536,512]{1,0:T(8,128)(2,1)S(1)}, u32[]{:S(2)}, u32[]{:S(2)}) collective-permute-start(bf16[1536,512]{1,0:T(8,128)(2,1)S(1)} %get-tuple-element.68), channel_id=1, source_target_pairs={{32,0},{9,1},{34,2},{11,3},{36,4},{13,5},{38,6},{15,7},{40,8},{17,... | collective-permute-start | bytes 4718600 | tf_op jit(solution)/shard_map/ppermute | solution.py:55
  22.3 24.8 %collective-permute-start.8 = (bf16[1536,512]{1,0:T(8,128)(2,1)S(1)}, bf16[1536,512]{1,0:T(8,128)(2,1)S(1)}, u32[]{:S(2)}, u32[]{:S(2)}) collective-permute-start(bf16[1536,512]{1,0:T(8,128)(2,1)S(1)} %get-tuple-element.69), channel_id=1, source_target_pairs={{96,0},{25,1},{98,2},{27,3},{100,4},{29,5},{102,6},{31,7},{104,8},... | collective-permute-start | bytes 4718600 | tf_op jit(solution)/shard_map/ppermute | solution.py:55
  22.3 16.4 %collective-permute-start.6 = (bf16[528,512]{1,0:T(8,128)(2,1)S(1)}, bf16[528,512]{1,0:T(8,128)(2,1)S(1)}, u32[]{:S(2)}, u32[]{:S(2)}) collective-permute-start(bf16[528,512]{1,0:T(8,128)(2,1)S(1)} %get-tuple-element.63), channel_id=1, source_target_pairs={{24,0},{97,1},{26,2},{99,3},{28,4},{101,5},{30,6},{103,7},{0,8},{1... | collective-permute-start | bytes 1622024 | tf_op jit(solution)/shard_map/ppermute | solution.py:55
  23.8 14.9 %collective-permute-start.5 = (bf16[512,512]{1,0:T(8,128)(2,1)S(1)}, bf16[512,512]{1,0:T(8,128)(2,1)S(1)}, u32[]{:S(2)}, u32[]{:S(2)}) collective-permute-start(bf16[512,512]{1,0:T(8,128)(2,1)S(1)} %get-tuple-element.62), channel_id=1, source_target_pairs={{8,0},{33,1},{10,2},{35,3},{12,4},{37,5},{14,6},{39,7},{16,8},{41,... | collective-permute-start | bytes 1572872 | tf_op jit(solution)/shard_map/ppermute | solution.py:55
  39.6 34.5 %collective-permute-start.10 = (bf16[528,512]{1,0:T(8,128)(2,1)S(1)}, bf16[528,512]{1,0:T(8,128)(2,1)S(1)}, u32[]{:S(2)}, u32[]{:S(2)}) collective-permute-start(bf16[528,512]{1,0:T(8,128)(2,1)S(1)} %get-tuple-element.75), channel_id=1, source_target_pairs={{32,0},{9,1},{34,2},{11,3},{36,4},{13,5},{38,6},{15,7},{40,8},{17,... | collective-permute-start | bytes 1622024 | tf_op jit(solution)/shard_map/ppermute | solution.py:55
  42.9 31.2 %collective-permute-start.11 = (bf16[528,512]{1,0:T(8,128)(2,1)S(1)}, bf16[528,512]{1,0:T(8,128)(2,1)S(1)}, u32[]{:S(2)}, u32[]{:S(2)}) collective-permute-start(bf16[528,512]{1,0:T(8,128)(2,1)S(1)} %get-tuple-element.76), channel_id=1, source_target_pairs={{96,0},{25,1},{98,2},{27,3},{100,4},{29,5},{102,6},{31,7},{104,8},... | collective-permute-start | bytes 1622024 | tf_op jit(solution)/shard_map/ppermute | solution.py:55
  47.1 41.1 %collective-permute-start.9 = (bf16[1024,512]{1,0:T(8,128)(2,1)S(1)}, bf16[1024,512]{1,0:T(8,128)(2,1)S(1)}, u32[]{:S(2)}, u32[]{:S(2)}) collective-permute-start(bf16[1024,512]{1,0:T(8,128)(2,1)S(1)} %get-tuple-element.70), channel_id=1, source_target_pairs={{64,0},{17,1},{66,2},{19,3},{68,4},{21,5},{70,6},{23,7},{72,8},{25... | collective-permute-start | bytes 3145736 | tf_op jit(solution)/shard_map/ppermute | solution.py:55
  48.7 43.0 %collective-permute-start.13 = (bf16[1024,512]{1,0:T(8,128)(2,1)S(1)}, bf16[1024,512]{1,0:T(8,128)(2,1)S(1)}, u32[]{:S(2)}, u32[]{:S(2)}) collective-permute-start(bf16[1024,512]{1,0:T(8,128)(2,1)S(1)} %get-tuple-element.82), channel_id=1, source_target_pairs={{64,0},{17,1},{66,2},{19,3},{68,4},{21,5},{70,6},{23,7},{72,8},{25... | collective-permute-start | bytes 3145736 | tf_op jit(solution)/shard_map/ppermute | solution.py:55
  74.2 4.8 %collective-permute-start.12 = (f32[8,512]{1,0:T(8,128)S(1)}, f32[8,512]{1,0:T(8,128)S(1)}, u32[]{:S(2)}, u32[]{:S(2)}) collective-permute-start(f32[8,512]{1,0:T(8,128)S(1)} %select_add_fusion.1), channel_id=1, source_target_pairs={{0,1},{1,0},{2,3},{3,2},{4,5},{5,4},{6,7},{7,6},{8,9},{9,8},{10,11... | collective-permute-start | bytes 49160 | tf_op jit(solution)/shard_map/ppermute | solution.py:59
  79.1 3.8 %collective-permute-start.14 = (f32[8,512]{1,0:T(8,128)S(1)}, f32[8,512]{1,0:T(8,128)S(1)}, u32[]{:S(2)}, u32[]{:S(2)}) collective-permute-start(f32[8,512]{1,0:T(8,128)S(1)} %fusion.2), channel_id=1, source_target_pairs={{0,2},{2,0},{4,6},{6,4},{1,3},{3,1},{5,7},{7,5},{8,10},{10,8},{12,... | collective-permute-start | bytes 49160 | tf_op jit(solution)/shard_map/ppermute | solution.py:59
  82.9 5.3 %collective-permute-start.15 = (f32[8,512]{1,0:T(8,128)S(1)}, f32[8,512]{1,0:T(8,128)S(1)}, u32[]{:S(2)}, u32[]{:S(2)}) collective-permute-start(f32[8,512]{1,0:T(8,128)S(1)} %add.35), channel_id=1, source_target_pairs={{0,4},{2,6},{4,0},{6,2},{1,5},{3,7},{5,1},{7,3},{8,12},{10,14},{12... | collective-permute-start | bytes 49160 | tf_op jit(solution)/shard_map/ppermute | solution.py:59
  88.2 7.7 %copy-start.1 = (f32[1024,512]{1,0:T(8,128)S(1)}, f32[1024,512]{1,0:T(8,128)}, u32[]{:S(2)}) copy-start(f32[1024,512]{1,0:T(8,128)} %refs_5_.1) | copy-start | bytes 6291460
  88.2 7.6 %collective-permute-start.16 = (f32[8,512]{1,0:T(8,128)S(1)}, f32[8,512]{1,0:T(8,128)S(1)}, u32[]{:S(2)}, u32[]{:S(2)}) collective-permute-start(f32[8,512]{1,0:T(8,128)S(1)} %add.36.refs_6_), channel_id=1, source_target_pairs={{80,0},{81,1},{82,2},{83,3},{84,4},{85,5},{86,6},{87,7},{88,8},{89... | collective-permute-start | bytes 49160 | tf_op jit(solution)/shard_map/ppermute | solution.py:55
  99.4 16.3 %collective-permute-start.18 = (bf16[1040,512]{1,0:T(8,128)(2,1)S(1)}, bf16[1040,512]{1,0:T(8,128)(2,1)S(1)}, u32[]{:S(2)}, u32[]{:S(2)}) collective-permute-start(bf16[1040,512]{1,0:T(8,128)(2,1)S(1)} %get-tuple-element.86.own.refs_2_), channel_id=1, source_target_pairs={{24,0},{97,1},{26,2},{99,3},{28,4},{101,5},{30,6},{103,7},{0,8},{1... | collective-permute-start | bytes 3194888 | tf_op jit(solution)/shard_map/ppermute | solution.py:55
  101.9 17.0 %collective-permute-start.17 = (bf16[1040,512]{1,0:T(8,128)(2,1)S(1)}, bf16[1040,512]{1,0:T(8,128)(2,1)S(1)}, u32[]{:S(2)}, u32[]{:S(2)}) collective-permute-start(bf16[1040,512]{1,0:T(8,128)(2,1)S(1)} %get-tuple-element.86.own.refs_2_), channel_id=1, source_target_pairs={{8,0},{33,1},{10,2},{35,3},{12,4},{37,5},{14,6},{39,7},{16,8},{41,... | collective-permute-start | bytes 3194888 | tf_op jit(solution)/shard_map/ppermute | solution.py:55
  119.8 23.3 %collective-permute-start.21 = (bf16[1536,512]{1,0:T(8,128)(2,1)S(1)}, bf16[1536,512]{1,0:T(8,128)(2,1)S(1)}, u32[]{:S(2)}, u32[]{:S(2)}) collective-permute-start(bf16[1536,512]{1,0:T(8,128)(2,1)S(1)} %get-tuple-element.94), channel_id=1, source_target_pairs={{32,0},{9,1},{34,2},{11,3},{36,4},{13,5},{38,6},{15,7},{40,8},{17,... | collective-permute-start | bytes 4718600 | tf_op jit(solution)/shard_map/ppermute | solution.py:55
  120.5 23.5 %collective-permute-start.22 = (bf16[1536,512]{1,0:T(8,128)(2,1)S(1)}, bf16[1536,512]{1,0:T(8,128)(2,1)S(1)}, u32[]{:S(2)}, u32[]{:S(2)}) collective-permute-start(bf16[1536,512]{1,0:T(8,128)(2,1)S(1)} %get-tuple-element.95), channel_id=1, source_target_pairs={{96,0},{25,1},{98,2},{27,3},{100,4},{29,5},{102,6},{31,7},{104,8},... | collective-permute-start | bytes 4718600 | tf_op jit(solution)/shard_map/ppermute | solution.py:55
  121.9 17.2 %collective-permute-start.20 = (bf16[528,512]{1,0:T(8,128)(2,1)S(1)}, bf16[528,512]{1,0:T(8,128)(2,1)S(1)}, u32[]{:S(2)}, u32[]{:S(2)}) collective-permute-start(bf16[528,512]{1,0:T(8,128)(2,1)S(1)} %get-tuple-element.89), channel_id=1, source_target_pairs={{24,0},{97,1},{26,2},{99,3},{28,4},{101,5},{30,6},{103,7},{0,8},{1... | collective-permute-start | bytes 1622024 | tf_op jit(solution)/shard_map/ppermute | solution.py:55
  124.2 14.9 %collective-permute-start.19 = (bf16[512,512]{1,0:T(8,128)(2,1)S(1)}, bf16[512,512]{1,0:T(8,128)(2,1)S(1)}, u32[]{:S(2)}, u32[]{:S(2)}) collective-permute-start(bf16[512,512]{1,0:T(8,128)(2,1)S(1)} %get-tuple-element.88), channel_id=1, source_target_pairs={{8,0},{33,1},{10,2},{35,3},{12,4},{37,5},{14,6},{39,7},{16,8},{41,... | collective-permute-start | bytes 1572872 | tf_op jit(solution)/shard_map/ppermute | solution.py:55
  140.0 31.4 %collective-permute-start.24 = (bf16[528,512]{1,0:T(8,128)(2,1)S(1)}, bf16[528,512]{1,0:T(8,128)(2,1)S(1)}, u32[]{:S(2)}, u32[]{:S(2)}) collective-permute-start(bf16[528,512]{1,0:T(8,128)(2,1)S(1)} %get-tuple-element.101), channel_id=1, source_target_pairs={{32,0},{9,1},{34,2},{11,3},{36,4},{13,5},{38,6},{15,7},{40,8},{17,... | collective-permute-start | bytes 1622024 | tf_op jit(solution)/shard_map/ppermute | solution.py:55
  141.4 33.0 %collective-permute-start.25 = (bf16[528,512]{1,0:T(8,128)(2,1)S(1)}, bf16[528,512]{1,0:T(8,128)(2,1)S(1)}, u32[]{:S(2)}, u32[]{:S(2)}) collective-permute-start(bf16[528,512]{1,0:T(8,128)(2,1)S(1)} %get-tuple-element.102), channel_id=1, source_target_pairs={{96,0},{25,1},{98,2},{27,3},{100,4},{29,5},{102,6},{31,7},{104,8},... | collective-permute-start | bytes 1622024 | tf_op jit(solution)/shard_map/ppermute | solution.py:55
  144.0 44.3 %collective-permute-start.23 = (bf16[1024,512]{1,0:T(8,128)(2,1)S(1)}, bf16[1024,512]{1,0:T(8,128)(2,1)S(1)}, u32[]{:S(2)}, u32[]{:S(2)}) collective-permute-start(bf16[1024,512]{1,0:T(8,128)(2,1)S(1)} %get-tuple-element.96), channel_id=1, source_target_pairs={{64,0},{17,1},{66,2},{19,3},{68,4},{21,5},{70,6},{23,7},{72,8},{25... | collective-permute-start | bytes 3145736 | tf_op jit(solution)/shard_map/ppermute | solution.py:55
  145.8 45.9 %collective-permute-start.27 = (bf16[1024,512]{1,0:T(8,128)(2,1)S(1)}, bf16[1024,512]{1,0:T(8,128)(2,1)S(1)}, u32[]{:S(2)}, u32[]{:S(2)}) collective-permute-start(bf16[1024,512]{1,0:T(8,128)(2,1)S(1)} %get-tuple-element.108), channel_id=1, source_target_pairs={{64,0},{17,1},{66,2},{19,3},{68,4},{21,5},{70,6},{23,7},{72,8},{25... | collective-permute-start | bytes 3145736 | tf_op jit(solution)/shard_map/ppermute | solution.py:55
  174.5 3.6 %collective-permute-start.26 = (f32[8,512]{1,0:T(8,128)S(1)}, f32[8,512]{1,0:T(8,128)S(1)}, u32[]{:S(2)}, u32[]{:S(2)}) collective-permute-start(f32[8,512]{1,0:T(8,128)S(1)} %select_add_fusion), channel_id=1, source_target_pairs={{0,1},{1,0},{2,3},{3,2},{4,5},{5,4},{6,7},{7,6},{8,9},{9,8},{10,11... | collective-permute-start | bytes 49160 | tf_op jit(solution)/shard_map/ppermute | solution.py:59
  178.2 4.9 %collective-permute-start.28 = (f32[8,512]{1,0:T(8,128)S(1)}, f32[8,512]{1,0:T(8,128)S(1)}, u32[]{:S(2)}, u32[]{:S(2)}) collective-permute-start(f32[8,512]{1,0:T(8,128)S(1)} %fusion.1), channel_id=1, source_target_pairs={{0,2},{2,0},{4,6},{6,4},{1,3},{3,1},{5,7},{7,5},{8,10},{10,8},{12,... | collective-permute-start | bytes 49160 | tf_op jit(solution)/shard_map/ppermute | solution.py:59
  183.1 5.2 %collective-permute-start.29 = (f32[8,512]{1,0:T(8,128)S(1)}, f32[8,512]{1,0:T(8,128)S(1)}, u32[]{:S(2)}, u32[]{:S(2)}) collective-permute-start(f32[8,512]{1,0:T(8,128)S(1)} %add.40), channel_id=1, source_target_pairs={{0,4},{2,6},{4,0},{6,2},{1,5},{3,7},{5,1},{7,3},{8,12},{10,14},{12... | collective-permute-start | bytes 49160 | tf_op jit(solution)/shard_map/ppermute | solution.py:59
  188.3 7.6 %collective-permute-start.30 = (f32[8,512]{1,0:T(8,128)S(1)}, f32[8,512]{1,0:T(8,128)S(1)}, u32[]{:S(2)}, u32[]{:S(2)}) collective-permute-start(f32[8,512]{1,0:T(8,128)S(1)} %add.41.refs_6_), channel_id=1, source_target_pairs={{80,0},{81,1},{82,2},{83,3},{84,4},{85,5},{86,6},{87,7},{88,8},{89... | collective-permute-start | bytes 49160 | tf_op jit(solution)/shard_map/ppermute | solution.py:55

commit v4 on v2

--- a/solution.py
+++ b/solution.py
@@ -63,9 +63,9 @@
     ((0, 1), (0, 3)),
     ((1, 0), (1, 1), (1, 3), (0, 2)),
     ((3, 0), (3, 1), (3, 3)),
-    ((2, 0), (2, 1)),
-    ((2, 3), (2, 2)),
+    ((2, 0), (2, 1), (2, 3)),
     ((1, 2), (3, 2)),
+    ((2, 2),),
 )
 
 
@@ -247,7 +247,7 @@
         move(far2, wanted[2 * CAP + r], near, r)
     for i, (k, table) in enumerate(tables):
         for r in range(CAP):
-            out, at = (out2a, i) if i < 2 else (out2b, i - 2)
+            out, at = (out2a, i) if i < 3 else (out2b, 0)
             move(table, asked[1, k * CAP + r], out, at * CAP + r)
     rows = sum(t[pl.ds(OWN_ROWS, 16), :].astype(jnp.float32) for _, t in tables)
     sums = jnp.sum(rows, axis=0, keepdims=True)
@@ -263,8 +263,8 @@
             piece,
             piece,
             piece,
-            jax.ShapeDtypeStruct((2 * CAP * BLOCK, C), b16),
-            jax.ShapeDtypeStruct((2 * CAP * BLOCK, C), b16),
+            jax.ShapeDtypeStruct((3 * CAP * BLOCK, C), b16),
+            piece,
             jax.ShapeDtypeStruct((8, C), jnp.float32),
         ),
         in_specs=[SMEM] * 2 + [VMEM] * 5,
@@ -461,12 +461,12 @@
         sums = sums + other
         col_sums = sums + swap(sums, "cols_0", 2)
         (total,) = run_tiles("across", 3, lists, words, own, (side2a,), total)
+        total, late1, late3 = lax.optimization_barrier((total, late1, late3))
+        (total,) = run_tiles("late", 4, lists, words, own, (late1, late3), total)
         total, side2b = lax.optimization_barrier((total, side2b))
-        (total,) = run_tiles("across_more", 4, lists, words, own, (side2b,), total)
-        total, late1, late3 = lax.optimization_barrier((total, late1, late3))
         finish = "more" if step < STEPS - 1 else "end"
         current, *own_next = run_tiles(
-            "late", 5, lists, words, own, (late1, late3), total, current, col_sums, finish
+            "last", 5, lists, words, own, (side2b,), total, current, col_sums, finish
         )
         if own_next:
             (own,) = own_next

time: 172 us -> 170 us (0.988)
  the two profiles are of different devices: /device:TPU:32 before, /device:TPU:0 now
where the time goes in v4:
time: 170 us; the launch traced here: 167 us
  starting transfers between devices  59.8 us (35%)
  Pallas kernels  53.5 us (31%)
  waiting for transfers between devices  50.5 us (30%)
  local copies, waits for them, and re-layouts  2.05 us (1%)
    ppermute x29, waiting for transfers between devices, fetch(): return lax.ppermute(value, ALL, pairs(first, second))  46.7 us
    ppermute x29, starting transfers between devices, fetch(): return lax.ppermute(value, ALL, pairs(first, second))  43.6 us
    pallas_call x12, Pallas kernels, run_tiles(): pl.pallas_call(functools.partial(tile_kernel, part, len(tables), earlier...  42.6 us
    ppermute x6, starting transfers between devices, swap(): lax.ppermute(value, axis, [(i, i ^ step) for i in range(lax.axis_size(axi...  16.2 us
    pallas_call x1, Pallas kernels, sort_tiles(): pl.pallas_call(sort_kernel, out_shape=jax.ShapeDtypeStruct((LIST,), i32),...  3.76 us
    ppermute x6, waiting for transfers between devices, swap(): lax.ppermute(value, axis, [(i, i ^ step) for i in range(lax.axis_size(axi...  3.72 us
    pallas_call x1, Pallas kernels, ask(): pl.pallas_call(ask_kernel, out_shape=(jax.ShapeDtypeStruct((64,), i32), j...  3.45 us
  transfers between devices with their start and end apart: 35, of which 21 were waited for; matrix products, arithmetic and copies ran while one was open for 0% of the time, Pallas kernels for 26%

profile of v4, /device:TPU:0, one launch (start us, length us, event | category | flops | bytes accessed | tf_op | source)
XLA Modules:
  0.0 167.1 jit_solution(2741805185179197163)
XLA Ops:
  0.0 1.6 copy-done
  1.7 1.6 collective-permute-start.4
  3.4 1.7 collective-permute-start.3
  5.8 3.5 %ask.1 = (s32[64]{0:T(128)S(1)}, s32[240]{0:T(256)S(1)}) custom-call(s32[3]{0:T(128)S(1)} %pad_add_fusion.1.place, s32[240]{0:T(256)S(1)} %bitcast.9, s32[240]{0:T(256)S(1)} %bitcast.10, s32[1]{0:T(128)S(6)} %copy.9.count, s32[1024]{0:T(1024)S(1)} %copy-done.2), custom_call_target="tpu_custom_call" | custom-call | tf_op jit(solution)/shard_map/ask/pallas_call | solution.py:115
  9.3 3.3 %collective-permute-start.2 = (s32[16]{0:T(128)S(1)}, s32[16]{0:T(128)S(1)}, u32[]{:S(2)}, u32[]{:S(2)}) collective-permute-start(s32[16]{0:T(128)S(1)} %get-tuple-element.134), channel_id=1, source_target_pairs={{32,0},{9,1},{34,2},{11,3},{36,4},{13,5},{38,6},{15,7},{40,8},{17,... | collective-permute-start | bytes 200 | tf_op jit(solution)/shard_map/ppermute | solution.py:55
  12.6 0.9 collective-permute-start.1
  13.5 0.6 collective-permute-start
  14.0 3.7 %collective-permute-done.1 = s32[16]{0:T(128)S(1)} collective-permute-done((s32[16]{0:T(128)S(1)}, s32[16]{0:T(128)S(1)}, u32[]{:S(2)}, u32[]{:S(2)}) %collective-permute-start.1) | collective-permute-done | bytes 96 | tf_op jit(solution)/shard_map/ppermute | solution.py:55
  17.7 0.5 collective-permute-done
  18.4 0.9 pick_early.2
  19.3 3.1 %collective-permute-start.10 = (bf16[1536,512]{1,0:T(8,128)(2,1)S(1)}, bf16[1536,512]{1,0:T(8,128)(2,1)S(1)}, u32[]{:S(2)}, u32[]{:S(2)}) collective-permute-start(bf16[1536,512]{1,0:T(8,128)(2,1)S(1)} %get-tuple-element.79), channel_id=1, source_target_pairs={{32,0},{9,1},{34,2},{11,3},{36,4},{13,5},{38,6},{15,7},{40,8},{17,... | collective-permute-start | bytes 4718600 | tf_op jit(solution)/shard_map/ppermute | solution.py:55
  22.4 1.5 collective-permute-start.6
  23.9 1.7 %collective-permute-start.5 = (bf16[512,512]{1,0:T(8,128)(2,1)S(1)}, bf16[512,512]{1,0:T(8,128)(2,1)S(1)}, u32[]{:S(2)}, u32[]{:S(2)}) collective-permute-start(bf16[512,512]{1,0:T(8,128)(2,1)S(1)} %get-tuple-element.72), channel_id=1, source_target_pairs={{8,0},{33,1},{10,2},{35,3},{12,4},{37,5},{14,6},{39,7},{16,8},{41,... | collective-permute-start | bytes 1572872 | tf_op jit(solution)/shard_map/ppermute | solution.py:55
  26.0 3.8 %sort_tiles.1.refs_0_ = s32[680]{0:T(1024)S(1)} custom-call(s32[240]{0:T(256)S(1)} %get-tuple-element.69.codes, s32[240]{0:T(256)S(1)} %bitcast.11, s32[1]{0:T(128)S(6)} %copy.9.count), custom_call_target="tpu_custom_call" | custom-call | tf_op jit(solution)/shard_map/sort_tiles/pallas_call | solution.py:163
  29.8 4.0 %near.2.refs_5_ = f32[1024,512]{1,0:T(8,128)S(1)} custom-call(s32[680]{0:T(1024)S(1)} %sort_tiles.1.refs_0_, s32[193,5,128]{2,1,0:T(8,128)S(1)} %concatenate.3.refs_1_, bf16[1040,512]{1,0:T(8,128)(2,1)S(1)} %first.1.own.refs_2_, bf16[1024,512]{1,0:T(8,128)(2,1)S(1)} %get-tuple-element.71.refs_3_), custom_call_target="tpu_custom_call" | custom-call | tf_op jit(solution)/shard_map/near/pallas_call | solution.py:414
  33.8 5.0 %collective-permute-done.5.low2 = bf16[512,512]{1,0:T(8,128)(2,1)S(1)} collective-permute-done((bf16[512,512]{1,0:T(8,128)(2,1)S(1)}, bf16[512,512]{1,0:T(8,128)(2,1)S(1)}, u32[]{:S(2)}, u32[]{:S(2)}) %collective-permute-start.5) | collective-permute-done | bytes 524320 | tf_op jit(solution)/shard_map/ppermute | solution.py:55
  38.8 0.9 pick_late.2
  39.7 2.3 %collective-permute-start.9 = (f32[8,512]{1,0:T(8,128)S(1)}, f32[8,512]{1,0:T(8,128)S(1)}, u32[]{:S(2)}, u32[]{:S(2)}) collective-permute-start(f32[8,512]{1,0:T(8,128)S(1)} %get-tuple-element.76), channel_id=1, source_target_pairs={{64,0},{17,1},{66,2},{19,3},{68,4},{21,5},{70,6},{23,7},{72,8},{25... | collective-permute-start | bytes 49160 | tf_op jit(solution)/shard_map/ppermute | solution.py:55
  42.0 1.9 %collective-permute-start.8 = (f32[8,512]{1,0:T(8,128)S(1)}, f32[8,512]{1,0:T(8,128)S(1)}, u32[]{:S(2)}, u32[]{:S(2)}) collective-permute-start(f32[8,512]{1,0:T(8,128)S(1)} %get-tuple-element.76), channel_id=1, source_target_pairs={{96,0},{25,1},{98,2},{27,3},{100,4},{29,5},{102,6},{31,7},{104,8},... | collective-permute-start | bytes 49160 | tf_op jit(solution)/shard_map/ppermute | solution.py:55
  43.9 1.3 collective-permute-start.7
  45.2 3.3 %collective-permute-done.9 = f32[8,512]{1,0:T(8,128)S(1)} collective-permute-done((f32[8,512]{1,0:T(8,128)S(1)}, f32[8,512]{1,0:T(8,128)S(1)}, u32[]{:S(2)}, u32[]{:S(2)}) %collective-permute-start.9) | collective-permute-done | bytes 16416 | tf_op jit(solution)/shard_map/ppermute | solution.py:55
  48.5 0.7 collective-permute-start.12
  49.2 1.7 %collective-permute-start.15 = (bf16[512,512]{1,0:T(8,128)(2,1)S(1)}, bf16[512,512]{1,0:T(8,128)(2,1)S(1)}, u32[]{:S(2)}, u32[]{:S(2)}) collective-permute-start(bf16[512,512]{1,0:T(8,128)(2,1)S(1)} %get-tuple-element.92), channel_id=1, source_target_pairs={{32,0},{9,1},{34,2},{11,3},{36,4},{13,5},{38,6},{15,7},{40,8},{17,... | collective-permute-start | bytes 1572872 | tf_op jit(solution)/shard_map/ppermute | solution.py:55
  50.9 0.3 collective-permute-start.16
  51.3 2.9 %collective-permute-start.17 = (bf16[512,512]{1,0:T(8,128)(2,1)S(1)}, bf16[512,512]{1,0:T(8,128)(2,1)S(1)}, u32[]{:S(2)}, u32[]{:S(2)}) collective-permute-start(bf16[512,512]{1,0:T(8,128)(2,1)S(1)} %get-tuple-element.97), channel_id=1, source_target_pairs={{64,0},{17,1},{66,2},{19,3},{68,4},{21,5},{70,6},{23,7},{72,8},{25... | collective-permute-start | bytes 1572872 | tf_op jit(solution)/shard_map/ppermute | solution.py:55
  54.2 4.1 %sides_1.2.refs_4_ = f32[1024,512]{1,0:T(8,128)S(1)} custom-call(s32[680]{0:T(1024)S(1)} %sort_tiles.1.refs_0_, s32[193,5,128]{2,1,0:T(8,128)S(1)} %concatenate.3.refs_1_, bf16[1040,512]{1,0:T(8,128)(2,1)S(1)} %first.1.own.refs_2_, bf16[1536,512]{1,0:T(8,128)(2,1)S(1)} %collective-permute-done.10.refs_3_, bf16[512,512]{1,0:T(8,128)(2,1)S(1)} %get-tuple-element.84.refs_4_, ...), custom_call_target="tpu_custom_call" | custom-call | tf_op jit(solution)/shard_map/sides_1/pallas_call | solution.py:414
  58.3 2.0 %collective-permute-start.14 = (f32[8,512]{1,0:T(8,128)S(1)}, f32[8,512]{1,0:T(8,128)S(1)}, u32[]{:S(2)}, u32[]{:S(2)}) collective-permute-start(f32[8,512]{1,0:T(8,128)S(1)} %add.41), channel_id=1, source_target_pairs={{0,2},{2,0},{4,6},{6,4},{1,3},{3,1},{5,7},{7,5},{8,10},{10,8},{12,... | collective-permute-start | bytes 49160 | tf_op jit(solution)/shard_map/ppermute | solution.py:59
  60.3 2.3 %sides_3.2.refs_4_ = f32[1024,512]{1,0:T(8,128)S(1)} custom-call(s32[680]{0:T(1024)S(1)} %sort_tiles.1.refs_0_, s32[193,5,128]{2,1,0:T(8,128)S(1)} %concatenate.3.refs_1_, bf16[1040,512]{1,0:T(8,128)(2,1)S(1)} %first.1.own.refs_2_, bf16[1536,512]{1,0:T(8,128)(2,1)S(1)} %collective-permute-done.11.refs_3_, f32[1024,512]{1,0:T(8,128)S(1)} %sides_1.2.refs_4_), custom_call_target="tpu_custom_call" | custom-call | tf_op jit(solution)/shard_map/sides_3/pallas_call | solution.py:414
  62.7 5.5 %collective-permute-start.18 = (f32[8,512]{1,0:T(8,128)S(1)}, f32[8,512]{1,0:T(8,128)S(1)}, u32[]{:S(2)}, u32[]{:S(2)}) collective-permute-start(f32[8,512]{1,0:T(8,128)S(1)} %add.42), channel_id=1, source_target_pairs={{0,4},{2,6},{4,0},{6,2},{1,5},{3,7},{5,1},{7,3},{8,12},{10,14},{12... | collective-permute-start | bytes 49160 | tf_op jit(solution)/shard_map/ppermute | solution.py:59
  68.2 1.7 %collective-permute-done.18 = f32[8,512]{1,0:T(8,128)S(1)} collective-permute-done((f32[8,512]{1,0:T(8,128)S(1)}, f32[8,512]{1,0:T(8,128)S(1)}, u32[]{:S(2)}, u32[]{:S(2)}) %collective-permute-start.18) | collective-permute-done | bytes 16416 | tf_op jit(solution)/shard_map/ppermute | solution.py:59
  69.9 0.7 collective-permute-done.12.refs_3_
  70.6 4.2 %across.2.refs_5_ = f32[1024,512]{1,0:T(8,128)S(1)} custom-call(s32[680]{0:T(1024)S(1)} %sort_tiles.1.refs_0_, s32[193,5,128]{2,1,0:T(8,128)S(1)} %concatenate.3.refs_1_, bf16[1040,512]{1,0:T(8,128)(2,1)S(1)} %first.1.own.refs_2_, bf16[1536,512]{1,0:T(8,128)(2,1)S(1)} %collective-permute-done.12.refs_3_, f32[1024,512]{1,0:T(8,128)S(1)} %sides_3.2.refs_4_), custom_call_target="tpu_custom_call" | custom-call | tf_op jit(solution)/shard_map/across/pallas_call | solution.py:414
  75.1 1.0 collective-permute-done.16.refs_4_
  76.1 3.1 %late.2.refs_4_ = f32[1024,512]{1,0:T(8,128)S(1)} custom-call(s32[680]{0:T(1024)S(1)} %sort_tiles.1.refs_0_, s32[193,5,128]{2,1,0:T(8,128)S(1)} %concatenate.3.refs_1_, bf16[1040,512]{1,0:T(8,128)(2,1)S(1)} %first.1.own.refs_2_, bf16[512,512]{1,0:T(8,128)(2,1)S(1)} %collective-permute-done.15.refs_3_, bf16[512,512]{1,0:T(8,128)(2,1)S(1)} %collective-permute-done.16.refs_4_, ...), custom_call_target="tpu_custom_call" | custom-call | tf_op jit(solution)/shard_map/late/pallas_call | solution.py:414
  79.2 2.6 %collective-permute-done.17.refs_3_ = bf16[512,512]{1,0:T(8,128)(2,1)S(1)} collective-permute-done((bf16[512,512]{1,0:T(8,128)(2,1)S(1)}, bf16[512,512]{1,0:T(8,128)(2,1)S(1)}, u32[]{:S(2)}, u32[]{:S(2)}) %collective-permute-start.17) | collective-permute-done | bytes 524320 | tf_op jit(solution)/shard_map/ppermute | solution.py:55
  81.8 3.3 %last.2 = (f32[1024,512]{1,0:T(8,128)S(1)}, bf16[1040,512]{1,0:T(8,128)(2,1)S(1)}) custom-call(s32[680]{0:T(1024)S(1)} %sort_tiles.1.refs_0_, s32[193,5,128]{2,1,0:T(8,128)S(1)} %concatenate.3.refs_1_, bf16[1040,512]{1,0:T(8,128)(2,1)S(1)} %first.1.own.refs_2_, bf16[512,512]{1,0:T(8,128)(2,1)S(1)} %collective-permute-done.17.refs_3_, ...), custom_call_target="tpu_custom_call" | custom-call | tf_op jit(solution)/shard_map/last/pallas_call | solution.py:414
  85.3 3.0 %collective-permute-start.19 = (bf16[1040,512]{1,0:T(8,128)(2,1)S(1)}, bf16[1040,512]{1,0:T(8,128)(2,1)S(1)}, u32[]{:S(2)}, u32[]{:S(2)}) collective-permute-start(bf16[1040,512]{1,0:T(8,128)(2,1)S(1)} %get-tuple-element.101.own.refs_2_), channel_id=1, source_target_pairs={{8,0},{33,1},{10,2},{35,3},{12,4},{37,5},{14,6},{39,7},{16,8},{41,... | collective-permute-start | bytes 3194888 | tf_op jit(solution)/shard_map/ppermute | solution.py:55
  88.4 12.9 %collective-permute-done.20.far3 = bf16[1040,512]{1,0:T(8,128)(2,1)S(1)} collective-permute-done((bf16[1040,512]{1,0:T(8,128)(2,1)S(1)}, bf16[1040,512]{1,0:T(8,128)(2,1)S(1)}, u32[]{:S(2)}, u32[]{:S(2)}) %collective-permute-start.20) | collective-permute-done | bytes 1064992 | tf_op jit(solution)/shard_map/ppermute | solution.py:55
  101.3 0.5 collective-permute-done.19.far1
  101.8 0.9 pick_early.3
  102.7 1.1 collective-permute-start.26
  103.8 1.0 collective-permute-start.27
  104.8 1.4 collective-permute-start.22
  106.3 2.3 %collective-permute-start.21 = (bf16[512,512]{1,0:T(8,128)(2,1)S(1)}, bf16[512,512]{1,0:T(8,128)(2,1)S(1)}, u32[]{:S(2)}, u32[]{:S(2)}) collective-permute-start(bf16[512,512]{1,0:T(8,128)(2,1)S(1)} %get-tuple-element.103), channel_id=1, source_target_pairs={{8,0},{33,1},{10,2},{35,3},{12,4},{37,5},{14,6},{39,7},{16,8},{41,... | collective-permute-start | bytes 1572872 | tf_op jit(solution)/shard_map/ppermute | solution.py:55
  108.5 4.0 %near.3.refs_5_ = f32[1024,512]{1,0:T(8,128)S(1)} custom-call(s32[680]{0:T(1024)S(1)} %sort_tiles.1.refs_0_, s32[193,5,128]{2,1,0:T(8,128)S(1)} %concatenate.3.refs_1_, bf16[1040,512]{1,0:T(8,128)(2,1)S(1)} %get-tuple-element.101.own.refs_2_, bf16[1024,512]{1,0:T(8,128)(2,1)S(1)} %get-tuple-element.102.refs_3_), custom_call_target="tpu_custom_call" | custom-call | tf_op jit(solution)/shard_map/near/pallas_call | solution.py:414
  112.6 9.7 %collective-permute-done.21.low2 = bf16[512,512]{1,0:T(8,128)(2,1)S(1)} collective-permute-done((bf16[512,512]{1,0:T(8,128)(2,1)S(1)}, bf16[512,512]{1,0:T(8,128)(2,1)S(1)}, u32[]{:S(2)}, u32[]{:S(2)}) %collective-permute-start.21) | collective-permute-done | bytes 524320 | tf_op jit(solution)/shard_map/ppermute | solution.py:55
  122.2 0.9 pick_late.3
  123.2 2.4 %collective-permute-start.24 = (f32[8,512]{1,0:T(8,128)S(1)}, f32[8,512]{1,0:T(8,128)S(1)}, u32[]{:S(2)}, u32[]{:S(2)}) collective-permute-start(f32[8,512]{1,0:T(8,128)S(1)} %get-tuple-element.107), channel_id=1, source_target_pairs={{96,0},{25,1},{98,2},{27,3},{100,4},{29,5},{102,6},{31,7},{104,8},... | collective-permute-start | bytes 49160 | tf_op jit(solution)/shard_map/ppermute | solution.py:55
  125.6 0.9 collective-permute-start.23
  126.5 2.3 %collective-permute-done.25 = f32[8,512]{1,0:T(8,128)S(1)} collective-permute-done((f32[8,512]{1,0:T(8,128)S(1)}, f32[8,512]{1,0:T(8,128)S(1)}, u32[]{:S(2)}, u32[]{:S(2)}) %collective-permute-start.25) | collective-permute-done | bytes 16416 | tf_op jit(solution)/shard_map/ppermute | solution.py:55
  128.8 0.5 collective-permute-done.23
  129.3 1.7 %collective-permute-start.28 = (bf16[1536,512]{1,0:T(8,128)(2,1)S(1)}, bf16[1536,512]{1,0:T(8,128)(2,1)S(1)}, u32[]{:S(2)}, u32[]{:S(2)}) collective-permute-start(bf16[1536,512]{1,0:T(8,128)(2,1)S(1)} %get-tuple-element.112), channel_id=1, source_target_pairs={{64,0},{17,1},{66,2},{19,3},{68,4},{21,5},{70,6},{23,7},{72,8},{25... | collective-permute-start | bytes 4718600 | tf_op jit(solution)/shard_map/ppermute | solution.py:55
  131.1 2.0 %collective-permute-start.31 = (bf16[512,512]{1,0:T(8,128)(2,1)S(1)}, bf16[512,512]{1,0:T(8,128)(2,1)S(1)}, u32[]{:S(2)}, u32[]{:S(2)}) collective-permute-start(bf16[512,512]{1,0:T(8,128)(2,1)S(1)} %get-tuple-element.123), channel_id=1, source_target_pairs={{32,0},{9,1},{34,2},{11,3},{36,4},{13,5},{38,6},{15,7},{40,8},{17,... | collective-permute-start | bytes 1572872 | tf_op jit(solution)/shard_map/ppermute | solution.py:55
  133.1 1.8 %collective-permute-start.33 = (bf16[512,512]{1,0:T(8,128)(2,1)S(1)}, bf16[512,512]{1,0:T(8,128)(2,1)S(1)}, u32[]{:S(2)}, u32[]{:S(2)}) collective-permute-start(bf16[512,512]{1,0:T(8,128)(2,1)S(1)} %get-tuple-element.128), channel_id=1, source_target_pairs={{64,0},{17,1},{66,2},{19,3},{68,4},{21,5},{70,6},{23,7},{72,8},{25... | collective-permute-start | bytes 1572872 | tf_op jit(solution)/shard_map/ppermute | solution.py:55
  134.9 4.1 %sides_1.3.refs_4_ = f32[1024,512]{1,0:T(8,128)S(1)} custom-call(s32[680]{0:T(1024)S(1)} %sort_tiles.1.refs_0_, s32[193,5,128]{2,1,0:T(8,128)S(1)} %concatenate.3.refs_1_, bf16[1040,512]{1,0:T(8,128)(2,1)S(1)} %get-tuple-element.101.own.refs_2_, bf16[1536,512]{1,0:T(8,128)(2,1)S(1)} %collective-permute-done.26.refs_3_, ...), custom_call_target="tpu_custom_call" | custom-call | tf_op jit(solution)/shard_map/sides_1/pallas_call | solution.py:414
  139.1 1.3 collective-permute-start.30
  140.3 2.3 %sides_3.3.refs_4_ = f32[1024,512]{1,0:T(8,128)S(1)} custom-call(s32[680]{0:T(1024)S(1)} %sort_tiles.1.refs_0_, s32[193,5,128]{2,1,0:T(8,128)S(1)} %concatenate.3.refs_1_, bf16[1040,512]{1,0:T(8,128)(2,1)S(1)} %get-tuple-element.101.own.refs_2_, bf16[1536,512]{1,0:T(8,128)(2,1)S(1)} %collective-permute-done.27.refs_3_, f32[1024,512]{1,0:T(8,128)S(1)} %sides_1.3.refs_4_), custom_call_target="tpu_custom_call" | custom-call | tf_op jit(solution)/shard_map/sides_3/pallas_call | solution.py:414
  142.9 7.4 %collective-permute-start.34 = (f32[8,512]{1,0:T(8,128)S(1)}, f32[8,512]{1,0:T(8,128)S(1)}, u32[]{:S(2)}, u32[]{:S(2)}) collective-permute-start(f32[8,512]{1,0:T(8,128)S(1)} %add.48), channel_id=1, source_target_pairs={{0,4},{2,6},{4,0},{6,2},{1,5},{3,7},{5,1},{7,3},{8,12},{10,14},{12... | collective-permute-start | bytes 49160 | tf_op jit(solution)/shard_map/ppermute | solution.py:59
  150.3 1.7 %collective-permute-done.34 = f32[8,512]{1,0:T(8,128)S(1)} collective-permute-done((f32[8,512]{1,0:T(8,128)S(1)}, f32[8,512]{1,0:T(8,128)S(1)}, u32[]{:S(2)}, u32[]{:S(2)}) %collective-permute-start.34) | collective-permute-done | bytes 16416 | tf_op jit(solution)/shard_map/ppermute | solution.py:59
  152.1 4.0 %across.3.refs_5_ = f32[1024,512]{1,0:T(8,128)S(1)} custom-call(s32[680]{0:T(1024)S(1)} %sort_tiles.1.refs_0_, s32[193,5,128]{2,1,0:T(8,128)S(1)} %concatenate.3.refs_1_, bf16[1040,512]{1,0:T(8,128)(2,1)S(1)} %get-tuple-element.101.own.refs_2_, bf16[1536,512]{1,0:T(8,128)(2,1)S(1)} %collective-permute-done.28.refs_3_, f32[1024,512]{1,0:T(8,128)S(1)} %sides_3.3.refs_4_), custom_call_target="tpu_custom_call" | custom-call | tf_op jit(solution)/shard_map/across/pallas_call | solution.py:414
  156.4 0.5 collective-permute-done.32.refs_4_
  156.9 2.9 %late.3.refs_4_ = f32[1024,512]{1,0:T(8,128)S(1)} custom-call(s32[680]{0:T(1024)S(1)} %sort_tiles.1.refs_0_, s32[193,5,128]{2,1,0:T(8,128)S(1)} %concatenate.3.refs_1_, bf16[1040,512]{1,0:T(8,128)(2,1)S(1)} %get-tuple-element.101.own.refs_2_, bf16[512,512]{1,0:T(8,128)(2,1)S(1)} %collective-permute-done.31.refs_3_, ...), custom_call_target="tpu_custom_call" | custom-call | tf_op jit(solution)/shard_map/late/pallas_call | solution.py:414
  159.8 2.8 %collective-permute-done.33.refs_3_ = bf16[512,512]{1,0:T(8,128)(2,1)S(1)} collective-permute-done((bf16[512,512]{1,0:T(8,128)(2,1)S(1)}, bf16[512,512]{1,0:T(8,128)(2,1)S(1)}, u32[]{:S(2)}, u32[]{:S(2)}) %collective-permute-start.33) | collective-permute-done | bytes 524320 | tf_op jit(solution)/shard_map/ppermute | solution.py:55
  162.5 4.3 %last.3 = f32[1024,512]{1,0:T(8,128)} custom-call(s32[680]{0:T(1024)S(1)} %sort_tiles.1.refs_0_, s32[193,5,128]{2,1,0:T(8,128)S(1)} %concatenate.3.refs_1_, bf16[1040,512]{1,0:T(8,128)(2,1)S(1)} %get-tuple-element.101.own.refs_2_, bf16[512,512]{1,0:T(8,128)(2,1)S(1)} %collective-permute-done.33.refs_3_, f32[1024,512]{1,0:T(8,128)S(1)} %late.3.refs_4_, ...), custom_call_target="tpu_custom_call" | custom-call | tf_op jit(solution)/shard_map/last/pallas_call | solution.py:414
  (52 shorter events, 2.2 us)
Async XLA Ops:
  0.0 1.6 copy-start
  1.6 4.2 %copy-start.2 = (s32[1024]{0:T(1024)S(1)}, s32[1024]{0:T(1024)}, u32[]{:S(2)}) copy-start(s32[1024]{0:T(1024)} %home.1) | copy-start | bytes 12292
  1.6 4.2 %copy-start.3 = (s32[1,240]{1,0:T(1,128)S(1)}, s32[1,240]{1,0:T(1,128)}, u32[]{:S(2)}) copy-start(s32[1,240]{1,0:T(1,128)} %param.8) | copy-start | bytes 2884
  1.6 4.2 %copy-start.4 = (s32[1,240]{1,0:T(1,128)S(1)}, s32[1,240]{1,0:T(1,128)}, u32[]{:S(2)}) copy-start(s32[1,240]{1,0:T(1,128)} %param.9) | copy-start | bytes 2884
  1.7 16.5 %collective-permute-start.4 = (bf16[1040,512]{1,0:T(8,128)(2,1)S(1)}, bf16[1040,512]{1,0:T(8,128)(2,1)S(1)}, u32[]{:S(2)}, u32[]{:S(2)}) collective-permute-start(bf16[1040,512]{1,0:T(8,128)(2,1)S(1)} %first.1.own.refs_2_), channel_id=1, source_target_pairs={{24,0},{97,1},{26,2},{99,3},{28,4},{101,5},{30,6},{103,7},{0,8},{1... | collective-permute-start | bytes 3194888 | tf_op jit(solution)/shard_map/ppermute | solution.py:55
  3.4 15.0 %collective-permute-start.3 = (bf16[1040,512]{1,0:T(8,128)(2,1)S(1)}, bf16[1040,512]{1,0:T(8,128)(2,1)S(1)}, u32[]{:S(2)}, u32[]{:S(2)}) collective-permute-start(bf16[1040,512]{1,0:T(8,128)(2,1)S(1)} %first.1.own.refs_2_), channel_id=1, source_target_pairs={{8,0},{33,1},{10,2},{35,3},{12,4},{37,5},{14,6},{39,7},{16,8},{41,... | collective-permute-start | bytes 3194888 | tf_op jit(solution)/shard_map/ppermute | solution.py:55
  9.3 4.7 %collective-permute-start.2 = (s32[16]{0:T(128)S(1)}, s32[16]{0:T(128)S(1)}, u32[]{:S(2)}, u32[]{:S(2)}) collective-permute-start(s32[16]{0:T(128)S(1)} %get-tuple-element.134), channel_id=1, source_target_pairs={{32,0},{9,1},{34,2},{11,3},{36,4},{13,5},{38,6},{15,7},{40,8},{17,... | collective-permute-start | bytes 200 | tf_op jit(solution)/shard_map/ppermute | solution.py:55
  12.6 5.1 %collective-permute-start.1 = (s32[16]{0:T(128)S(1)}, s32[16]{0:T(128)S(1)}, u32[]{:S(2)}, u32[]{:S(2)}) collective-permute-start(s32[16]{0:T(128)S(1)} %get-tuple-element.135), channel_id=1, source_target_pairs={{64,0},{17,1},{66,2},{19,3},{68,4},{21,5},{70,6},{23,7},{72,8},{25... | collective-permute-start | bytes 200 | tf_op jit(solution)/shard_map/ppermute | solution.py:55
  13.5 4.8 %collective-permute-start = (s32[16]{0:T(128)S(1)}, s32[16]{0:T(128)S(1)}, u32[]{:S(2)}, u32[]{:S(2)}) collective-permute-start(s32[16]{0:T(128)S(1)} %get-tuple-element.136), channel_id=1, source_target_pairs={{96,0},{25,1},{98,2},{27,3},{100,4},{29,5},{102,6},{31,7},{104,8},... | collective-permute-start | bytes 200 | tf_op jit(solution)/shard_map/ppermute | solution.py:55
  18.4 7.3 %copy-start.6 = (s32[192,5,128]{2,0,1:T(8,128)S(1)}, s32[192,5,128]{2,0,1:T(8,128)}, u32[]{:S(2)}) copy-start(s32[192,5,128]{2,0,1:T(8,128)} %param.13) | copy-start | bytes 1474564
  19.3 6.7 %copy-start.5 = (s32[1,240]{1,0:T(1,128)S(1)}, s32[1,240]{1,0:T(1,128)}, u32[]{:S(2)}) copy-start(s32[1,240]{1,0:T(1,128)} %param.10) | copy-start | bytes 2884
  19.3 29.2 %collective-permute-start.10 = (bf16[1536,512]{1,0:T(8,128)(2,1)S(1)}, bf16[1536,512]{1,0:T(8,128)(2,1)S(1)}, u32[]{:S(2)}, u32[]{:S(2)}) collective-permute-start(bf16[1536,512]{1,0:T(8,128)(2,1)S(1)} %get-tuple-element.79), channel_id=1, source_target_pairs={{32,0},{9,1},{34,2},{11,3},{36,4},{13,5},{38,6},{15,7},{40,8},{17,... | collective-permute-start | bytes 4718600 | tf_op jit(solution)/shard_map/ppermute | solution.py:55
  22.4 26.1 %collective-permute-start.11 = (bf16[1536,512]{1,0:T(8,128)(2,1)S(1)}, bf16[1536,512]{1,0:T(8,128)(2,1)S(1)}, u32[]{:S(2)}, u32[]{:S(2)}) collective-permute-start(bf16[1536,512]{1,0:T(8,128)(2,1)S(1)} %get-tuple-element.80), channel_id=1, source_target_pairs={{96,0},{25,1},{98,2},{27,3},{100,4},{29,5},{102,6},{31,7},{104,8},... | collective-permute-start | bytes 4718600 | tf_op jit(solution)/shard_map/ppermute | solution.py:55
  22.4 16.4 %collective-permute-start.6 = (bf16[528,512]{1,0:T(8,128)(2,1)S(1)}, bf16[528,512]{1,0:T(8,128)(2,1)S(1)}, u32[]{:S(2)}, u32[]{:S(2)}) collective-permute-start(bf16[528,512]{1,0:T(8,128)(2,1)S(1)} %get-tuple-element.73), channel_id=1, source_target_pairs={{24,0},{97,1},{26,2},{99,3},{28,4},{101,5},{30,6},{103,7},{0,8},{1... | collective-permute-start | bytes 1622024 | tf_op jit(solution)/shard_map/ppermute | solution.py:55
  23.9 14.9 %collective-permute-start.5 = (bf16[512,512]{1,0:T(8,128)(2,1)S(1)}, bf16[512,512]{1,0:T(8,128)(2,1)S(1)}, u32[]{:S(2)}, u32[]{:S(2)}) collective-permute-start(bf16[512,512]{1,0:T(8,128)(2,1)S(1)} %get-tuple-element.72), channel_id=1, source_target_pairs={{8,0},{33,1},{10,2},{35,3},{12,4},{37,5},{14,6},{39,7},{16,8},{41,... | collective-permute-start | bytes 1572872 | tf_op jit(solution)/shard_map/ppermute | solution.py:55
  39.7 8.8 %collective-permute-start.9 = (f32[8,512]{1,0:T(8,128)S(1)}, f32[8,512]{1,0:T(8,128)S(1)}, u32[]{:S(2)}, u32[]{:S(2)}) collective-permute-start(f32[8,512]{1,0:T(8,128)S(1)} %get-tuple-element.76), channel_id=1, source_target_pairs={{64,0},{17,1},{66,2},{19,3},{68,4},{21,5},{70,6},{23,7},{72,8},{25... | collective-permute-start | bytes 49160 | tf_op jit(solution)/shard_map/ppermute | solution.py:55
  42.0 6.5 %collective-permute-start.8 = (f32[8,512]{1,0:T(8,128)S(1)}, f32[8,512]{1,0:T(8,128)S(1)}, u32[]{:S(2)}, u32[]{:S(2)}) collective-permute-start(f32[8,512]{1,0:T(8,128)S(1)} %get-tuple-element.76), channel_id=1, source_target_pairs={{96,0},{25,1},{98,2},{27,3},{100,4},{29,5},{102,6},{31,7},{104,8},... | collective-permute-start | bytes 49160 | tf_op jit(solution)/shard_map/ppermute | solution.py:55
  43.9 4.6 %collective-permute-start.7 = (f32[8,512]{1,0:T(8,128)S(1)}, f32[8,512]{1,0:T(8,128)S(1)}, u32[]{:S(2)}, u32[]{:S(2)}) collective-permute-start(f32[8,512]{1,0:T(8,128)S(1)} %get-tuple-element.76), channel_id=1, source_target_pairs={{32,0},{9,1},{34,2},{11,3},{36,4},{13,5},{38,6},{15,7},{40,8},{17,... | collective-permute-start | bytes 49160 | tf_op jit(solution)/shard_map/ppermute | solution.py:55
  48.5 22.1 %collective-permute-start.12 = (bf16[1536,512]{1,0:T(8,128)(2,1)S(1)}, bf16[1536,512]{1,0:T(8,128)(2,1)S(1)}, u32[]{:S(2)}, u32[]{:S(2)}) collective-permute-start(bf16[1536,512]{1,0:T(8,128)(2,1)S(1)} %get-tuple-element.81), channel_id=1, source_target_pairs={{64,0},{17,1},{66,2},{19,3},{68,4},{21,5},{70,6},{23,7},{72,8},{25... | collective-permute-start | bytes 4718600 | tf_op jit(solution)/shard_map/ppermute | solution.py:55
  49.2 25.9 %collective-permute-start.15 = (bf16[512,512]{1,0:T(8,128)(2,1)S(1)}, bf16[512,512]{1,0:T(8,128)(2,1)S(1)}, u32[]{:S(2)}, u32[]{:S(2)}) collective-permute-start(bf16[512,512]{1,0:T(8,128)(2,1)S(1)} %get-tuple-element.92), channel_id=1, source_target_pairs={{32,0},{9,1},{34,2},{11,3},{36,4},{13,5},{38,6},{15,7},{40,8},{17,... | collective-permute-start | bytes 1572872 | tf_op jit(solution)/shard_map/ppermute | solution.py:55
  50.9 25.2 %collective-permute-start.16 = (bf16[512,512]{1,0:T(8,128)(2,1)S(1)}, bf16[512,512]{1,0:T(8,128)(2,1)S(1)}, u32[]{:S(2)}, u32[]{:S(2)}) collective-permute-start(bf16[512,512]{1,0:T(8,128)(2,1)S(1)} %get-tuple-element.93), channel_id=1, source_target_pairs={{96,0},{25,1},{98,2},{27,3},{100,4},{29,5},{102,6},{31,7},{104,8},... | collective-permute-start | bytes 1572872 | tf_op jit(solution)/shard_map/ppermute | solution.py:55
  51.3 30.5 %collective-permute-start.17 = (bf16[512,512]{1,0:T(8,128)(2,1)S(1)}, bf16[512,512]{1,0:T(8,128)(2,1)S(1)}, u32[]{:S(2)}, u32[]{:S(2)}) collective-permute-start(bf16[512,512]{1,0:T(8,128)(2,1)S(1)} %get-tuple-element.97), channel_id=1, source_target_pairs={{64,0},{17,1},{66,2},{19,3},{68,4},{21,5},{70,6},{23,7},{72,8},{25... | collective-permute-start | bytes 1572872 | tf_op jit(solution)/shard_map/ppermute | solution.py:55
  54.2 4.2 %collective-permute-start.13 = (f32[8,512]{1,0:T(8,128)S(1)}, f32[8,512]{1,0:T(8,128)S(1)}, u32[]{:S(2)}, u32[]{:S(2)}) collective-permute-start(f32[8,512]{1,0:T(8,128)S(1)} %add_add_fusion.1), channel_id=1, source_target_pairs={{0,1},{1,0},{2,3},{3,2},{4,5},{5,4},{6,7},{7,6},{8,9},{9,8},{10,11... | collective-permute-start | bytes 49160 | tf_op jit(solution)/shard_map/ppermute | solution.py:59
  58.3 4.3 %collective-permute-start.14 = (f32[8,512]{1,0:T(8,128)S(1)}, f32[8,512]{1,0:T(8,128)S(1)}, u32[]{:S(2)}, u32[]{:S(2)}) collective-permute-start(f32[8,512]{1,0:T(8,128)S(1)} %add.41), channel_id=1, source_target_pairs={{0,2},{2,0},{4,6},{6,4},{1,3},{3,1},{5,7},{7,5},{8,10},{10,8},{12,... | collective-permute-start | bytes 49160 | tf_op jit(solution)/shard_map/ppermute | solution.py:59
  62.7 7.3 %collective-permute-start.18 = (f32[8,512]{1,0:T(8,128)S(1)}, f32[8,512]{1,0:T(8,128)S(1)}, u32[]{:S(2)}, u32[]{:S(2)}) collective-permute-start(f32[8,512]{1,0:T(8,128)S(1)} %add.42), channel_id=1, source_target_pairs={{0,4},{2,6},{4,0},{6,2},{1,5},{3,7},{5,1},{7,3},{8,12},{10,14},{12... | collective-permute-start | bytes 49160 | tf_op jit(solution)/shard_map/ppermute | solution.py:59
  74.8 7.0 %copy-start.1 = (f32[1024,512]{1,0:T(8,128)S(1)}, f32[1024,512]{1,0:T(8,128)}, u32[]{:S(2)}) copy-start(f32[1024,512]{1,0:T(8,128)} %refs_5_.1) | copy-start | bytes 6291460
  85.1 16.3 %collective-permute-start.20 = (bf16[1040,512]{1,0:T(8,128)(2,1)S(1)}, bf16[1040,512]{1,0:T(8,128)(2,1)S(1)}, u32[]{:S(2)}, u32[]{:S(2)}) collective-permute-start(bf16[1040,512]{1,0:T(8,128)(2,1)S(1)} %get-tuple-element.101.own.refs_2_), channel_id=1, source_target_pairs={{24,0},{97,1},{26,2},{99,3},{28,4},{101,5},{30,6},{103,7},{0,8},{1... | collective-permute-start | bytes 3194888 | tf_op jit(solution)/shard_map/ppermute | solution.py:55
  85.3 16.5 %collective-permute-start.19 = (bf16[1040,512]{1,0:T(8,128)(2,1)S(1)}, bf16[1040,512]{1,0:T(8,128)(2,1)S(1)}, u32[]{:S(2)}, u32[]{:S(2)}) collective-permute-start(bf16[1040,512]{1,0:T(8,128)(2,1)S(1)} %get-tuple-element.101.own.refs_2_), channel_id=1, source_target_pairs={{8,0},{33,1},{10,2},{35,3},{12,4},{37,5},{14,6},{39,7},{16,8},{41,... | collective-permute-start | bytes 3194888 | tf_op jit(solution)/shard_map/ppermute | solution.py:55
  102.7 26.6 %collective-permute-start.26 = (bf16[1536,512]{1,0:T(8,128)(2,1)S(1)}, bf16[1536,512]{1,0:T(8,128)(2,1)S(1)}, u32[]{:S(2)}, u32[]{:S(2)}) collective-permute-start(bf16[1536,512]{1,0:T(8,128)(2,1)S(1)} %get-tuple-element.110), channel_id=1, source_target_pairs={{32,0},{9,1},{34,2},{11,3},{36,4},{13,5},{38,6},{15,7},{40,8},{17,... | collective-permute-start | bytes 4718600 | tf_op jit(solution)/shard_map/ppermute | solution.py:55
  103.8 25.5 %collective-permute-start.27 = (bf16[1536,512]{1,0:T(8,128)(2,1)S(1)}, bf16[1536,512]{1,0:T(8,128)(2,1)S(1)}, u32[]{:S(2)}, u32[]{:S(2)}) collective-permute-start(bf16[1536,512]{1,0:T(8,128)(2,1)S(1)} %get-tuple-element.111), channel_id=1, source_target_pairs={{96,0},{25,1},{98,2},{27,3},{100,4},{29,5},{102,6},{31,7},{104,8},... | collective-permute-start | bytes 4718600 | tf_op jit(solution)/shard_map/ppermute | solution.py:55
  104.8 17.4 %collective-permute-start.22 = (bf16[528,512]{1,0:T(8,128)(2,1)S(1)}, bf16[528,512]{1,0:T(8,128)(2,1)S(1)}, u32[]{:S(2)}, u32[]{:S(2)}) collective-permute-start(bf16[528,512]{1,0:T(8,128)(2,1)S(1)} %get-tuple-element.104), channel_id=1, source_target_pairs={{24,0},{97,1},{26,2},{99,3},{28,4},{101,5},{30,6},{103,7},{0,8},{1... | collective-permute-start | bytes 1622024 | tf_op jit(solution)/shard_map/ppermute | solution.py:55
  106.3 16.0 %collective-permute-start.21 = (bf16[512,512]{1,0:T(8,128)(2,1)S(1)}, bf16[512,512]{1,0:T(8,128)(2,1)S(1)}, u32[]{:S(2)}, u32[]{:S(2)}) collective-permute-start(bf16[512,512]{1,0:T(8,128)(2,1)S(1)} %get-tuple-element.103), channel_id=1, source_target_pairs={{8,0},{33,1},{10,2},{35,3},{12,4},{37,5},{14,6},{39,7},{16,8},{41,... | collective-permute-start | bytes 1572872 | tf_op jit(solution)/shard_map/ppermute | solution.py:55
  123.1 5.7 %collective-permute-start.25 = (f32[8,512]{1,0:T(8,128)S(1)}, f32[8,512]{1,0:T(8,128)S(1)}, u32[]{:S(2)}, u32[]{:S(2)}) collective-permute-start(f32[8,512]{1,0:T(8,128)S(1)} %get-tuple-element.107), channel_id=1, source_target_pairs={{64,0},{17,1},{66,2},{19,3},{68,4},{21,5},{70,6},{23,7},{72,8},{25... | collective-permute-start | bytes 49160 | tf_op jit(solution)/shard_map/ppermute | solution.py:55
  123.2 5.6 %collective-permute-start.24 = (f32[8,512]{1,0:T(8,128)S(1)}, f32[8,512]{1,0:T(8,128)S(1)}, u32[]{:S(2)}, u32[]{:S(2)}) collective-permute-start(f32[8,512]{1,0:T(8,128)S(1)} %get-tuple-element.107), channel_id=1, source_target_pairs={{96,0},{25,1},{98,2},{27,3},{100,4},{29,5},{102,6},{31,7},{104,8},... | collective-permute-start | bytes 49160 | tf_op jit(solution)/shard_map/ppermute | solution.py:55
  125.6 3.7 %collective-permute-start.23 = (f32[8,512]{1,0:T(8,128)S(1)}, f32[8,512]{1,0:T(8,128)S(1)}, u32[]{:S(2)}, u32[]{:S(2)}) collective-permute-start(f32[8,512]{1,0:T(8,128)S(1)} %get-tuple-element.107), channel_id=1, source_target_pairs={{32,0},{9,1},{34,2},{11,3},{36,4},{13,5},{38,6},{15,7},{40,8},{17,... | collective-permute-start | bytes 49160 | tf_op jit(solution)/shard_map/ppermute | solution.py:55
  129.3 22.7 %collective-permute-start.28 = (bf16[1536,512]{1,0:T(8,128)(2,1)S(1)}, bf16[1536,512]{1,0:T(8,128)(2,1)S(1)}, u32[]{:S(2)}, u32[]{:S(2)}) collective-permute-start(bf16[1536,512]{1,0:T(8,128)(2,1)S(1)} %get-tuple-element.112), channel_id=1, source_target_pairs={{64,0},{17,1},{66,2},{19,3},{68,4},{21,5},{70,6},{23,7},{72,8},{25... | collective-permute-start | bytes 4718600 | tf_op jit(solution)/shard_map/ppermute | solution.py:55
  131.1 25.3 %collective-permute-start.31 = (bf16[512,512]{1,0:T(8,128)(2,1)S(1)}, bf16[512,512]{1,0:T(8,128)(2,1)S(1)}, u32[]{:S(2)}, u32[]{:S(2)}) collective-permute-start(bf16[512,512]{1,0:T(8,128)(2,1)S(1)} %get-tuple-element.123), channel_id=1, source_target_pairs={{32,0},{9,1},{34,2},{11,3},{36,4},{13,5},{38,6},{15,7},{40,8},{17,... | collective-permute-start | bytes 1572872 | tf_op jit(solution)/shard_map/ppermute | solution.py:55
  133.1 23.8 %collective-permute-start.32 = (bf16[512,512]{1,0:T(8,128)(2,1)S(1)}, bf16[512,512]{1,0:T(8,128)(2,1)S(1)}, u32[]{:S(2)}, u32[]{:S(2)}) collective-permute-start(bf16[512,512]{1,0:T(8,128)(2,1)S(1)} %get-tuple-element.124), channel_id=1, source_target_pairs={{96,0},{25,1},{98,2},{27,3},{100,4},{29,5},{102,6},{31,7},{104,8},... | collective-permute-start | bytes 1572872 | tf_op jit(solution)/shard_map/ppermute | solution.py:55
  133.1 29.4 %collective-permute-start.33 = (bf16[512,512]{1,0:T(8,128)(2,1)S(1)}, bf16[512,512]{1,0:T(8,128)(2,1)S(1)}, u32[]{:S(2)}, u32[]{:S(2)}) collective-permute-start(bf16[512,512]{1,0:T(8,128)(2,1)S(1)} %get-tuple-element.128), channel_id=1, source_target_pairs={{64,0},{17,1},{66,2},{19,3},{68,4},{21,5},{70,6},{23,7},{72,8},{25... | collective-permute-start | bytes 1572872 | tf_op jit(solution)/shard_map/ppermute | solution.py:55
  134.9 4.1 %collective-permute-start.29 = (f32[8,512]{1,0:T(8,128)S(1)}, f32[8,512]{1,0:T(8,128)S(1)}, u32[]{:S(2)}, u32[]{:S(2)}) collective-permute-start(f32[8,512]{1,0:T(8,128)S(1)} %add_add_fusion), channel_id=1, source_target_pairs={{0,1},{1,0},{2,3},{3,2},{4,5},{5,4},{6,7},{7,6},{8,9},{9,8},{10,11... | collective-permute-start | bytes 49160 | tf_op jit(solution)/shard_map/ppermute | solution.py:59
  139.1 3.8 %collective-permute-start.30 = (f32[8,512]{1,0:T(8,128)S(1)}, f32[8,512]{1,0:T(8,128)S(1)}, u32[]{:S(2)}, u32[]{:S(2)}) collective-permute-start(f32[8,512]{1,0:T(8,128)S(1)} %add.47), channel_id=1, source_target_pairs={{0,2},{2,0},{4,6},{6,4},{1,3},{3,1},{5,7},{7,5},{8,10},{10,8},{12,... | collective-permute-start | bytes 49160 | tf_op jit(solution)/shard_map/ppermute | solution.py:59
  142.9 9.2 %collective-permute-start.34 = (f32[8,512]{1,0:T(8,128)S(1)}, f32[8,512]{1,0:T(8,128)S(1)}, u32[]{:S(2)}, u32[]{:S(2)}) collective-permute-start(f32[8,512]{1,0:T(8,128)S(1)} %add.48), channel_id=1, source_target_pairs={{0,4},{2,6},{4,0},{6,2},{1,5},{3,7},{5,1},{7,3},{8,12},{10,14},{12... | collective-permute-start | bytes 49160 | tf_op jit(solution)/shard_map/ppermute | solution.py:59
